TPU v7x, 32 devices: a whole 2x2x4 slice. The times are simulated.
32 devices in a mesh: row: 8 (over y, x, core), col: 4 (over z).
Axes of the slice: x: 2, y: 2, z: 4, core: 2. Of those that a mesh axis runs over, the one named last changes fastest.
Arguments:
- sample_counts: int32 [64], replicated, may hold values from 100 to 2000
- slot_silo: int32 [64], replicated, may hold values from 0 to 63, each once
- gate_weight: bfloat16 [28672, 8192], P('row', 'col'), may hold values from -3 to 3
- up_weight: bfloat16 [28672, 8192], P('row', 'col'), may hold values from -3 to 3
- down_weight: bfloat16 [8192, 28672], P('row', 'col'), may hold values from -3 to 3
- gate_a: bfloat16 [1024, 8192], P(('row', 'col')), may hold values from -6 to 6
- up_a: bfloat16 [1024, 8192], P(('row', 'col')), may hold values from -6 to 6
- down_a: bfloat16 [1024, 28672], P(('row', 'col')), may hold values from -6 to 6
- gate_b: bfloat16 [1024, 28672], P(('row', 'col')), may hold values from -6 to 6
- up_b: bfloat16 [1024, 28672], P(('row', 'col')), may hold values from -6 to 6
- down_b: bfloat16 [1024, 8192], P(('row', 'col')), may hold values from -6 to 6
Outputs:
- merged_gate: bfloat16 [28672, 8192], P('row', 'col')
- merged_up: bfloat16 [28672, 8192], P('row', 'col')
- merged_down: bfloat16 [8192, 28672], P('row', 'col')
Inputs may be any that keep to these rules, and one draw needn't show every extreme that they name: `slot_silo`: a permutation of the silos.
All inputs are finite; a program needn't handle non-finite values.
Results may differ from a plain program's by a relative error of at most 0.0043.
Values may be sent and summed in bfloat16 or wider, within the bound.
No kernel may reach another device: no remote copies, remote signals or barrier semaphores. Data moves between devices by JAX's collectives and lax.ppermute only.
A program may use at most 256 MiB of HBM per device.

v0:
```python
import functools

import jax
import jax.numpy as jnp
from jax import lax
from jax.experimental import pallas as pl
from jax.experimental.pallas import tpu as pltpu
from jax.sharding import PartitionSpec as P


RANK = 16
BLOCK = 256


def rows_scale(sample_counts, slot_silo, row_ids):
    slot_ids = row_ids // RANK
    silo_table = jnp.arange(slot_silo.shape[0], dtype=jnp.int32)
    silo_ids = jnp.sum(
        jnp.where(slot_ids[:, None] == silo_table[None, :], slot_silo[None, :], 0), axis=1
    )
    counts_f = sample_counts.astype(jnp.float32)
    shares = counts_f / jnp.sum(counts_f)
    return jnp.sum(
        jnp.where(silo_ids[:, None] == silo_table[None, :], shares[None, :], 0.0), axis=1
    )


def columns_of(array, index, parts):
    width = array.shape[1] // parts
    return lax.dynamic_slice_in_dim(array, index * width, width, axis=1)


def spread_rows(factors):
    n_row = lax.axis_size("row")
    mine = lax.axis_index("row")
    pieces = []
    for i in range(n_row):
        piece = jnp.concatenate([columns_of(f, mine ^ i, n_row) for f in factors], axis=1)
        if i:
            piece = lax.ppermute(piece, "row", [(k, k ^ i) for k in range(n_row)])
        pieces.append(piece)
    return jnp.concatenate(pieces)


def spread_cols(factors):
    n_col = lax.axis_size("col")
    mine = lax.axis_index("col")
    pieces = []
    for s in range(n_col):
        at = (mine + s) % n_col
        piece = jnp.concatenate([columns_of(f, at, n_col) for f in factors], axis=1)
        if s:
            piece = lax.ppermute(piece, "col", [(j, (j + s) % n_col) for j in range(n_col)])
        pieces.append(piece)
    return pieces


def gather_rows(block):
    n_row = lax.axis_size("row")
    pieces = [None] * n_row
    pieces[0] = block
    for i in range(2, n_row, 2):
        pieces[i] = lax.ppermute(block, "row", [(k, k ^ i) for k in range(n_row)])
    for i in range(0, n_row, 2):
        pieces[i ^ 1] = lax.ppermute(pieces[i], "row", [(k, k ^ 1) for k in range(n_row)])
    return pieces


def merge_kernel(n_row, n_col, tile, strides, column, *refs):
    b_ref, weight_ref = refs[:2]
    a_refs = refs[2 : 2 + n_row]
    out_ref, a_all, sems = refs[-3:]
    depth = a_refs[0].shape[0] // n_col
    row_stride, col_stride = strides

    @pl.when(pl.program_id(0) == 0)
    def _():
        mine = lax.axis_index("col")
        copies = []
        for s in range(n_col):
            owner = lax.rem(mine + (n_col - s), n_col)
            for i in range(n_row):
                start = pl.multiple_of(owner * col_stride + i * row_stride, depth)
                copies.append(
                    pltpu.make_async_copy(
                        a_refs[i].at[pl.ds(s * depth, depth), pl.ds(column, a_all.shape[1])],
                        a_all.at[pl.ds(start, depth)],
                        sems.at[s * n_row + i],
                    )
                )
        for copy in copies:
            copy.start()
        for copy in copies:
            copy.wait()

    b = b_ref[...]
    for start in range(0, out_ref.shape[1], tile):
        at = slice(start, start + tile)
        update = lax.dot_general(
            b, a_all[:, at], (((0,), (0,)), ((), ())), preferred_element_type=jnp.float32
        )
        out_ref[:, at] = (weight_ref[:, at].astype(jnp.float32) + update).astype(out_ref.dtype)


def merge_rows(weight, b, a_pieces, column, first=0, done=None, rows_outer=False):
    n_row = lax.axis_size("row")
    n_col = lax.axis_size("col")
    rank, rows = b.shape
    width = weight.shape[1]
    skip = first // BLOCK
    depth = rank // (n_row * n_col)
    strides = (n_col * depth, depth) if rows_outer else (depth, n_row * depth)
    tile = width
    while tile > 2048:
        tile //= 2
    operands = [b, weight, *a_pieces]
    in_specs = [
        pl.BlockSpec((rank, BLOCK), lambda g: (0, g)),
        pl.BlockSpec((BLOCK, width), lambda g: (g + skip, 0)),
    ] + [pl.BlockSpec(memory_space=pl.ANY)] * n_row
    aliases = {}
    if done is not None:
        aliases = {len(operands): 0}
        operands.append(done)
        in_specs.append(pl.BlockSpec(memory_space=pl.ANY))
    return pl.pallas_call(
        functools.partial(merge_kernel, n_row, n_col, tile, strides, column),
        grid=(rows // BLOCK,),
        in_specs=in_specs,
        out_specs=pl.BlockSpec((BLOCK, width), lambda g: (g + skip, 0)),
        out_shape=jax.ShapeDtypeStruct(weight.shape, weight.dtype),
        scratch_shapes=[
            pltpu.VMEM((rank, width), jnp.bfloat16),
            pltpu.SemaphoreType.DMA((n_row * n_col,)),
        ],
        input_output_aliases=aliases,
        compiler_params=pltpu.CompilerParams(
            dimension_semantics=("arbitrary",), vmem_limit_bytes=60 * 1024 * 1024
        ),
        cost_estimate=pl.CostEstimate(
            flops=2 * rank * rows * width,
            bytes_accessed=2 * (rank * (rows + width) + 2 * rows * width),
            transcendentals=0,
        ),
    )(*operands)


def local(
    sample_counts,
    slot_silo,
    gate_weight,
    up_weight,
    down_weight,
    gate_a,
    up_a,
    down_a,
    gate_b,
    up_b,
    down_b,
):
    n_col = lax.axis_size("col")
    depth = gate_a.shape[0]

    def whole_of(factor):
        return lax.all_gather(factor, "col", axis=0, tiled=True)

    down_raw = whole_of(down_b)
    cols = spread_cols((gate_a, up_a, down_a))
    mine_b = spread_rows((gate_b, up_b))
    down_whole = spread_rows((down_raw,))

    gate_rows, up_rows = gate_weight.shape[0], up_weight.shape[0]
    last = max(BLOCK, up_rows * 3 // 16 // BLOCK * BLOCK)
    cut = gate_rows + up_rows - last
    gate_whole = whole_of(mine_b[:, :gate_rows])
    up_whole = whole_of(mine_b[:, gate_rows:cut])
    up_last = whole_of(mine_b[:, cut:])

    mine = lax.axis_index("col")
    owners = (mine + n_col - jnp.arange(n_col, dtype=jnp.int32)) % n_col
    shards = lax.axis_index("row") * n_col + owners
    row_ids = (shards[:, None] * depth + jnp.arange(depth, dtype=jnp.int32)[None, :]).reshape(-1)
    scale = rows_scale(sample_counts, slot_silo, row_ids)

    gate_cols = gate_weight.shape[1]
    both_cols = gate_cols + up_weight.shape[1]

    def gathered(start, end):
        block = jnp.concatenate([piece[:, start:end] for piece in cols])
        block = (scale[:, None] * block.astype(jnp.float32)).astype(jnp.bfloat16)
        return gather_rows(block)

    down_pieces = gathered(both_cols, both_cols + down_weight.shape[1])
    mlp_pieces = gathered(0, both_cols)

    merged_down = merge_rows(down_weight, down_whole, down_pieces, 0, rows_outer=True)
    merged_gate = merge_rows(gate_weight, gate_whole, mlp_pieces, 0)
    merged_up = merge_rows(up_weight, up_whole, mlp_pieces, gate_cols)
    merged_up = merge_rows(up_weight, up_last, mlp_pieces, gate_cols, up_rows - last, merged_up)
    return merged_gate, merged_up, merged_down


def solution(mesh):
    return jax.shard_map(
        local,
        mesh=mesh,
        in_specs=(
            P(),
            P(),
            P("row", "col"),
            P("row", "col"),
            P("row", "col"),
            P(("row", "col"), None),
            P(("row", "col"), None),
            P(("row", "col"), None),
            P(("row", "col"), None),
            P(("row", "col"), None),
            P(("row", "col"), None),
        ),
        out_specs=(P("row", "col"), P("row", "col"), P("row", "col")),
        check_vma=False,
    )
```

profile of v0, /device:TPU:15, one launch (start us, length us, event | category | flops | bytes accessed | tf_op | source)
XLA Modules:
  0.0 468.6 jit_solution(6252225155655461429)
XLA Ops:
  7.2 0.7 all-gather.11.cloned.1.call-update
  8.0 2.4 constant_dynamic-slice_fusion.19
  10.4 0.7 collective-permute-start
  11.5 1.5 collective-permute-start.2
  13.4 1.7 collective-permute-start.4
  15.5 8.0 %collective-permute-done.1 = bf16[32,7168]{1,0:T(8,128)(2,1)S(1)} collective-permute-done((bf16[32,7168]{1,0:T(8,128)(2,1)S(1)}, bf16[32,7168]{1,0:T(8,128)(2,1)S(1)}, u32[]{:S(2)}, u32[]{:S(2)}) %collective-permute-start.1) | collective-permute-done | bytes 458784 | tf_op jit(solution)/shard_map/ppermute | solution.py:40
  23.4 1.3 collective-permute-start.6
  24.8 9.4 %collective-permute-done.2 = bf16[32,7168]{1,0:T(8,128)(2,1)S(1)} collective-permute-done((bf16[32,7168]{1,0:T(8,128)(2,1)S(1)}, bf16[32,7168]{1,0:T(8,128)(2,1)S(1)}, u32[]{:S(2)}, u32[]{:S(2)}) %collective-permute-start.2) | collective-permute-done | bytes 458784 | tf_op jit(solution)/shard_map/ppermute | solution.py:40
  34.3 20.8 %collective-permute-done.4 = bf16[32,7168]{1,0:T(8,128)(2,1)S(1)} collective-permute-done((bf16[32,7168]{1,0:T(8,128)(2,1)S(1)}, bf16[32,7168]{1,0:T(8,128)(2,1)S(1)}, u32[]{:S(2)}, u32[]{:S(2)}) %collective-permute-start.4) | collective-permute-done | bytes 458784 | tf_op jit(solution)/shard_map/ppermute | solution.py:40
  55.3 1.8 copy-done
  57.1 1.3 slice.41
  58.6 1.7 slice.40
  60.3 0.9 constant_dynamic-slice_fusion.18
  61.2 1.4 constant_dynamic-slice_fusion.16
  62.6 0.9 pad_maximum_fusion
  63.5 1.4 collective-permute-start.7
  64.9 3.0 slice.36
  67.9 0.9 pad_maximum_fusion.1
  68.8 0.8 collective-permute-start.8
  69.7 0.9 pad_maximum_fusion.2
  70.6 1.2 collective-permute-start.9
  73.4 43.0 %collective-permute-done.7 = bf16[32,11264]{1,0:T(8,128)(2,1)S(1)} collective-permute-done((bf16[32,11264]{1,0:T(8,128)(2,1)}, bf16[32,11264]{1,0:T(8,128)(2,1)S(1)}, u32[]{:S(2)}, u32[]{:S(2)}) %collective-permute-start.7) | collective-permute-done | bytes 720928 | tf_op jit(solution)/shard_map/ppermute | solution.py:53
  116.5 80.0 %collective-permute-done.8 = bf16[32,11264]{1,0:T(8,128)(2,1)S(1)} collective-permute-done((bf16[32,11264]{1,0:T(8,128)(2,1)}, bf16[32,11264]{1,0:T(8,128)(2,1)S(1)}, u32[]{:S(2)}, u32[]{:S(2)}) %collective-permute-start.8) | collective-permute-done | bytes 720928 | tf_op jit(solution)/shard_map/ppermute | solution.py:53
  196.5 10.0 %collective-permute-done.9 = bf16[32,11264]{1,0:T(8,128)(2,1)} collective-permute-done((bf16[32,11264]{1,0:T(8,128)(2,1)}, bf16[32,11264]{1,0:T(8,128)(2,1)}, u32[]{:S(2)}, u32[]{:S(2)}) %collective-permute-start.9) | collective-permute-done | bytes 720928 | tf_op jit(solution)/shard_map/ppermute | solution.py:53
  206.5 1.0 slice.44
  208.4 2.3 collective-permute-start.29
  210.7 1.0 slice.39
  212.4 1.7 constant_dynamic-slice_fusion
  214.1 97.1 %collective-permute-done.11.refs_4_ = bf16[128,4096]{1,0:T(8,128)(2,1)} collective-permute-done((bf16[128,4096]{1,0:T(8,128)(2,1)S(1)}, bf16[128,4096]{1,0:T(8,128)(2,1)}, u32[]{:S(2)}, u32[]{:S(2)}) %collective-permute-start.11) | collective-permute-done | bytes 1048608 | tf_op jit(solution)/shard_map/ppermute | solution.py:63
  311.2 1.3 collective-permute-start.17
  312.7 1.6 collective-permute-start.19
  314.4 1.6 collective-permute-start.21
  316.2 4.0 collective-permute-done.18
  320.2 1.6 collective-permute-start.26
  321.8 4.7 collective-permute-done.19
  327.0 1.3 collective-permute-done.21
  328.4 9.1 %collective-permute-done.22 = bf16[128,1024]{1,0:T(8,128)(2,1)S(1)} collective-permute-done((bf16[128,1024]{1,0:T(8,128)(2,1)S(1)}, bf16[128,1024]{1,0:T(8,128)(2,1)S(1)}, u32[]{:S(2)}, u32[]{:S(2)}) %collective-permute-start.22) | collective-permute-done | bytes 262176 | tf_op jit(solution)/shard_map/ppermute | solution.py:40
  337.9 9.3 %collective-permute-done.23 = bf16[128,1024]{1,0:T(8,128)(2,1)S(1)} collective-permute-done((bf16[128,1024]{1,0:T(8,128)(2,1)S(1)}, bf16[128,1024]{1,0:T(8,128)(2,1)S(1)}, u32[]{:S(2)}, u32[]{:S(2)}) %collective-permute-start.23) | collective-permute-done | bytes 262176 | tf_op jit(solution)/shard_map/ppermute | solution.py:40
  347.4 25.4 %collective-permute-done.15.refs_8_ = bf16[128,4096]{1,0:T(8,128)(2,1)} collective-permute-done((bf16[128,4096]{1,0:T(8,128)(2,1)S(1)}, bf16[128,4096]{1,0:T(8,128)(2,1)}, u32[]{:S(2)}, u32[]{:S(2)}) %collective-permute-start.15) | collective-permute-done | bytes 1048608 | tf_op jit(solution)/shard_map/ppermute | solution.py:63
  372.8 1.0 collective-permute-start.10
  373.9 1.1 copy-done.10
  375.0 1.2 copy-done.11
  376.3 1.3 copy-done.12
  377.5 25.9 %shard_map.133 = bf16[1024,7168]{1,0:T(8,128)(2,1)} custom-call(bf16[1024,1024]{1,0:T(8,128)(2,1)} %copy-done.9, bf16[1024,7168]{1,0:T(8,128)(2,1)} %refs_1_.7, bf16[128,7168]{1,0:T(8,128)(2,1)} %copy-done.3, bf16[128,7168]{1,0:T(8,128)(2,1)} %copy-done.10, bf16[128,7168]{1,0:T(8,128)(2,1)} %collective-permute-done.25.refs_4_, bf16[128,7168]{1,0:T(8,128)(2,1)} %copy-done.11, ...), custom_call_target="tpu_custom_call" | custom-call | flops 15032385536 | bytes 46137344 | tf_op jit(solution)/shard_map/pallas_call | solution.py:126
  403.6 0.9 copy-done.5
  404.9 23.2 %shard_map.131.refs_10_ = bf16[3584,2048]{1,0:T(8,128)(2,1)} custom-call(bf16[1024,3072]{1,0:T(8,128)(2,1)} %all-gather.9.cloned.1.call-done.refs_0_, bf16[3584,2048]{1,0:T(8,128)(2,1)} %refs_1_.6, bf16[128,4096]{1,0:T(8,128)(2,1)} %copy-done.1, bf16[128,4096]{1,0:T(8,128)(2,1)} %collective-permute-done.10.refs_3_, ...), custom_call_target="tpu_custom_call" | custom-call | flops 12884901888 | bytes 35651584 | tf_op jit(solution)/shard_map/pallas_call | solution.py:126
  428.2 7.5 %shard_map.132 = bf16[3584,2048]{1,0:T(8,128)(2,1)} custom-call(bf16[1024,512]{1,0:T(8,128)(2,1)} %all-gather.7.cloned.1.call-done.refs_0_, bf16[3584,2048]{1,0:T(8,128)(2,1)} %refs_1_.6, bf16[128,4096]{1,0:T(8,128)(2,1)} %copy-done.1, bf16[128,4096]{1,0:T(8,128)(2,1)} %collective-permute-done.10.refs_3_, ...), custom_call_target="tpu_custom_call", output_to_operand_aliasing={{}: (10, {})} | custom-call | flops 2147483648 | bytes 9437184 | tf_op jit(solution)/shard_map/pallas_call | solution.py:126
  435.7 26.3 %shard_map.130 = bf16[3584,2048]{1,0:T(8,128)(2,1)} custom-call(bf16[1024,3584]{1,0:T(8,128)(2,1)} %all-gather.5.cloned.1.call-done.refs_0_, bf16[3584,2048]{1,0:T(8,128)(2,1)} %refs_1_.4, bf16[128,4096]{1,0:T(8,128)(2,1)} %copy-done.1, bf16[128,4096]{1,0:T(8,128)(2,1)} %collective-permute-done.10.refs_3_, ...), custom_call_target="tpu_custom_call" | custom-call | flops 15032385536 | bytes 40894464 | tf_op jit(solution)/shard_map/pallas_call | solution.py:126
  (110 shorter events, 6.9 us)
Async XLA Ops:
  7.2 205.2 %all-gather.11.cloned.1.call-start = ((), (), s32[]{:S(2)}) async-start(), calls=%async_computation.3 | async-start | bytes 2621440 | tf_op jit(solution)/shard_map/all_gather | solution.py:165
  7.9 395.7 %all-gather.9.cloned.1.call-start = ((), (), s32[]{:S(2)}) async-start(), calls=%async_computation.2 | async-start | bytes 7864320 | tf_op jit(solution)/shard_map/all_gather | solution.py:165
  10.4 4.7 %collective-permute-start = (bf16[32,7168]{1,0:T(8,128)(2,1)S(1)}, bf16[32,7168]{1,0:T(8,128)(2,1)S(1)}, u32[]{:S(2)}, u32[]{:S(2)}) collective-permute-start(bf16[32,7168]{1,0:T(8,128)(2,1)S(1)} %pad_maximum_fusion.3), channel_id=1, source_target_pairs={{0,4},{4,0},{8,12},{12,8},{16,20},{20,16},{24,28},{28,24},{1,5},{5... | collective-permute-start | bytes 1376264 | tf_op jit(solution)/shard_map/ppermute | solution.py:40
  11.2 12.2 %collective-permute-start.1 = (bf16[32,7168]{1,0:T(8,128)(2,1)S(1)}, bf16[32,7168]{1,0:T(8,128)(2,1)S(1)}, u32[]{:S(2)}, u32[]{:S(2)}) collective-permute-start(bf16[32,7168]{1,0:T(8,128)(2,1)S(1)} %pad_maximum_fusion.4), channel_id=1, source_target_pairs={{0,8},{4,12},{8,0},{12,4},{16,24},{20,28},{24,16},{28,20},{1,9},{5... | collective-permute-start | bytes 1376264 | tf_op jit(solution)/shard_map/ppermute | solution.py:40
  11.5 22.7 %collective-permute-start.2 = (bf16[32,7168]{1,0:T(8,128)(2,1)S(1)}, bf16[32,7168]{1,0:T(8,128)(2,1)S(1)}, u32[]{:S(2)}, u32[]{:S(2)}) collective-permute-start(bf16[32,7168]{1,0:T(8,128)(2,1)S(1)} %pad_maximum_fusion.5), channel_id=1, source_target_pairs={{0,12},{4,8},{8,4},{12,0},{16,28},{20,24},{24,20},{28,16},{1,13},{... | collective-permute-start | bytes 1376264 | tf_op jit(solution)/shard_map/ppermute | solution.py:40
  13.0 21.2 %collective-permute-start.3 = (bf16[32,7168]{1,0:T(8,128)(2,1)S(1)}, bf16[32,7168]{1,0:T(8,128)(2,1)S(1)}, u32[]{:S(2)}, u32[]{:S(2)}) collective-permute-start(bf16[32,7168]{1,0:T(8,128)(2,1)S(1)} %pad_maximum_fusion.6), channel_id=1, source_target_pairs={{0,16},{4,20},{8,24},{12,28},{16,0},{20,4},{24,8},{28,12},{1,17},{... | collective-permute-start | bytes 1376264 | tf_op jit(solution)/shard_map/ppermute | solution.py:40
  13.4 41.8 %collective-permute-start.4 = (bf16[32,7168]{1,0:T(8,128)(2,1)S(1)}, bf16[32,7168]{1,0:T(8,128)(2,1)S(1)}, u32[]{:S(2)}, u32[]{:S(2)}) collective-permute-start(bf16[32,7168]{1,0:T(8,128)(2,1)S(1)} %pad_maximum_fusion.7), channel_id=1, source_target_pairs={{0,20},{4,16},{8,28},{12,24},{16,4},{20,0},{24,12},{28,8},{1,21},{... | collective-permute-start | bytes 1376264 | tf_op jit(solution)/shard_map/ppermute | solution.py:40
  15.2 40.0 %collective-permute-start.5 = (bf16[32,7168]{1,0:T(8,128)(2,1)S(1)}, bf16[32,7168]{1,0:T(8,128)(2,1)S(1)}, u32[]{:S(2)}, u32[]{:S(2)}) collective-permute-start(bf16[32,7168]{1,0:T(8,128)(2,1)S(1)} %pad_maximum_fusion.8), channel_id=1, source_target_pairs={{0,24},{4,28},{8,16},{12,20},{16,8},{20,12},{24,0},{28,4},{1,25},{... | collective-permute-start | bytes 1376264 | tf_op jit(solution)/shard_map/ppermute | solution.py:40
  23.4 31.8 %collective-permute-start.6 = (bf16[32,7168]{1,0:T(8,128)(2,1)S(1)}, bf16[32,7168]{1,0:T(8,128)(2,1)S(1)}, u32[]{:S(2)}, u32[]{:S(2)}) collective-permute-start(bf16[32,7168]{1,0:T(8,128)(2,1)S(1)} %pad_maximum_fusion.9), channel_id=1, source_target_pairs={{0,28},{4,24},{8,20},{12,16},{16,12},{20,8},{24,4},{28,0},{1,29},{... | collective-permute-start | bytes 1376264 | tf_op jit(solution)/shard_map/ppermute | solution.py:40
  55.3 1.8 copy-start
  57.1 3.2 copy-start.2
  58.5 369.7 %all-gather.7.cloned.1.call-start = ((), (), s32[]{:S(2)}) async-start(), calls=%async_computation.1 | async-start | bytes 1310720 | tf_op jit(solution)/shard_map/all_gather | solution.py:165
  60.3 375.4 %all-gather.5.cloned.1.call-start = ((), (), s32[]{:S(2)}) async-start(), calls=%async_computation | async-start | bytes 9175040 | tf_op jit(solution)/shard_map/all_gather | solution.py:165
  63.5 52.9 %collective-permute-start.7 = (bf16[32,11264]{1,0:T(8,128)(2,1)}, bf16[32,11264]{1,0:T(8,128)(2,1)S(1)}, u32[]{:S(2)}, u32[]{:S(2)}) collective-permute-start(bf16[32,11264]{1,0:T(8,128)(2,1)} %pad_maximum_fusion), channel_id=1, source_target_pairs={{0,1},{1,2},{2,3},{3,0},{4,5},{5,6},{6,7},{7,4},{8,9},{9,10},{10,1... | collective-permute-start | bytes 2162696 | tf_op jit(solution)/shard_map/ppermute | solution.py:53
  67.9 4.0 copy-start.14
  67.9 4.7 copy-start.13
  68.8 127.6 %collective-permute-start.8 = (bf16[32,11264]{1,0:T(8,128)(2,1)}, bf16[32,11264]{1,0:T(8,128)(2,1)S(1)}, u32[]{:S(2)}, u32[]{:S(2)}) collective-permute-start(bf16[32,11264]{1,0:T(8,128)(2,1)} %pad_maximum_fusion.1), channel_id=1, source_target_pairs={{0,2},{1,3},{2,0},{3,1},{4,6},{5,7},{6,4},{7,5},{8,10},{9,11},{10,... | collective-permute-start | bytes 2162696 | tf_op jit(solution)/shard_map/ppermute | solution.py:53
  69.7 137.9 %copy-start.4 = (bf16[32,7168]{1,0:T(8,128)(2,1)S(1)}, bf16[32,7168]{1,0:T(8,128)(2,1)}, u32[]{:S(2)}) copy-start(bf16[32,7168]{1,0:T(8,128)(2,1)} %get-tuple-element.11) | copy-start | bytes 1376260
  70.6 135.9 %collective-permute-start.9 = (bf16[32,11264]{1,0:T(8,128)(2,1)}, bf16[32,11264]{1,0:T(8,128)(2,1)}, u32[]{:S(2)}, u32[]{:S(2)}) collective-permute-start(bf16[32,11264]{1,0:T(8,128)(2,1)} %pad_maximum_fusion.2), channel_id=1, source_target_pairs={{0,3},{1,0},{2,1},{3,2},{4,7},{5,4},{6,5},{7,6},{8,11},{9,8},{10,9... | collective-permute-start | bytes 2162696 | tf_op jit(solution)/shard_map/ppermute | solution.py:53
  116.4 91.1 %copy-start.7 = (bf16[32,11264]{1,0:T(8,128)(2,1)}, bf16[32,11264]{1,0:T(8,128)(2,1)S(1)}, u32[]{:S(2)}) copy-start(bf16[32,11264]{1,0:T(8,128)(2,1)S(1)} %collective-permute-done.7) | copy-start | bytes 2162692
  196.5 11.1 %copy-start.8 = (bf16[32,11264]{1,0:T(8,128)(2,1)}, bf16[32,11264]{1,0:T(8,128)(2,1)S(1)}, u32[]{:S(2)}) copy-start(bf16[32,11264]{1,0:T(8,128)(2,1)S(1)} %collective-permute-done.8) | copy-start | bytes 2162692
  207.6 4.1 slice-start
  207.6 4.1 slice-start.1
  208.0 108.0 %copy-start.3 = (bf16[128,7168]{1,0:T(8,128)(2,1)}, bf16[128,7168]{1,0:T(8,128)(2,1)S(1)}, u32[]{:S(2)}) copy-start(bf16[128,7168]{1,0:T(8,128)(2,1)S(1)} %multiply_convert_fusion.refs_2_) | copy-start | bytes 5505028
  208.0 104.7 %collective-permute-start.25 = (bf16[128,7168]{1,0:T(8,128)(2,1)S(1)}, bf16[128,7168]{1,0:T(8,128)(2,1)}, u32[]{:S(2)}, u32[]{:S(2)}) collective-permute-start(bf16[128,7168]{1,0:T(8,128)(2,1)S(1)} %multiply_convert_fusion.refs_2_), channel_id=1, source_target_pairs={{0,8},{4,12},{8,0},{12,4},{16,24},{20,28},{24,16},{28,20},{1,9},{5... | collective-permute-start | bytes 5505032 | tf_op jit(solution)/shard_map/ppermute | solution.py:63
  208.3 106.0 %collective-permute-start.27 = (bf16[128,7168]{1,0:T(8,128)(2,1)S(1)}, bf16[128,7168]{1,0:T(8,128)(2,1)}, u32[]{:S(2)}, u32[]{:S(2)}) collective-permute-start(bf16[128,7168]{1,0:T(8,128)(2,1)S(1)} %multiply_convert_fusion.refs_2_), channel_id=1, source_target_pairs={{0,16},{4,20},{8,24},{12,28},{16,0},{20,4},{24,8},{28,12},{1,17},{... | collective-permute-start | bytes 5505032 | tf_op jit(solution)/shard_map/ppermute | solution.py:63
  208.4 106.0 %collective-permute-start.29 = (bf16[128,7168]{1,0:T(8,128)(2,1)S(1)}, bf16[128,7168]{1,0:T(8,128)(2,1)}, u32[]{:S(2)}, u32[]{:S(2)}) collective-permute-start(bf16[128,7168]{1,0:T(8,128)(2,1)S(1)} %multiply_convert_fusion.refs_2_), channel_id=1, source_target_pairs={{0,24},{4,28},{8,16},{12,20},{16,8},{20,12},{24,0},{28,4},{1,25},{... | collective-permute-start | bytes 5505032 | tf_op jit(solution)/shard_map/ppermute | solution.py:63
  212.0 160.8 %copy-start.1 = (bf16[128,4096]{1,0:T(8,128)(2,1)}, bf16[128,4096]{1,0:T(8,128)(2,1)S(1)}, u32[]{:S(2)}) copy-start(bf16[128,4096]{1,0:T(8,128)(2,1)S(1)} %multiply_convert_fusion.1.refs_2_) | copy-start | bytes 3145732
  212.0 99.2 %collective-permute-start.11 = (bf16[128,4096]{1,0:T(8,128)(2,1)S(1)}, bf16[128,4096]{1,0:T(8,128)(2,1)}, u32[]{:S(2)}, u32[]{:S(2)}) collective-permute-start(bf16[128,4096]{1,0:T(8,128)(2,1)S(1)} %multiply_convert_fusion.1.refs_2_), channel_id=1, source_target_pairs={{0,8},{4,12},{8,0},{12,4},{16,24},{20,28},{24,16},{28,20},{1,9},{5... | collective-permute-start | bytes 3145736 | tf_op jit(solution)/shard_map/ppermute | solution.py:63
  212.3 100.1 %collective-permute-start.13 = (bf16[128,4096]{1,0:T(8,128)(2,1)S(1)}, bf16[128,4096]{1,0:T(8,128)(2,1)}, u32[]{:S(2)}, u32[]{:S(2)}) collective-permute-start(bf16[128,4096]{1,0:T(8,128)(2,1)S(1)} %multiply_convert_fusion.1.refs_2_), channel_id=1, source_target_pairs={{0,16},{4,20},{8,24},{12,28},{16,0},{20,4},{24,8},{28,12},{1,17},{... | collective-permute-start | bytes 3145736 | tf_op jit(solution)/shard_map/ppermute | solution.py:63
  311.2 4.8 %collective-permute-start.17 = (bf16[128,1024]{1,0:T(8,128)(2,1)S(1)}, bf16[128,1024]{1,0:T(8,128)(2,1)S(1)}, u32[]{:S(2)}, u32[]{:S(2)}) collective-permute-start(bf16[128,1024]{1,0:T(8,128)(2,1)S(1)} %get-tuple-element.9), channel_id=1, source_target_pairs={{0,4},{4,0},{8,12},{12,8},{16,20},{20,16},{24,28},{28,24},{1,5},{5... | collective-permute-start | bytes 786440 | tf_op jit(solution)/shard_map/ppermute | solution.py:40
  312.5 7.8 %collective-permute-start.18 = (bf16[128,1024]{1,0:T(8,128)(2,1)S(1)}, bf16[128,1024]{1,0:T(8,128)(2,1)S(1)}, u32[]{:S(2)}, u32[]{:S(2)}) collective-permute-start(bf16[128,1024]{1,0:T(8,128)(2,1)S(1)} %get-tuple-element.8), channel_id=1, source_target_pairs={{0,8},{4,12},{8,0},{12,4},{16,24},{20,28},{24,16},{28,20},{1,9},{5... | collective-permute-start | bytes 786440 | tf_op jit(solution)/shard_map/ppermute | solution.py:40
  312.7 13.8 %collective-permute-start.19 = (bf16[128,1024]{1,0:T(8,128)(2,1)S(1)}, bf16[128,1024]{1,0:T(8,128)(2,1)S(1)}, u32[]{:S(2)}, u32[]{:S(2)}) collective-permute-start(bf16[128,1024]{1,0:T(8,128)(2,1)S(1)} %get-tuple-element.7), channel_id=1, source_target_pairs={{0,12},{4,8},{8,4},{12,0},{16,28},{20,24},{24,20},{28,16},{1,13},{... | collective-permute-start | bytes 786440 | tf_op jit(solution)/shard_map/ppermute | solution.py:40
  314.3 12.2 %collective-permute-start.20 = (bf16[128,1024]{1,0:T(8,128)(2,1)S(1)}, bf16[128,1024]{1,0:T(8,128)(2,1)S(1)}, u32[]{:S(2)}, u32[]{:S(2)}) collective-permute-start(bf16[128,1024]{1,0:T(8,128)(2,1)S(1)} %get-tuple-element.6), channel_id=1, source_target_pairs={{0,16},{4,20},{8,24},{12,28},{16,0},{20,4},{24,8},{28,12},{1,17},{... | collective-permute-start | bytes 786440 | tf_op jit(solution)/shard_map/ppermute | solution.py:40
  314.4 14.0 %collective-permute-start.21 = (bf16[128,1024]{1,0:T(8,128)(2,1)S(1)}, bf16[128,1024]{1,0:T(8,128)(2,1)S(1)}, u32[]{:S(2)}, u32[]{:S(2)}) collective-permute-start(bf16[128,1024]{1,0:T(8,128)(2,1)S(1)} %get-tuple-element.5), channel_id=1, source_target_pairs={{0,20},{4,16},{8,28},{12,24},{16,4},{20,0},{24,12},{28,8},{1,21},{... | collective-permute-start | bytes 786440 | tf_op jit(solution)/shard_map/ppermute | solution.py:40
  316.0 57.8 %collective-permute-start.24 = (bf16[128,7168]{1,0:T(8,128)(2,1)S(1)}, bf16[128,7168]{1,0:T(8,128)(2,1)S(1)}, u32[]{:S(2)}, u32[]{:S(2)}) collective-permute-start(bf16[128,7168]{1,0:T(8,128)(2,1)S(1)} %multiply_convert_fusion.refs_2_), channel_id=1, source_target_pairs={{0,4},{4,0},{8,12},{12,8},{16,20},{20,16},{24,28},{28,24},{1,5},{5... | collective-permute-start | bytes 5505032 | tf_op jit(solution)/shard_map/ppermute | solution.py:65
  320.2 53.6 %collective-permute-start.26 = (bf16[128,7168]{1,0:T(8,128)(2,1)}, bf16[128,7168]{1,0:T(8,128)(2,1)S(1)}, u32[]{:S(2)}, u32[]{:S(2)}) collective-permute-start(bf16[128,7168]{1,0:T(8,128)(2,1)} %collective-permute-done.25.refs_4_), channel_id=1, source_target_pairs={{0,4},{4,0},{8,12},{12,8},{16,20},{20,16},{24,28},{28,24},{1,5},{5... | collective-permute-start | bytes 5505032 | tf_op jit(solution)/shard_map/ppermute | solution.py:65
  326.5 49.7 %collective-permute-start.28 = (bf16[128,7168]{1,0:T(8,128)(2,1)}, bf16[128,7168]{1,0:T(8,128)(2,1)S(1)}, u32[]{:S(2)}, u32[]{:S(2)}) collective-permute-start(bf16[128,7168]{1,0:T(8,128)(2,1)} %collective-permute-done.27.refs_6_), channel_id=1, source_target_pairs={{0,4},{4,0},{8,12},{12,8},{16,20},{20,16},{24,28},{28,24},{1,5},{5... | collective-permute-start | bytes 5505032 | tf_op jit(solution)/shard_map/ppermute | solution.py:65
  326.5 51.0 %collective-permute-start.30 = (bf16[128,7168]{1,0:T(8,128)(2,1)}, bf16[128,7168]{1,0:T(8,128)(2,1)}, u32[]{:S(2)}, u32[]{:S(2)}) collective-permute-start(bf16[128,7168]{1,0:T(8,128)(2,1)} %collective-permute-done.29.refs_8_), channel_id=1, source_target_pairs={{0,4},{4,0},{8,12},{12,8},{16,20},{20,16},{24,28},{28,24},{1,5},{5... | collective-permute-start | bytes 5505032 | tf_op jit(solution)/shard_map/ppermute | solution.py:65
  328.4 9.1 %collective-permute-start.22 = (bf16[128,1024]{1,0:T(8,128)(2,1)S(1)}, bf16[128,1024]{1,0:T(8,128)(2,1)S(1)}, u32[]{:S(2)}, u32[]{:S(2)}) collective-permute-start(bf16[128,1024]{1,0:T(8,128)(2,1)S(1)} %get-tuple-element.4), channel_id=1, source_target_pairs={{0,24},{4,28},{8,16},{12,20},{16,8},{20,12},{24,0},{28,4},{1,25},{... | collective-permute-start | bytes 786440 | tf_op jit(solution)/shard_map/ppermute | solution.py:40
  337.4 9.8 %collective-permute-start.23 = (bf16[128,1024]{1,0:T(8,128)(2,1)S(1)}, bf16[128,1024]{1,0:T(8,128)(2,1)S(1)}, u32[]{:S(2)}, u32[]{:S(2)}) collective-permute-start(bf16[128,1024]{1,0:T(8,128)(2,1)S(1)} %get-tuple-element.3), channel_id=1, source_target_pairs={{0,28},{4,24},{8,20},{12,16},{16,12},{20,8},{24,4},{28,0},{1,29},{... | collective-permute-start | bytes 786440 | tf_op jit(solution)/shard_map/ppermute | solution.py:40
  347.2 25.6 %collective-permute-start.15 = (bf16[128,4096]{1,0:T(8,128)(2,1)S(1)}, bf16[128,4096]{1,0:T(8,128)(2,1)}, u32[]{:S(2)}, u32[]{:S(2)}) collective-permute-start(bf16[128,4096]{1,0:T(8,128)(2,1)S(1)} %multiply_convert_fusion.1.refs_2_), channel_id=1, source_target_pairs={{0,24},{4,28},{8,16},{12,20},{16,8},{20,12},{24,0},{28,4},{1,25},{... | collective-permute-start | bytes 3145736 | tf_op jit(solution)/shard_map/ppermute | solution.py:63
  347.4 26.5 %copy-start.9 = (bf16[1024,1024]{1,0:T(8,128)(2,1)}, bf16[1024,1024]{1,0:T(8,128)(2,1)S(1)}, u32[]{:S(2)}) copy-start(bf16[1024,1024]{1,0:T(8,128)(2,1)S(1)} %constant_dynamic-update-slice_fusion.7.refs_0_) | copy-start | bytes 6291460
  372.8 30.7 %collective-permute-start.10 = (bf16[128,4096]{1,0:T(8,128)(2,1)S(1)}, bf16[128,4096]{1,0:T(8,128)(2,1)}, u32[]{:S(2)}, u32[]{:S(2)}) collective-permute-start(bf16[128,4096]{1,0:T(8,128)(2,1)S(1)} %multiply_convert_fusion.1.refs_2_), channel_id=1, source_target_pairs={{0,4},{4,0},{8,12},{12,8},{16,20},{20,16},{24,28},{28,24},{1,5},{5... | collective-permute-start | bytes 3145736 | tf_op jit(solution)/shard_map/ppermute | solution.py:65
  373.8 29.7 %collective-permute-start.12 = (bf16[128,4096]{1,0:T(8,128)(2,1)}, bf16[128,4096]{1,0:T(8,128)(2,1)S(1)}, u32[]{:S(2)}, u32[]{:S(2)}) collective-permute-start(bf16[128,4096]{1,0:T(8,128)(2,1)} %collective-permute-done.11.refs_4_), channel_id=1, source_target_pairs={{0,4},{4,0},{8,12},{12,8},{16,20},{20,16},{24,28},{28,24},{1,5},{5... | collective-permute-start | bytes 3145736 | tf_op jit(solution)/shard_map/ppermute | solution.py:65
  375.0 28.5 %collective-permute-start.14 = (bf16[128,4096]{1,0:T(8,128)(2,1)}, bf16[128,4096]{1,0:T(8,128)(2,1)S(1)}, u32[]{:S(2)}, u32[]{:S(2)}) collective-permute-start(bf16[128,4096]{1,0:T(8,128)(2,1)} %collective-permute-done.13.refs_6_), channel_id=1, source_target_pairs={{0,4},{4,0},{8,12},{12,8},{16,20},{20,16},{24,28},{28,24},{1,5},{5... | collective-permute-start | bytes 3145736 | tf_op jit(solution)/shard_map/ppermute | solution.py:65
  377.5 26.0 %collective-permute-start.16 = (bf16[128,4096]{1,0:T(8,128)(2,1)}, bf16[128,4096]{1,0:T(8,128)(2,1)}, u32[]{:S(2)}, u32[]{:S(2)}) collective-permute-start(bf16[128,4096]{1,0:T(8,128)(2,1)} %collective-permute-done.15.refs_8_), channel_id=1, source_target_pairs={{0,4},{4,0},{8,12},{12,8},{16,20},{20,16},{24,28},{28,24},{1,5},{5... | collective-permute-start | bytes 3145736 | tf_op jit(solution)/shard_map/ppermute | solution.py:65
  403.5 1.4 copy-start.6
  (4 other events, 4.7 us)
Sparse Core Ops, SparseCore 0:
  9.5 44.9 all-gather.10
  58.6 170.1 all-gather.8
  230.4 29.2 all-gather.6
  261.7 129.4 all-gather.4
where the time goes:
time: 470 us; the launch traced here: 469 us
  waiting for transfers between devices  323 us (69%)
  Pallas kernels  83 us (18%)
  local copies, waits for them, and re-layouts  21.8 us (5%)
  starting transfers between devices  21.4 us (5%)
  between operations  14.3 us (3%)
  other arithmetic  5.2 us (1%)
    ppermute x3, waiting for transfers between devices, spread_cols(): lax.ppermute(piece, 'col', [(j, (j + s) % n_col) for j in range(n_col)])  133 us
    ppermute x6, waiting for transfers between devices, gather_rows(): pieces[i] = lax.ppermute(block, 'row', [(k, k ^ i) for k in range(n_row)])  122 us
    pallas_call x4, Pallas kernels, merge_rows(): pl.pallas_call(functools.partial(merge_kernel, n_row, n_col, tile, stride...  83 us
    ppermute x14, waiting for transfers between devices, spread_rows(): piece = lax.ppermute(piece, 'row', [(k, k ^ i) for k in range(n_row)])  66.7 us
    ppermute x14, starting transfers between devices, spread_rows(): piece = lax.ppermute(piece, 'row', [(k, k ^ i) for k in range(n_row)])  11.3 us
  transfers between devices with their start and end apart: 35, of which 13 were waited for; matrix products, arithmetic and copies ran while one was open for 4% of the time, Pallas kernels for 12%

commit v1 on v0

v1 whole, which is shorter than its diff:
```python
import functools

import jax
import jax.numpy as jnp
from jax import lax
from jax.experimental import pallas as pl
from jax.experimental.pallas import tpu as pltpu
from jax.sharding import PartitionSpec as P


RANK = 16
BLOCK = 512


def rows_scale(sample_counts, slot_silo, row_ids):
    slot_ids = row_ids // RANK
    silo_table = jnp.arange(slot_silo.shape[0], dtype=jnp.int32)
    silo_ids = jnp.sum(
        jnp.where(slot_ids[:, None] == silo_table[None, :], slot_silo[None, :], 0), axis=1
    )
    counts_f = sample_counts.astype(jnp.float32)
    shares = counts_f / jnp.sum(counts_f)
    return jnp.sum(
        jnp.where(silo_ids[:, None] == silo_table[None, :], shares[None, :], 0.0), axis=1
    )


def columns_of(array, index, parts):
    width = array.shape[1] // parts
    return lax.dynamic_slice_in_dim(array, index * width, width, axis=1)


def spread_rows(factors):
    n_row = lax.axis_size("row")
    mine = lax.axis_index("row")
    pieces = []
    for i in range(n_row):
        piece = jnp.concatenate([columns_of(f, mine ^ i, n_row) for f in factors], axis=1)
        if i:
            piece = lax.ppermute(piece, "row", [(k, k ^ i) for k in range(n_row)])
        pieces.append(piece)
    return pieces


def spread_cols(factors):
    n_col = lax.axis_size("col")
    mine = lax.axis_index("col")
    pieces = []
    for s in range(n_col):
        at = (mine + s) % n_col
        piece = jnp.concatenate([columns_of(f, at, n_col) for f in factors], axis=1)
        if s:
            piece = lax.ppermute(piece, "col", [(j, (j + s) % n_col) for j in range(n_col)])
        pieces.append(piece)
    return pieces


def gather_rows(block):
    n_row = lax.axis_size("row")
    pieces = [None] * n_row
    pieces[0] = block
    for i in range(2, n_row, 2):
        pieces[i] = lax.ppermute(block, "row", [(k, k ^ i) for k in range(n_row)])
    for i in range(0, n_row, 2):
        pieces[i ^ 1] = lax.ppermute(pieces[i], "row", [(k, k ^ 1) for k in range(n_row)])
    return pieces


def line_gather(block):
    n_col = lax.axis_size("col")
    up = down = block
    ups, downs = [None], [None]
    for s in range(1, n_col):
        up = lax.ppermute(up, "col", [(j, j + 1) for j in range(s - 1, n_col - 1)])
        down = lax.ppermute(down, "col", [(j, j - 1) for j in range(1, n_col + 1 - s)])
        ups.append(up)
        downs.append(down)
    return [(block,)] + [(ups[s], downs[n_col - s]) for s in range(1, n_col)]


def merge_kernel(n_row, n_col, block, tile, a_column, b_column, *refs):
    weight_ref = refs[0]
    a_refs = refs[1 : 1 + n_row]
    own_ref = refs[1 + n_row]
    pairs = refs[2 + n_row : 2 * n_col + n_row]
    out_ref, a_two, b_all, a_sems, b_sems = refs[-5:]
    depth = a_refs[0].shape[1]
    group = n_row * depth
    t, g = pl.program_id(0), pl.program_id(1)
    tiles, parts = pl.num_programs(0), b_sems.shape[0]

    def a_copies(t, slot):
        columns = pl.ds(pl.multiple_of(a_column + t * tile, 128), tile)
        return [
            pltpu.make_async_copy(
                a_refs[i].at[:, :, columns],
                a_two.at[slot, :, pl.ds(i * depth, depth)],
                a_sems.at[slot, i],
            )
            for i in range(n_row)
        ]

    def b_copy(ref, s, part):
        return pltpu.make_async_copy(
            ref.at[:, pl.ds(b_column + part * block, block)],
            b_all.at[part, pl.ds(s * group, group)],
            b_sems.at[part, s],
        )

    def b_start(part):
        mine = lax.axis_index("col")
        b_copy(own_ref, 0, part).start()
        for s in range(1, n_col):
            up_ref, down_ref = pairs[2 * (s - 1) : 2 * s]

            @pl.when(mine >= s)
            def _():
                b_copy(up_ref, s, part).start()

            @pl.when(mine < s)
            def _():
                b_copy(down_ref, s, part).start()

    @pl.when((t == 0) & (g == 0))
    def _():
        for copy in a_copies(0, 0):
            copy.start()
        for part in range(parts):
            b_start(part)

    @pl.when((g == 0) & (t + 1 < tiles))
    def _():
        for copy in a_copies(t + 1, lax.rem(t + 1, 2)):
            copy.start()

    @pl.when(t == 0)
    def _():
        for part in range(parts):

            @pl.when(g == part)
            def _():
                for s in range(n_col):
                    b_copy(own_ref, s, part).wait()

    slot = lax.rem(t, 2)

    @pl.when(g == 0)
    def _():
        for copy in a_copies(t, slot):
            copy.wait()

    update = lax.dot_general(
        b_all[g],
        a_two[slot].reshape(n_col * group, tile),
        (((0,), (0,)), ((), ())),
        preferred_element_type=jnp.float32,
    )
    out_ref[...] = (weight_ref[...].astype(jnp.float32) + update).astype(out_ref.dtype)


def merge_rows(weight, a_pieces, a_column, arrivals, b_column, first, rows, done=None):
    n_row = lax.axis_size("row")
    n_col = lax.axis_size("col")
    depth = a_pieces[0].shape[1]
    rank = n_row * n_col * depth
    width = weight.shape[1]
    block = next(b for b in range(896, 0, -128) if rows % b == 0 and first % b == 0)
    sizes = (512, 256, 128) if rows == block else (1024, 512, 256, 128)
    tile = next(size for size in sizes if width % size == 0)
    skip = first // block
    operands = [weight, *a_pieces]
    for arrival in arrivals:
        operands.extend(arrival)
    anywhere = pl.BlockSpec(memory_space=pl.ANY)
    spec = pl.BlockSpec((block, tile), lambda t, g: (g + skip, t))
    aliases = {}
    if done is not None:
        aliases = {len(operands): 0}
        operands.append(done)
    return pl.pallas_call(
        functools.partial(merge_kernel, n_row, n_col, block, tile, a_column, b_column),
        grid=(width // tile, rows // block),
        in_specs=[spec] + [anywhere] * (len(operands) - 1),
        out_specs=spec,
        out_shape=jax.ShapeDtypeStruct(weight.shape, weight.dtype),
        scratch_shapes=[
            pltpu.VMEM((2, n_col, n_row * depth, tile), jnp.bfloat16),
            pltpu.VMEM((rows // block, rank, block), jnp.bfloat16),
            pltpu.SemaphoreType.DMA((2, n_row)),
            pltpu.SemaphoreType.DMA((rows // block, n_col)),
        ],
        input_output_aliases=aliases,
        compiler_params=pltpu.CompilerParams(
            dimension_semantics=("arbitrary", "arbitrary"), vmem_limit_bytes=60 * 1024 * 1024
        ),
        cost_estimate=pl.CostEstimate(
            flops=2 * rank * rows * width,
            bytes_accessed=2 * (rank * (rows + width) + 2 * rows * width),
            transcendentals=0,
        ),
    )(*operands)


def shares_of(total, weights):
    unit = BLOCK
    while total % unit or total // unit < sum(weights):
        unit //= 2
    blocks = total // unit
    parts, left, rest = [], blocks, sum(weights)
    for weight in weights:
        part = left if weight == rest else max(1, left * weight // rest)
        part = min(part, left)
        parts.append(part * unit)
        left -= part
        rest -= weight
    return [part for part in parts if part]


def local(
    sample_counts,
    slot_silo,
    gate_weight,
    up_weight,
    down_weight,
    gate_a,
    up_a,
    down_a,
    gate_b,
    up_b,
    down_b,
):
    n_col = lax.axis_size("col")
    depth = gate_a.shape[0]

    cols = spread_cols((gate_a, up_a, down_a))
    gate_mine = jnp.concatenate(spread_rows((gate_b,)))
    rest_mine = jnp.concatenate(spread_rows((down_b, up_b)))

    mine = lax.axis_index("col")
    owners = (mine + n_col - jnp.arange(n_col, dtype=jnp.int32)) % n_col
    shards = lax.axis_index("row") * n_col + owners
    row_ids = (shards[:, None] * depth + jnp.arange(depth, dtype=jnp.int32)[None, :]).reshape(-1)
    scale = rows_scale(sample_counts, slot_silo, row_ids)

    gate_cols = gate_weight.shape[1]
    both_cols = gate_cols + up_weight.shape[1]

    def gathered(start, end):
        block = jnp.concatenate([piece[:, start:end] for piece in cols])
        block = (scale[:, None] * block.astype(jnp.float32)).astype(jnp.bfloat16)
        return gather_rows(block.reshape(n_col, depth, end - start))

    mlp_pieces = gathered(0, both_cols)
    down_pieces = gathered(both_cols, both_cols + down_weight.shape[1])

    down_rows = down_weight.shape[0]

    def merged(weight, a_pieces, a_column, source, start, weights):
        done, first = None, 0
        for rows in shares_of(weight.shape[0], weights):
            at = start + first
            arrivals = line_gather(source[:, at : at + rows])
            done = merge_rows(weight, a_pieces, a_column, arrivals, 0, first, rows, done)
            first += rows
        return done

    merged_gate = merged(gate_weight, mlp_pieces, 0, gate_mine, 0, (1, 1))
    merged_up = merged(up_weight, mlp_pieces, gate_cols, rest_mine, down_rows, (4, 3))

    arrivals = line_gather(rest_mine[:, :down_rows])
    merged_down = merge_rows(down_weight, down_pieces, 0, arrivals, 0, 0, down_rows)
    return merged_gate, merged_up, merged_down


def solution(mesh):
    return jax.shard_map(
        local,
        mesh=mesh,
        in_specs=(
            P(),
            P(),
            P("row", "col"),
            P("row", "col"),
            P("row", "col"),
            P(("row", "col"), None),
            P(("row", "col"), None),
            P(("row", "col"), None),
            P(("row", "col"), None),
            P(("row", "col"), None),
            P(("row", "col"), None),
        ),
        out_specs=(P("row", "col"), P("row", "col"), P("row", "col")),
        check_vma=False,
    )
```

time: 470 us -> 488 us (1.038)
  the two profiles are of different devices: /device:TPU:15 before, /device:TPU:0 now
where the time goes in v1:
time: 488 us; the launch traced here: 485 us
  waiting for transfers between devices  286 us (59%)
  starting transfers between devices  85.7 us (18%)
  Pallas kernels  82.5 us (17%)
  local copies, waits for them, and re-layouts  23.4 us (5%)
  other arithmetic  6.19 us (1%)
    ppermute x15, waiting for transfers between devices, line_gather(): lax.ppermute(down, 'col', [(j, j - 1) for j in range(1, n_col + 1 - s)])  172 us
    pallas_call x5, Pallas kernels, merge_rows(): pl.pallas_call(functools.partial(merge_kernel, n_row, n_col, block, tile,...  82.5 us
    ppermute x14, waiting for transfers between devices, spread_rows(): piece = lax.ppermute(piece, 'row', [(k, k ^ i) for k in range(n_row)])  46.8 us
    ppermute x6, waiting for transfers between devices, gather_rows(): pieces[i] = lax.ppermute(block, 'row', [(k, k ^ i) for k in range(n_row)])  44.3 us
    ppermute x15, starting transfers between devices, line_gather(): up = lax.ppermute(up, 'col', [(j, j + 1) for j in range(s - 1, n_col - 1)])  34.8 us
    ppermute x15, waiting for transfers between devices, line_gather(): up = lax.ppermute(up, 'col', [(j, j + 1) for j in range(s - 1, n_col - 1)])  22 us
    ppermute x15, starting transfers between devices, line_gather(): lax.ppermute(down, 'col', [(j, j - 1) for j in range(1, n_col + 1 - s)])  19.3 us
    ppermute x14, starting transfers between devices, spread_rows(): piece = lax.ppermute(piece, 'row', [(k, k ^ i) for k in range(n_row)])  16.9 us
  transfers between devices with their start and end apart: 61, of which 20 were waited for; matrix products, arithmetic and copies ran while one was open for 5% of the time, Pallas kernels for 12%

profile of v1, /device:TPU:0, one launch (start us, length us, event | category | flops | bytes accessed | tf_op | source)
XLA Modules:
  0.0 485.4 jit_solution(17784233322449445228)
XLA Ops:
  0.7 2.5 constant_dynamic-slice_fusion.34
  4.9 5.1 %collective-permute-start.2 = (bf16[32,11264]{1,0:T(8,128)(2,1)}, bf16[32,11264]{1,0:T(8,128)(2,1)}, u32[]{:S(2)}, u32[]{:S(2)}) collective-permute-start(bf16[32,11264]{1,0:T(8,128)(2,1)} %pad_maximum_fusion.4), channel_id=1, source_target_pairs={{0,3},{1,0},{2,1},{3,2},{4,7},{5,4},{6,5},{7,6},{8,11},{9,8},{10,9... | collective-permute-start | bytes 2162696 | tf_op jit(solution)/shard_map/ppermute | solution.py:53
  12.8 2.7 constant_dynamic-slice_fusion.16
  15.5 1.5 collective-permute-start.11
  17.2 2.4 constant_dynamic-slice_fusion
  24.5 1.6 collective-permute-start.13
  27.0 3.7 collective-permute-done.12
  30.7 1.6 collective-permute-start.14
  32.4 2.4 collective-permute-start.15
  34.9 8.0 %collective-permute-done.14 = bf16[32,3584]{1,0:T(8,128)(2,1)S(1)} collective-permute-done((bf16[32,3584]{1,0:T(8,128)(2,1)S(1)}, bf16[32,3584]{1,0:T(8,128)(2,1)S(1)}, u32[]{:S(2)}, u32[]{:S(2)}) %collective-permute-start.14) | collective-permute-done | bytes 229408 | tf_op jit(solution)/shard_map/ppermute | solution.py:40
  42.9 1.6 collective-permute-start.16
  44.6 6.0 %collective-permute-done.16 = bf16[32,3584]{1,0:T(8,128)(2,1)S(1)} collective-permute-done((bf16[32,3584]{1,0:T(8,128)(2,1)S(1)}, bf16[32,3584]{1,0:T(8,128)(2,1)S(1)}, u32[]{:S(2)}, u32[]{:S(2)}) %collective-permute-start.16) | collective-permute-done | bytes 229408 | tf_op jit(solution)/shard_map/ppermute | solution.py:40
  50.6 1.5 collective-permute-start.30
  53.5 6.7 %collective-permute-done.30 = bf16[32,4608]{1,0:T(8,128)(2,1)S(1)} collective-permute-done((bf16[32,4608]{1,0:T(8,128)(2,1)S(1)}, bf16[32,4608]{1,0:T(8,128)(2,1)S(1)}, u32[]{:S(2)}, u32[]{:S(2)}) %collective-permute-start.30) | collective-permute-done | bytes 294944 | tf_op jit(solution)/shard_map/ppermute | solution.py:40
  60.2 1.5 collective-permute-start.32
  61.7 5.1 %collective-permute-done.31 = bf16[32,4608]{1,0:T(8,128)(2,1)S(1)} collective-permute-done((bf16[32,4608]{1,0:T(8,128)(2,1)S(1)}, bf16[32,4608]{1,0:T(8,128)(2,1)S(1)}, u32[]{:S(2)}, u32[]{:S(2)}) %collective-permute-start.31) | collective-permute-done | bytes 294944 | tf_op jit(solution)/shard_map/ppermute | solution.py:40
  67.9 2.2 collective-permute-done.32
  71.4 11.1 %collective-permute-done.33 = bf16[32,4608]{1,0:T(8,128)(2,1)S(1)} collective-permute-done((bf16[32,4608]{1,0:T(8,128)(2,1)S(1)}, bf16[32,4608]{1,0:T(8,128)(2,1)S(1)}, u32[]{:S(2)}, u32[]{:S(2)}) %collective-permute-start.33) | collective-permute-done | bytes 294944 | tf_op jit(solution)/shard_map/ppermute | solution.py:40
  83.6 4.8 collective-permute-start.23
  88.5 3.9 collective-permute-done.35
  93.8 5.5 %collective-permute-start.36 = (bf16[256,1536]{1,0:T(8,128)(2,1)S(1)}, bf16[256,1536]{1,0:T(8,128)(2,1)}, u32[]{:S(2)}, u32[]{:S(2)}) collective-permute-start(bf16[256,1536]{1,0:T(8,128)(2,1)S(1)} %slice.49.refs_9_), channel_id=1, source_target_pairs={{0,1},{1,2},{2,3},{4,5},{5,6},{6,7},{8,9},{9,10},{10,11},{12,13},{... | collective-permute-start | bytes 2359304 | tf_op jit(solution)/shard_map/ppermute | solution.py:74
  100.8 3.8 collective-permute-start.55
  106.2 1.7 slice.50.refs_9_
  111.2 22.0 %collective-permute-done.55.refs_10_ = bf16[256,1024]{1,0:T(8,128)(2,1)} collective-permute-done((bf16[256,1024]{1,0:T(8,128)(2,1)}, bf16[256,1024]{1,0:T(8,128)(2,1)}, u32[]{:S(2)}, u32[]{:S(2)}) %collective-permute-start.55) | collective-permute-done | bytes 524320 | tf_op jit(solution)/shard_map/ppermute | solution.py:74
  133.1 4.4 collective-permute-start.17
  140.2 5.2 %collective-permute-start.42 = (bf16[256,2048]{1,0:T(8,128)(2,1)S(1)}, bf16[256,2048]{1,0:T(8,128)(2,1)S(1)}, u32[]{:S(2)}, u32[]{:S(2)}) collective-permute-start(bf16[256,2048]{1,0:T(8,128)(2,1)S(1)} %slice.50.refs_9_), channel_id=1, source_target_pairs={{0,1},{1,2},{2,3},{4,5},{5,6},{6,7},{8,9},{9,10},{10,11},{12,13},{... | collective-permute-start | bytes 3145736 | tf_op jit(solution)/shard_map/ppermute | solution.py:74
  147.1 35.3 %collective-permute-done.37.refs_15_ = bf16[256,1536]{1,0:T(8,128)(2,1)S(1)} collective-permute-done((bf16[256,1536]{1,0:T(8,128)(2,1)S(1)}, bf16[256,1536]{1,0:T(8,128)(2,1)S(1)}, u32[]{:S(2)}, u32[]{:S(2)}) %collective-permute-start.37) | collective-permute-done | bytes 786464 | tf_op jit(solution)/shard_map/ppermute | solution.py:75
  184.5 1.6 collective-permute-start.4
  186.0 18.8 %collective-permute-done.43.refs_15_ = bf16[256,2048]{1,0:T(8,128)(2,1)S(1)} collective-permute-done((bf16[256,2048]{1,0:T(8,128)(2,1)S(1)}, bf16[256,2048]{1,0:T(8,128)(2,1)S(1)}, u32[]{:S(2)}, u32[]{:S(2)}) %collective-permute-start.43) | collective-permute-done | bytes 1048608 | tf_op jit(solution)/shard_map/ppermute | solution.py:75
  205.0 9.4 %collective-permute-done.57.refs_13_ = bf16[256,1024]{1,0:T(8,128)(2,1)S(1)} collective-permute-done((bf16[256,1024]{1,0:T(8,128)(2,1)}, bf16[256,1024]{1,0:T(8,128)(2,1)S(1)}, u32[]{:S(2)}, u32[]{:S(2)}) %collective-permute-start.57) | collective-permute-done | bytes 524320 | tf_op jit(solution)/shard_map/ppermute | solution.py:75
  222.6 26.5 %collective-permute-done.6.refs_5_ = bf16[4,32,4096]{2,1,0:T(8,128)(2,1)S(1)} collective-permute-done((bf16[4,32,4096]{2,1,0:T(8,128)(2,1)S(1)}, bf16[4,32,4096]{2,1,0:T(8,128)(2,1)S(1)}, u32[]{:S(2)}, u32[]{:S(2)}) %collective-permute-start.6) | collective-permute-done | bytes 1048608 | tf_op jit(solution)/shard_map/ppermute | solution.py:63
  251.2 1.6 collective-permute-start.21
  254.5 3.6 collective-permute-done.38.refs_13_
  258.1 2.4 collective-permute-start.51
  260.5 28.7 %collective-permute-done.58.refs_11_ = bf16[256,1024]{1,0:T(8,128)(2,1)S(1)} collective-permute-done((bf16[256,1024]{1,0:T(8,128)(2,1)S(1)}, bf16[256,1024]{1,0:T(8,128)(2,1)S(1)}, u32[]{:S(2)}, u32[]{:S(2)}) %collective-permute-start.58) | collective-permute-done | bytes 524320 | tf_op jit(solution)/shard_map/ppermute | solution.py:75
  289.2 1.5 collective-permute-start.53
  292.1 1.7 collective-permute-start.46
  293.7 21.1 %collective-permute-done.44.refs_13_ = bf16[256,2048]{1,0:T(8,128)(2,1)} collective-permute-done((bf16[256,2048]{1,0:T(8,128)(2,1)S(1)}, bf16[256,2048]{1,0:T(8,128)(2,1)}, u32[]{:S(2)}, u32[]{:S(2)}) %collective-permute-start.44) | collective-permute-done | bytes 1048608 | tf_op jit(solution)/shard_map/ppermute | solution.py:75
  316.6 16.9 %collective-permute-done.51.refs_5_ = bf16[4,32,7168]{2,1,0:T(8,128)(2,1)S(1)} collective-permute-done((bf16[4,32,7168]{2,1,0:T(8,128)(2,1)S(1)}, bf16[4,32,7168]{2,1,0:T(8,128)(2,1)S(1)}, u32[]{:S(2)}, u32[]{:S(2)}) %collective-permute-start.51) | collective-permute-done | bytes 1835040 | tf_op jit(solution)/shard_map/ppermute | solution.py:63
  335.1 1.6 collective-permute-done.26.refs_11_
  338.0 1.6 collective-permute-start.22
  343.3 1.6 collective-permute-start.47
  345.0 12.5 %shard_map.130.refs_16_ = bf16[3584,2048]{1,0:T(8,128)(2,1)} custom-call(bf16[3584,2048]{1,0:T(8,128)(2,1)} %refs_0_.6, bf16[4,32,4096]{2,1,0:T(8,128)(2,1)} %copy-done, bf16[4,32,4096]{2,1,0:T(8,128)(2,1)} %copy-done.1, bf16[4,32,4096]{2,1,0:T(8,128)(2,1)} %copy-done.2, bf16[4,32,4096]{2,1,0:T(8,128)(2,1)} %copy-done.5, bf16[4,32,4096]{2,1,0:T(8,128)(2,1)} %copy-done.3, ...), custom_call_target="tpu_custom_call" | custom-call | flops 6442450944 | bytes 19922944 | tf_op jit(solution)/shard_map/pallas_call | solution.py:180
  357.5 53.9 %collective-permute-done.39.refs_11_ = bf16[256,1536]{1,0:T(8,128)(2,1)} collective-permute-done((bf16[256,1536]{1,0:T(8,128)(2,1)}, bf16[256,1536]{1,0:T(8,128)(2,1)}, u32[]{:S(2)}, u32[]{:S(2)}) %collective-permute-start.39) | collective-permute-done | bytes 786464 | tf_op jit(solution)/shard_map/ppermute | solution.py:75
  412.4 16.0 %shard_map.131 = bf16[3584,2048]{1,0:T(8,128)(2,1)} custom-call(bf16[3584,2048]{1,0:T(8,128)(2,1)} %refs_0_.6, bf16[4,32,4096]{2,1,0:T(8,128)(2,1)} %copy-done, bf16[4,32,4096]{2,1,0:T(8,128)(2,1)} %copy-done.1, bf16[4,32,4096]{2,1,0:T(8,128)(2,1)} %copy-done.2, bf16[4,32,4096]{2,1,0:T(8,128)(2,1)} %copy-done.5, ...), custom_call_target="tpu_custom_call", output_to_operand_aliasing={{}: (16, {})} | custom-call | flops 8589934592 | bytes 25165824 | tf_op jit(solution)/shard_map/pallas_call | solution.py:180
  429.4 16.0 %shard_map.132.refs_16_ = bf16[3584,2048]{1,0:T(8,128)(2,1)} custom-call(bf16[3584,2048]{1,0:T(8,128)(2,1)} %refs_0_.8, bf16[4,32,4096]{2,1,0:T(8,128)(2,1)} %copy-done, bf16[4,32,4096]{2,1,0:T(8,128)(2,1)} %copy-done.1, bf16[4,32,4096]{2,1,0:T(8,128)(2,1)} %copy-done.2, bf16[4,32,4096]{2,1,0:T(8,128)(2,1)} %copy-done.5, bf16[4,32,4096]{2,1,0:T(8,128)(2,1)} %copy-done.3, ...), custom_call_target="tpu_custom_call" | custom-call | flops 8589934592 | bytes 25165824 | tf_op jit(solution)/shard_map/pallas_call | solution.py:180
  446.3 12.9 %shard_map.133 = bf16[3584,2048]{1,0:T(8,128)(2,1)} custom-call(bf16[3584,2048]{1,0:T(8,128)(2,1)} %refs_0_.8, bf16[4,32,4096]{2,1,0:T(8,128)(2,1)} %copy-done, bf16[4,32,4096]{2,1,0:T(8,128)(2,1)} %copy-done.1, bf16[4,32,4096]{2,1,0:T(8,128)(2,1)} %copy-done.2, bf16[4,32,4096]{2,1,0:T(8,128)(2,1)} %copy-done.5, ...), custom_call_target="tpu_custom_call", output_to_operand_aliasing={{}: (16, {})} | custom-call | flops 6442450944 | bytes 19922944 | tf_op jit(solution)/shard_map/pallas_call | solution.py:180
  460.1 25.2 %shard_map.134 = bf16[1024,7168]{1,0:T(8,128)(2,1)} custom-call(bf16[1024,7168]{1,0:T(8,128)(2,1)} %refs_0_.9, bf16[4,32,7168]{2,1,0:T(8,128)(2,1)} %copy-done.14, bf16[4,32,7168]{2,1,0:T(8,128)(2,1)} %collective-permute-done.48.refs_2_, bf16[4,32,7168]{2,1,0:T(8,128)(2,1)} %copy-done.36, bf16[4,32,7168]{2,1,0:T(8,128)(2,1)} %collective-permute-done.50.refs_4_, ...), custom_call_target="tpu_custom_call" | custom-call | flops 15032385536 | bytes 46137344 | tf_op jit(solution)/shard_map/pallas_call | solution.py:180
  (225 shorter events, 54.4 us)
Async XLA Ops:
  4.9 88.9 %collective-permute-start.2 = (bf16[32,11264]{1,0:T(8,128)(2,1)}, bf16[32,11264]{1,0:T(8,128)(2,1)}, u32[]{:S(2)}, u32[]{:S(2)}) collective-permute-start(bf16[32,11264]{1,0:T(8,128)(2,1)} %pad_maximum_fusion.4), channel_id=1, source_target_pairs={{0,3},{1,0},{2,1},{3,2},{4,7},{5,4},{6,5},{7,6},{8,11},{9,8},{10,9... | collective-permute-start | bytes 2162696 | tf_op jit(solution)/shard_map/ppermute | solution.py:53
  10.9 89.9 %collective-permute-start.1 = (bf16[32,11264]{1,0:T(8,128)(2,1)}, bf16[32,11264]{1,0:T(8,128)(2,1)}, u32[]{:S(2)}, u32[]{:S(2)}) collective-permute-start(bf16[32,11264]{1,0:T(8,128)(2,1)} %pad_maximum_fusion.3), channel_id=1, source_target_pairs={{0,2},{1,3},{2,0},{3,1},{4,6},{5,7},{6,4},{7,5},{8,10},{9,11},{10,... | collective-permute-start | bytes 2162696 | tf_op jit(solution)/shard_map/ppermute | solution.py:53
  11.8 92.8 %collective-permute-start = (bf16[32,11264]{1,0:T(8,128)(2,1)}, bf16[32,11264]{1,0:T(8,128)(2,1)}, u32[]{:S(2)}, u32[]{:S(2)}) collective-permute-start(bf16[32,11264]{1,0:T(8,128)(2,1)} %pad_maximum_fusion.2), channel_id=1, source_target_pairs={{0,1},{1,2},{2,3},{3,0},{4,5},{5,6},{6,7},{7,4},{8,9},{9,10},{10,1... | collective-permute-start | bytes 2162696 | tf_op jit(solution)/shard_map/ppermute | solution.py:53
  30.7 12.2 %collective-permute-start.14 = (bf16[32,3584]{1,0:T(8,128)(2,1)S(1)}, bf16[32,3584]{1,0:T(8,128)(2,1)S(1)}, u32[]{:S(2)}, u32[]{:S(2)}) collective-permute-start(bf16[32,3584]{1,0:T(8,128)(2,1)S(1)} %copy-done.33), channel_id=1, source_target_pairs={{0,20},{4,16},{8,28},{12,24},{16,4},{20,0},{24,12},{28,8},{1,21},{... | collective-permute-start | bytes 688136 | tf_op jit(solution)/shard_map/ppermute | solution.py:40
  52.3 14.6 %collective-permute-start.31 = (bf16[32,4608]{1,0:T(8,128)(2,1)S(1)}, bf16[32,4608]{1,0:T(8,128)(2,1)S(1)}, u32[]{:S(2)}, u32[]{:S(2)}) collective-permute-start(bf16[32,4608]{1,0:T(8,128)(2,1)S(1)} %pad_maximum_fusion.7), channel_id=1, source_target_pairs={{0,12},{4,8},{8,4},{12,0},{16,28},{20,24},{24,20},{28,16},{1,13},{... | collective-permute-start | bytes 884744 | tf_op jit(solution)/shard_map/ppermute | solution.py:40
  66.8 15.7 %collective-permute-start.33 = (bf16[32,4608]{1,0:T(8,128)(2,1)S(1)}, bf16[32,4608]{1,0:T(8,128)(2,1)S(1)}, u32[]{:S(2)}, u32[]{:S(2)}) collective-permute-start(bf16[32,4608]{1,0:T(8,128)(2,1)S(1)} %pad_maximum_fusion.9), channel_id=1, source_target_pairs={{0,20},{4,16},{8,28},{12,24},{16,4},{20,0},{24,12},{28,8},{1,21},{... | collective-permute-start | bytes 884744 | tf_op jit(solution)/shard_map/ppermute | solution.py:40
  70.1 13.6 %collective-permute-start.34 = (bf16[32,4608]{1,0:T(8,128)(2,1)S(1)}, bf16[32,4608]{1,0:T(8,128)(2,1)S(1)}, u32[]{:S(2)}, u32[]{:S(2)}) collective-permute-start(bf16[32,4608]{1,0:T(8,128)(2,1)S(1)} %pad_maximum_fusion.10), channel_id=1, source_target_pairs={{0,24},{4,28},{8,16},{12,20},{16,8},{20,12},{24,0},{28,4},{1,25},{... | collective-permute-start | bytes 884744 | tf_op jit(solution)/shard_map/ppermute | solution.py:40
  83.6 55.3 %collective-permute-start.23 = (bf16[256,1536]{1,0:T(8,128)(2,1)S(1)}, bf16[256,1536]{1,0:T(8,128)(2,1)}, u32[]{:S(2)}, u32[]{:S(2)}) collective-permute-start(bf16[256,1536]{1,0:T(8,128)(2,1)S(1)} %slice.48.refs_9_), channel_id=1, source_target_pairs={{0,1},{1,2},{2,3},{4,5},{5,6},{6,7},{8,9},{9,10},{10,11},{12,13},{... | collective-permute-start | bytes 2359304 | tf_op jit(solution)/shard_map/ppermute | solution.py:74
  92.4 47.8 %collective-permute-start.24 = (bf16[256,1536]{1,0:T(8,128)(2,1)S(1)}, bf16[256,1536]{1,0:T(8,128)(2,1)}, u32[]{:S(2)}, u32[]{:S(2)}) collective-permute-start(bf16[256,1536]{1,0:T(8,128)(2,1)S(1)} %slice.48.refs_9_), channel_id=1, source_target_pairs={{1,0},{2,1},{3,2},{5,4},{6,5},{7,6},{9,8},{10,9},{11,10},{13,12},{... | collective-permute-start | bytes 2359304 | tf_op jit(solution)/shard_map/ppermute | solution.py:75
  93.8 51.7 %collective-permute-start.36 = (bf16[256,1536]{1,0:T(8,128)(2,1)S(1)}, bf16[256,1536]{1,0:T(8,128)(2,1)}, u32[]{:S(2)}, u32[]{:S(2)}) collective-permute-start(bf16[256,1536]{1,0:T(8,128)(2,1)S(1)} %slice.49.refs_9_), channel_id=1, source_target_pairs={{0,1},{1,2},{2,3},{4,5},{5,6},{6,7},{8,9},{9,10},{10,11},{12,13},{... | collective-permute-start | bytes 2359304 | tf_op jit(solution)/shard_map/ppermute | solution.py:74
  100.8 32.3 %collective-permute-start.55 = (bf16[256,1024]{1,0:T(8,128)(2,1)}, bf16[256,1024]{1,0:T(8,128)(2,1)}, u32[]{:S(2)}, u32[]{:S(2)}) collective-permute-start(bf16[256,1024]{1,0:T(8,128)(2,1)} %slice.54.refs_9_), channel_id=1, source_target_pairs={{0,1},{1,2},{2,3},{4,5},{5,6},{6,7},{8,9},{9,10},{10,11},{12,13},{... | collective-permute-start | bytes 1572872 | tf_op jit(solution)/shard_map/ppermute | solution.py:74
  104.6 33.0 %collective-permute-start.56 = (bf16[256,1024]{1,0:T(8,128)(2,1)}, bf16[256,1024]{1,0:T(8,128)(2,1)}, u32[]{:S(2)}, u32[]{:S(2)}) collective-permute-start(bf16[256,1024]{1,0:T(8,128)(2,1)} %slice.54.refs_9_), channel_id=1, source_target_pairs={{1,0},{2,1},{3,2},{5,4},{6,5},{7,6},{9,8},{10,9},{11,10},{13,12},{... | collective-permute-start | bytes 1572872 | tf_op jit(solution)/shard_map/ppermute | solution.py:75
  133.1 49.3 %collective-permute-start.17 = (bf16[256,2048]{1,0:T(8,128)(2,1)S(1)}, bf16[256,2048]{1,0:T(8,128)(2,1)S(1)}, u32[]{:S(2)}, u32[]{:S(2)}) collective-permute-start(bf16[256,2048]{1,0:T(8,128)(2,1)S(1)} %slice.47.refs_9_), channel_id=1, source_target_pairs={{0,1},{1,2},{2,3},{4,5},{5,6},{6,7},{8,9},{9,10},{10,11},{12,13},{... | collective-permute-start | bytes 3145736 | tf_op jit(solution)/shard_map/ppermute | solution.py:74
  137.6 46.1 %collective-permute-start.18 = (bf16[256,2048]{1,0:T(8,128)(2,1)S(1)}, bf16[256,2048]{1,0:T(8,128)(2,1)S(1)}, u32[]{:S(2)}, u32[]{:S(2)}) collective-permute-start(bf16[256,2048]{1,0:T(8,128)(2,1)S(1)} %slice.47.refs_9_), channel_id=1, source_target_pairs={{1,0},{2,1},{3,2},{5,4},{6,5},{7,6},{9,8},{10,9},{11,10},{13,12},{... | collective-permute-start | bytes 3145736 | tf_op jit(solution)/shard_map/ppermute | solution.py:75
  138.9 43.5 %collective-permute-start.37 = (bf16[256,1536]{1,0:T(8,128)(2,1)S(1)}, bf16[256,1536]{1,0:T(8,128)(2,1)S(1)}, u32[]{:S(2)}, u32[]{:S(2)}) collective-permute-start(bf16[256,1536]{1,0:T(8,128)(2,1)S(1)} %slice.49.refs_9_), channel_id=1, source_target_pairs={{1,0},{2,1},{3,2},{5,4},{6,5},{7,6},{9,8},{10,9},{11,10},{13,12},{... | collective-permute-start | bytes 2359304 | tf_op jit(solution)/shard_map/ppermute | solution.py:75
  140.2 44.2 %collective-permute-start.42 = (bf16[256,2048]{1,0:T(8,128)(2,1)S(1)}, bf16[256,2048]{1,0:T(8,128)(2,1)S(1)}, u32[]{:S(2)}, u32[]{:S(2)}) collective-permute-start(bf16[256,2048]{1,0:T(8,128)(2,1)S(1)} %slice.50.refs_9_), channel_id=1, source_target_pairs={{0,1},{1,2},{2,3},{4,5},{5,6},{6,7},{8,9},{9,10},{10,11},{12,13},{... | collective-permute-start | bytes 3145736 | tf_op jit(solution)/shard_map/ppermute | solution.py:74
  145.5 59.3 %collective-permute-start.43 = (bf16[256,2048]{1,0:T(8,128)(2,1)S(1)}, bf16[256,2048]{1,0:T(8,128)(2,1)S(1)}, u32[]{:S(2)}, u32[]{:S(2)}) collective-permute-start(bf16[256,2048]{1,0:T(8,128)(2,1)S(1)} %slice.50.refs_9_), channel_id=1, source_target_pairs={{1,0},{2,1},{3,2},{5,4},{6,5},{7,6},{9,8},{10,9},{11,10},{13,12},{... | collective-permute-start | bytes 3145736 | tf_op jit(solution)/shard_map/ppermute | solution.py:75
  182.4 37.9 %collective-permute-start.3 = (bf16[4,32,4096]{2,1,0:T(8,128)(2,1)S(1)}, bf16[4,32,4096]{2,1,0:T(8,128)(2,1)S(1)}, u32[]{:S(2)}, u32[]{:S(2)}) collective-permute-start(bf16[4,32,4096]{2,1,0:T(8,128)(2,1)S(1)} %fusion.1.refs_1_), channel_id=1, source_target_pairs={{0,4},{4,0},{8,12},{12,8},{16,20},{20,16},{24,28},{28,24},{1,5},{5... | collective-permute-start | bytes 3145736 | tf_op jit(solution)/shard_map/ppermute | solution.py:65
  182.4 32.0 %collective-permute-start.57 = (bf16[256,1024]{1,0:T(8,128)(2,1)}, bf16[256,1024]{1,0:T(8,128)(2,1)S(1)}, u32[]{:S(2)}, u32[]{:S(2)}) collective-permute-start(bf16[256,1024]{1,0:T(8,128)(2,1)} %collective-permute-done.56.refs_15_), channel_id=1, source_target_pairs={{1,0},{2,1},{5,4},{6,5},{9,8},{10,9},{13,12},{14,13},{17,16},{18,1... | collective-permute-start | bytes 1572872 | tf_op jit(solution)/shard_map/ppermute | solution.py:75
  183.7 35.3 %collective-permute-start.59 = (bf16[256,1024]{1,0:T(8,128)(2,1)}, bf16[256,1024]{1,0:T(8,128)(2,1)S(1)}, u32[]{:S(2)}, u32[]{:S(2)}) collective-permute-start(bf16[256,1024]{1,0:T(8,128)(2,1)} %collective-permute-done.55.refs_10_), channel_id=1, source_target_pairs={{1,2},{2,3},{5,6},{6,7},{9,10},{10,11},{13,14},{14,15},{17,18},{18... | collective-permute-start | bytes 1572872 | tf_op jit(solution)/shard_map/ppermute | solution.py:74
  184.5 36.8 %collective-permute-start.4 = (bf16[4,32,4096]{2,1,0:T(8,128)(2,1)S(1)}, bf16[4,32,4096]{2,1,0:T(8,128)(2,1)S(1)}, u32[]{:S(2)}, u32[]{:S(2)}) collective-permute-start(bf16[4,32,4096]{2,1,0:T(8,128)(2,1)S(1)} %fusion.1.refs_1_), channel_id=1, source_target_pairs={{0,8},{4,12},{8,0},{12,4},{16,24},{20,28},{24,16},{28,20},{1,9},{5... | collective-permute-start | bytes 3145736 | tf_op jit(solution)/shard_map/ppermute | solution.py:63
  204.9 44.2 %collective-permute-start.6 = (bf16[4,32,4096]{2,1,0:T(8,128)(2,1)S(1)}, bf16[4,32,4096]{2,1,0:T(8,128)(2,1)S(1)}, u32[]{:S(2)}, u32[]{:S(2)}) collective-permute-start(bf16[4,32,4096]{2,1,0:T(8,128)(2,1)S(1)} %fusion.1.refs_1_), channel_id=1, source_target_pairs={{0,16},{4,20},{8,24},{12,28},{16,0},{20,4},{24,8},{28,12},{1,17},{... | collective-permute-start | bytes 3145736 | tf_op jit(solution)/shard_map/ppermute | solution.py:63
  214.4 35.4 %collective-permute-start.8 = (bf16[4,32,4096]{2,1,0:T(8,128)(2,1)S(1)}, bf16[4,32,4096]{2,1,0:T(8,128)(2,1)S(1)}, u32[]{:S(2)}, u32[]{:S(2)}) collective-permute-start(bf16[4,32,4096]{2,1,0:T(8,128)(2,1)S(1)} %fusion.1.refs_1_), channel_id=1, source_target_pairs={{0,24},{4,28},{8,16},{12,20},{16,8},{20,12},{24,0},{28,4},{1,25},{... | collective-permute-start | bytes 3145736 | tf_op jit(solution)/shard_map/ppermute | solution.py:63
  219.0 32.1 %collective-permute-start.25 = (bf16[256,1536]{1,0:T(8,128)(2,1)}, bf16[256,1536]{1,0:T(8,128)(2,1)S(1)}, u32[]{:S(2)}, u32[]{:S(2)}) collective-permute-start(bf16[256,1536]{1,0:T(8,128)(2,1)} %collective-permute-done.24.refs_15_), channel_id=1, source_target_pairs={{1,0},{2,1},{5,4},{6,5},{9,8},{10,9},{13,12},{14,13},{17,16},{18,1... | collective-permute-start | bytes 2359304 | tf_op jit(solution)/shard_map/ppermute | solution.py:75
  220.3 32.5 %collective-permute-start.27 = (bf16[256,1536]{1,0:T(8,128)(2,1)}, bf16[256,1536]{1,0:T(8,128)(2,1)S(1)}, u32[]{:S(2)}, u32[]{:S(2)}) collective-permute-start(bf16[256,1536]{1,0:T(8,128)(2,1)} %collective-permute-done.23.refs_10_), channel_id=1, source_target_pairs={{1,2},{2,3},{5,6},{6,7},{9,10},{10,11},{13,14},{14,15},{17,18},{18... | collective-permute-start | bytes 2359304 | tf_op jit(solution)/shard_map/ppermute | solution.py:74
  221.3 36.8 %collective-permute-start.38 = (bf16[256,1536]{1,0:T(8,128)(2,1)S(1)}, bf16[256,1536]{1,0:T(8,128)(2,1)}, u32[]{:S(2)}, u32[]{:S(2)}) collective-permute-start(bf16[256,1536]{1,0:T(8,128)(2,1)S(1)} %collective-permute-done.37.refs_15_), channel_id=1, source_target_pairs={{1,0},{2,1},{5,4},{6,5},{9,8},{10,9},{13,12},{14,13},{17,16},{18,1... | collective-permute-start | bytes 2359304 | tf_op jit(solution)/shard_map/ppermute | solution.py:75
  249.8 40.9 %collective-permute-start.19 = (bf16[256,2048]{1,0:T(8,128)(2,1)S(1)}, bf16[256,2048]{1,0:T(8,128)(2,1)}, u32[]{:S(2)}, u32[]{:S(2)}) collective-permute-start(bf16[256,2048]{1,0:T(8,128)(2,1)S(1)} %collective-permute-done.18.refs_15_), channel_id=1, source_target_pairs={{1,0},{2,1},{5,4},{6,5},{9,8},{10,9},{13,12},{14,13},{17,16},{18,1... | collective-permute-start | bytes 3145736 | tf_op jit(solution)/shard_map/ppermute | solution.py:75
  251.2 40.9 %collective-permute-start.21 = (bf16[256,2048]{1,0:T(8,128)(2,1)S(1)}, bf16[256,2048]{1,0:T(8,128)(2,1)}, u32[]{:S(2)}, u32[]{:S(2)}) collective-permute-start(bf16[256,2048]{1,0:T(8,128)(2,1)S(1)} %collective-permute-done.17.refs_10_), channel_id=1, source_target_pairs={{1,2},{2,3},{5,6},{6,7},{9,10},{10,11},{13,14},{14,15},{17,18},{18... | collective-permute-start | bytes 3145736 | tf_op jit(solution)/shard_map/ppermute | solution.py:74
  252.8 36.4 %collective-permute-start.58 = (bf16[256,1024]{1,0:T(8,128)(2,1)S(1)}, bf16[256,1024]{1,0:T(8,128)(2,1)S(1)}, u32[]{:S(2)}, u32[]{:S(2)}) collective-permute-start(bf16[256,1024]{1,0:T(8,128)(2,1)S(1)} %collective-permute-done.57.refs_13_), channel_id=1, source_target_pairs={{1,0},{5,4},{9,8},{13,12},{17,16},{21,20},{25,24},{29,28}} | collective-permute-start | bytes 1572872 | tf_op jit(solution)/shard_map/ppermute | solution.py:75
  258.1 57.2 %collective-permute-start.49 = (bf16[4,32,7168]{2,1,0:T(8,128)(2,1)S(1)}, bf16[4,32,7168]{2,1,0:T(8,128)(2,1)S(1)}, u32[]{:S(2)}, u32[]{:S(2)}) collective-permute-start(bf16[4,32,7168]{2,1,0:T(8,128)(2,1)S(1)} %fusion.refs_1_), channel_id=1, source_target_pairs={{0,8},{4,12},{8,0},{12,4},{16,24},{20,28},{24,16},{28,20},{1,9},{5... | collective-permute-start | bytes 5505032 | tf_op jit(solution)/shard_map/ppermute | solution.py:63
  258.1 75.4 %collective-permute-start.51 = (bf16[4,32,7168]{2,1,0:T(8,128)(2,1)S(1)}, bf16[4,32,7168]{2,1,0:T(8,128)(2,1)S(1)}, u32[]{:S(2)}, u32[]{:S(2)}) collective-permute-start(bf16[4,32,7168]{2,1,0:T(8,128)(2,1)S(1)} %fusion.refs_1_), channel_id=1, source_target_pairs={{0,16},{4,20},{8,24},{12,28},{16,0},{20,4},{24,8},{28,12},{1,17},{... | collective-permute-start | bytes 5505032 | tf_op jit(solution)/shard_map/ppermute | solution.py:63
  289.2 45.9 %collective-permute-start.53 = (bf16[4,32,7168]{2,1,0:T(8,128)(2,1)S(1)}, bf16[4,32,7168]{2,1,0:T(8,128)(2,1)S(1)}, u32[]{:S(2)}, u32[]{:S(2)}) collective-permute-start(bf16[4,32,7168]{2,1,0:T(8,128)(2,1)S(1)} %fusion.refs_1_), channel_id=1, source_target_pairs={{0,24},{4,28},{8,16},{12,20},{16,8},{20,12},{24,0},{28,4},{1,25},{... | collective-permute-start | bytes 5505032 | tf_op jit(solution)/shard_map/ppermute | solution.py:63
  290.7 24.0 %collective-permute-start.44 = (bf16[256,2048]{1,0:T(8,128)(2,1)S(1)}, bf16[256,2048]{1,0:T(8,128)(2,1)}, u32[]{:S(2)}, u32[]{:S(2)}) collective-permute-start(bf16[256,2048]{1,0:T(8,128)(2,1)S(1)} %collective-permute-done.43.refs_15_), channel_id=1, source_target_pairs={{1,0},{2,1},{5,4},{6,5},{9,8},{10,9},{13,12},{14,13},{17,16},{18,1... | collective-permute-start | bytes 3145736 | tf_op jit(solution)/shard_map/ppermute | solution.py:75
  292.1 22.7 %collective-permute-start.46 = (bf16[256,2048]{1,0:T(8,128)(2,1)S(1)}, bf16[256,2048]{1,0:T(8,128)(2,1)}, u32[]{:S(2)}, u32[]{:S(2)}) collective-permute-start(bf16[256,2048]{1,0:T(8,128)(2,1)S(1)} %collective-permute-done.42.refs_10_), channel_id=1, source_target_pairs={{1,2},{2,3},{5,6},{6,7},{9,10},{10,11},{13,14},{14,15},{17,18},{18... | collective-permute-start | bytes 3145736 | tf_op jit(solution)/shard_map/ppermute | solution.py:74
  314.8 24.9 %collective-permute-start.5 = (bf16[4,32,4096]{2,1,0:T(8,128)(2,1)S(1)}, bf16[4,32,4096]{2,1,0:T(8,128)(2,1)S(1)}, u32[]{:S(2)}, u32[]{:S(2)}) collective-permute-start(bf16[4,32,4096]{2,1,0:T(8,128)(2,1)S(1)} %collective-permute-done.4.refs_3_), channel_id=1, source_target_pairs={{0,4},{4,0},{8,12},{12,8},{16,20},{20,16},{24,28},{28,24},{1,5},{5... | collective-permute-start | bytes 3145736 | tf_op jit(solution)/shard_map/ppermute | solution.py:65
  314.8 26.1 %collective-permute-start.7 = (bf16[4,32,4096]{2,1,0:T(8,128)(2,1)S(1)}, bf16[4,32,4096]{2,1,0:T(8,128)(2,1)S(1)}, u32[]{:S(2)}, u32[]{:S(2)}) collective-permute-start(bf16[4,32,4096]{2,1,0:T(8,128)(2,1)S(1)} %collective-permute-done.6.refs_5_), channel_id=1, source_target_pairs={{0,4},{4,0},{8,12},{12,8},{16,20},{20,16},{24,28},{28,24},{1,5},{5... | collective-permute-start | bytes 3145736 | tf_op jit(solution)/shard_map/ppermute | solution.py:65
  315.3 21.4 %collective-permute-start.26 = (bf16[256,1536]{1,0:T(8,128)(2,1)S(1)}, bf16[256,1536]{1,0:T(8,128)(2,1)S(1)}, u32[]{:S(2)}, u32[]{:S(2)}) collective-permute-start(bf16[256,1536]{1,0:T(8,128)(2,1)S(1)} %collective-permute-done.25.refs_13_), channel_id=1, source_target_pairs={{1,0},{5,4},{9,8},{13,12},{17,16},{21,20},{25,24},{29,28}} | collective-permute-start | bytes 2359304 | tf_op jit(solution)/shard_map/ppermute | solution.py:75
  336.7 74.7 %collective-permute-start.20 = (bf16[256,2048]{1,0:T(8,128)(2,1)}, bf16[256,2048]{1,0:T(8,128)(2,1)}, u32[]{:S(2)}, u32[]{:S(2)}) collective-permute-start(bf16[256,2048]{1,0:T(8,128)(2,1)} %collective-permute-done.19.refs_13_), channel_id=1, source_target_pairs={{1,0},{5,4},{9,8},{13,12},{17,16},{21,20},{25,24},{29,28}} | collective-permute-start | bytes 3145736 | tf_op jit(solution)/shard_map/ppermute | solution.py:75
  338.0 73.9 %collective-permute-start.22 = (bf16[256,2048]{1,0:T(8,128)(2,1)}, bf16[256,2048]{1,0:T(8,128)(2,1)}, u32[]{:S(2)}, u32[]{:S(2)}) collective-permute-start(bf16[256,2048]{1,0:T(8,128)(2,1)} %collective-permute-done.21.refs_12_), channel_id=1, source_target_pairs={{2,3},{6,7},{10,11},{14,15},{18,19},{22,23},{26,27},{30,31}} | collective-permute-start | bytes 3145736 | tf_op jit(solution)/shard_map/ppermute | solution.py:74
  339.7 72.3 %collective-permute-start.45 = (bf16[256,2048]{1,0:T(8,128)(2,1)}, bf16[256,2048]{1,0:T(8,128)(2,1)}, u32[]{:S(2)}, u32[]{:S(2)}) collective-permute-start(bf16[256,2048]{1,0:T(8,128)(2,1)} %collective-permute-done.44.refs_13_), channel_id=1, source_target_pairs={{1,0},{5,4},{9,8},{13,12},{17,16},{21,20},{25,24},{29,28}} | collective-permute-start | bytes 3145736 | tf_op jit(solution)/shard_map/ppermute | solution.py:75
  341.0 70.4 %collective-permute-start.39 = (bf16[256,1536]{1,0:T(8,128)(2,1)}, bf16[256,1536]{1,0:T(8,128)(2,1)}, u32[]{:S(2)}, u32[]{:S(2)}) collective-permute-start(bf16[256,1536]{1,0:T(8,128)(2,1)} %collective-permute-done.38.refs_13_), channel_id=1, source_target_pairs={{1,0},{5,4},{9,8},{13,12},{17,16},{21,20},{25,24},{29,28}} | collective-permute-start | bytes 2359304 | tf_op jit(solution)/shard_map/ppermute | solution.py:75
  343.3 85.1 %collective-permute-start.47 = (bf16[256,2048]{1,0:T(8,128)(2,1)}, bf16[256,2048]{1,0:T(8,128)(2,1)}, u32[]{:S(2)}, u32[]{:S(2)}) collective-permute-start(bf16[256,2048]{1,0:T(8,128)(2,1)} %collective-permute-done.46.refs_12_), channel_id=1, source_target_pairs={{2,3},{6,7},{10,11},{14,15},{18,19},{22,23},{26,27},{30,31}} | collective-permute-start | bytes 3145736 | tf_op jit(solution)/shard_map/ppermute | solution.py:74
  411.4 47.9 %collective-permute-start.48 = (bf16[4,32,7168]{2,1,0:T(8,128)(2,1)S(1)}, bf16[4,32,7168]{2,1,0:T(8,128)(2,1)}, u32[]{:S(2)}, u32[]{:S(2)}) collective-permute-start(bf16[4,32,7168]{2,1,0:T(8,128)(2,1)S(1)} %fusion.refs_1_), channel_id=1, source_target_pairs={{0,4},{4,0},{8,12},{12,8},{16,20},{20,16},{24,28},{28,24},{1,5},{5... | collective-permute-start | bytes 5505032 | tf_op jit(solution)/shard_map/ppermute | solution.py:65
  411.4 47.9 %collective-permute-start.50 = (bf16[4,32,7168]{2,1,0:T(8,128)(2,1)}, bf16[4,32,7168]{2,1,0:T(8,128)(2,1)}, u32[]{:S(2)}, u32[]{:S(2)}) collective-permute-start(bf16[4,32,7168]{2,1,0:T(8,128)(2,1)} %copy-done.36), channel_id=1, source_target_pairs={{0,4},{4,0},{8,12},{12,8},{16,20},{20,16},{24,28},{28,24},{1,5},{5... | collective-permute-start | bytes 5505032 | tf_op jit(solution)/shard_map/ppermute | solution.py:65
  411.9 47.4 %collective-permute-start.52 = (bf16[4,32,7168]{2,1,0:T(8,128)(2,1)}, bf16[4,32,7168]{2,1,0:T(8,128)(2,1)}, u32[]{:S(2)}, u32[]{:S(2)}) collective-permute-start(bf16[4,32,7168]{2,1,0:T(8,128)(2,1)} %copy-done.37), channel_id=1, source_target_pairs={{0,4},{4,0},{8,12},{12,8},{16,20},{20,16},{24,28},{28,24},{1,5},{5... | collective-permute-start | bytes 5505032 | tf_op jit(solution)/shard_map/ppermute | solution.py:65
  412.0 47.3 %collective-permute-start.54 = (bf16[4,32,7168]{2,1,0:T(8,128)(2,1)}, bf16[4,32,7168]{2,1,0:T(8,128)(2,1)}, u32[]{:S(2)}, u32[]{:S(2)}) collective-permute-start(bf16[4,32,7168]{2,1,0:T(8,128)(2,1)} %copy-done.38), channel_id=1, source_target_pairs={{0,4},{4,0},{8,12},{12,8},{16,20},{20,16},{24,28},{28,24},{1,5},{5... | collective-permute-start | bytes 5505032 | tf_op jit(solution)/shard_map/ppermute | solution.py:65
  428.4 17.0 %collective-permute-start.41 = (bf16[256,1536]{1,0:T(8,128)(2,1)S(1)}, bf16[256,1536]{1,0:T(8,128)(2,1)S(1)}, u32[]{:S(2)}, u32[]{:S(2)}) collective-permute-start(bf16[256,1536]{1,0:T(8,128)(2,1)S(1)} %copy-done.21), channel_id=1, source_target_pairs={{2,3},{6,7},{10,11},{14,15},{18,19},{22,23},{26,27},{30,31}} | collective-permute-start | bytes 2359304 | tf_op jit(solution)/shard_map/ppermute | solution.py:74
  445.5 13.8 %collective-permute-start.60 = (bf16[256,1024]{1,0:T(8,128)(2,1)S(1)}, bf16[256,1024]{1,0:T(8,128)(2,1)S(1)}, u32[]{:S(2)}, u32[]{:S(2)}) collective-permute-start(bf16[256,1024]{1,0:T(8,128)(2,1)S(1)} %copy-done.41), channel_id=1, source_target_pairs={{2,3},{6,7},{10,11},{14,15},{18,19},{22,23},{26,27},{30,31}} | collective-permute-start | bytes 1572872 | tf_op jit(solution)/shard_map/ppermute | solution.py:74
  (59 other events, 1996.1 us)

commit v2 on v1

--- a/solution.py
+++ b/solution.py
@@ -45,13 +45,12 @@
 def spread_cols(factors):
     n_col = lax.axis_size("col")
     mine = lax.axis_index("col")
-    pieces = []
-    for s in range(n_col):
-        at = (mine + s) % n_col
-        piece = jnp.concatenate([columns_of(f, at, n_col) for f in factors], axis=1)
+    pieces = [None] * n_col
+    for s in reversed(range(n_col)):
+        piece = jnp.concatenate([columns_of(f, mine ^ s, n_col) for f in factors], axis=1)
         if s:
-            piece = lax.ppermute(piece, "col", [(j, (j + s) % n_col) for j in range(n_col)])
-        pieces.append(piece)
+            piece = lax.ppermute(piece, "col", [(j, j ^ s) for j in range(n_col)])
+        pieces[s] = piece
     return pieces
 
 
@@ -78,11 +77,12 @@
     return [(block,)] + [(ups[s], downs[n_col - s]) for s in range(1, n_col)]
 
 
-def merge_kernel(n_row, n_col, block, tile, a_column, b_column, *refs):
+def merge_kernel(n_row, n_col, block, tile, a_column, b_column, have, *refs):
     weight_ref = refs[0]
     a_refs = refs[1 : 1 + n_row]
     own_ref = refs[1 + n_row]
-    pairs = refs[2 + n_row : 2 * n_col + n_row]
+    came = iter(refs[2 + n_row :])
+    came = [next(came) if there else None for there in have]
     out_ref, a_two, b_all, a_sems, b_sems = refs[-5:]
     depth = a_refs[0].shape[1]
     group = n_row * depth
@@ -100,33 +100,48 @@
             for i in range(n_row)
         ]
 
+    def place(s):
+        mine = lax.axis_index("col")
+        slab = mine ^ lax.rem(mine + (n_col - s), n_col)
+        return pl.ds(pl.multiple_of(slab * group, group), group)
+
     def b_copy(ref, s, part):
         return pltpu.make_async_copy(
             ref.at[:, pl.ds(b_column + part * block, block)],
-            b_all.at[part, pl.ds(s * group, group)],
+            b_all.at[part, place(s)],
             b_sems.at[part, s],
         )
 
-    def b_start(part):
+    def b_each(part, act):
         mine = lax.axis_index("col")
-        b_copy(own_ref, 0, part).start()
+        act(own_ref, 0, part)
         for s in range(1, n_col):
-            up_ref, down_ref = pairs[2 * (s - 1) : 2 * s]
+            up_ref, down_ref = came[2 * (s - 1) : 2 * s]
 
             @pl.when(mine >= s)
             def _():
-                b_copy(up_ref, s, part).start()
+                act(up_ref, s, part)
 
             @pl.when(mine < s)
             def _():
-                b_copy(down_ref, s, part).start()
+                act(down_ref, s, part)
+
+    def b_start(ref, s, part):
+        if ref is None:
+            b_all[part, place(s)] = jnp.zeros((group, block), b_all.dtype)
+        else:
+            b_copy(ref, s, part).start()
+
+    def b_wait(ref, s, part):
+        if ref is not None:
+            b_copy(ref, s, part).wait()
 
     @pl.when((t == 0) & (g == 0))
     def _():
         for copy in a_copies(0, 0):
             copy.start()
         for part in range(parts):
-            b_start(part)
+            b_each(part, b_start)
 
     @pl.when((g == 0) & (t + 1 < tiles))
     def _():
@@ -139,8 +154,7 @@
 
             @pl.when(g == part)
             def _():
-                for s in range(n_col):
-                    b_copy(own_ref, s, part).wait()
+                b_each(part, b_wait)
 
     slot = lax.rem(t, 2)
 
@@ -156,6 +170,107 @@
         preferred_element_type=jnp.float32,
     )
     out_ref[...] = (weight_ref[...].astype(jnp.float32) + update).astype(out_ref.dtype)
+
+
+def finish_kernel(n_row, n_col, block, tile, a_column, *refs):
+    part_ref = refs[0]
+    a_refs = refs[1 : 1 + n_row]
+    up_ref, down_ref = refs[1 + n_row : 3 + n_row]
+    out_ref, a_two, b_all, a_sems, b_sems = refs[-5:]
+    depth = a_refs[0].shape[1]
+    t, g = pl.program_id(0), pl.program_id(1)
+    tiles, parts = pl.num_programs(0), b_sems.shape[0]
+    mine = lax.axis_index("col")
+
+    def a_copies(t, slot):
+        columns = pl.ds(pl.multiple_of(a_column + t * tile, 128), tile)
+        return [
+            pltpu.make_async_copy(
+                a_refs[i].at[n_col - 1, :, columns],
+                a_two.at[slot, pl.ds(i * depth, depth)],
+                a_sems.at[slot, i],
+            )
+            for i in range(n_row)
+        ]
+
+    def b_copy(ref, part):
+        return pltpu.make_async_copy(
+            ref.at[:, pl.ds(part * block, block)], b_all.at[part], b_sems.at[part]
+        )
+
+    @pl.when((t == 0) & (g == 0))
+    def _():
+        for copy in a_copies(0, 0):
+            copy.start()
+
+        @pl.when(mine == n_col - 1)
+        def _():
+            for part in range(parts):
+                b_copy(up_ref, part).start()
+
+        @pl.when(mine != n_col - 1)
+        def _():
+            for part in range(parts):
+                b_copy(down_ref, part).start()
+
+    @pl.when((g == 0) & (t + 1 < tiles))
+    def _():
+        for copy in a_copies(t + 1, lax.rem(t + 1, 2)):
+            copy.start()
+
+    @pl.when(t == 0)
+    def _():
+        for part in range(parts):
+
+            @pl.when(g == part)
+            def _():
+                b_copy(up_ref, part).wait()
+
+    slot = lax.rem(t, 2)
+
+    @pl.when(g == 0)
+    def _():
+        for copy in a_copies(t, slot):
+            copy.wait()
+
+    update = lax.dot_general(
+        b_all[g], a_two[slot], (((0,), (0,)), ((), ())), preferred_element_type=jnp.float32
+    )
+    out_ref[...] = (part_ref[...].astype(jnp.float32) + update).astype(out_ref.dtype)
+
+
+def finish_rows(done, a_pieces, a_column, arrival, first, rows):
+    n_row = lax.axis_size("row")
+    n_col = lax.axis_size("col")
+    depth = a_pieces[0].shape[1]
+    width = done.shape[1]
+    block = next(b for b in range(896, 0, -128) if rows % b == 0 and first % b == 0)
+    tile = next(size for size in (1024, 512, 256, 128) if width % size == 0)
+    skip = first // block
+    anywhere = pl.BlockSpec(memory_space=pl.ANY)
+    spec = pl.BlockSpec((block, tile), lambda t, g: (g + skip, t))
+    return pl.pallas_call(
+        functools.partial(finish_kernel, n_row, n_col, block, tile, a_column),
+        grid=(width // tile, rows // block),
+        in_specs=[spec] + [anywhere] * (n_row + 2),
+        out_specs=spec,
+        out_shape=jax.ShapeDtypeStruct(done.shape, done.dtype),
+        scratch_shapes=[
+            pltpu.VMEM((2, n_row * depth, tile), jnp.bfloat16),
+            pltpu.VMEM((rows // block, n_row * depth, block), jnp.bfloat16),
+            pltpu.SemaphoreType.DMA((2, n_row)),
+            pltpu.SemaphoreType.DMA((rows // block,)),
+        ],
+        input_output_aliases={0: 0},
+        compiler_params=pltpu.CompilerParams(
+            dimension_semantics=("arbitrary", "arbitrary"), vmem_limit_bytes=60 * 1024 * 1024
+        ),
+        cost_estimate=pl.CostEstimate(
+            flops=2 * n_row * depth * rows * width,
+            bytes_accessed=4 * rows * width,
+            transcendentals=0,
+        ),
+    )(done, *a_pieces, *arrival)
 
 
 def merge_rows(weight, a_pieces, a_column, arrivals, b_column, first, rows, done=None):
@@ -168,9 +283,10 @@
     sizes = (512, 256, 128) if rows == block else (1024, 512, 256, 128)
     tile = next(size for size in sizes if width % size == 0)
     skip = first // block
-    operands = [weight, *a_pieces]
-    for arrival in arrivals:
-        operands.extend(arrival)
+    operands = [weight, *a_pieces, arrivals[0][0]]
+    came = [array for arrival in arrivals[1:] for array in arrival]
+    have = tuple(array is not None for array in came)
+    operands.extend(array for array in came if array is not None)
     anywhere = pl.BlockSpec(memory_space=pl.ANY)
     spec = pl.BlockSpec((block, tile), lambda t, g: (g + skip, t))
     aliases = {}
@@ -178,7 +294,7 @@
         aliases = {len(operands): 0}
         operands.append(done)
     return pl.pallas_call(
-        functools.partial(merge_kernel, n_row, n_col, block, tile, a_column, b_column),
+        functools.partial(merge_kernel, n_row, n_col, block, tile, a_column, b_column, have),
         grid=(width // tile, rows // block),
         in_specs=[spec] + [anywhere] * (len(operands) - 1),
         out_specs=spec,
@@ -237,7 +353,7 @@
     rest_mine = jnp.concatenate(spread_rows((down_b, up_b)))
 
     mine = lax.axis_index("col")
-    owners = (mine + n_col - jnp.arange(n_col, dtype=jnp.int32)) % n_col
+    owners = mine ^ jnp.arange(n_col, dtype=jnp.int32)
     shards = lax.axis_index("row") * n_col + owners
     row_ids = (shards[:, None] * depth + jnp.arange(depth, dtype=jnp.int32)[None, :]).reshape(-1)
     scale = rows_scale(sample_counts, slot_silo, row_ids)
@@ -255,17 +371,24 @@
 
     down_rows = down_weight.shape[0]
 
-    def merged(weight, a_pieces, a_column, source, start, weights):
+    def merged(weight, a_pieces, a_column, source, start, weights, split=False):
         done, first = None, 0
         for rows in shares_of(weight.shape[0], weights):
             at = start + first
             arrivals = line_gather(source[:, at : at + rows])
+            late = None
+            if split and first + rows == weight.shape[0] and n_col > 2:
+                late = arrivals[-1][0], arrivals[1][1]
+                arrivals[-1] = None, arrivals[-1][1]
+                arrivals[1] = arrivals[1][0], None
             done = merge_rows(weight, a_pieces, a_column, arrivals, 0, first, rows, done)
+            if late:
+                done = finish_rows(done, a_pieces, a_column, late, first, rows)
             first += rows
         return done
 
     merged_gate = merged(gate_weight, mlp_pieces, 0, gate_mine, 0, (1, 1))
-    merged_up = merged(up_weight, mlp_pieces, gate_cols, rest_mine, down_rows, (4, 3))
+    merged_up = merged(up_weight, mlp_pieces, gate_cols, rest_mine, down_rows, (4, 3), True)
 
     arrivals = line_gather(rest_mine[:, :down_rows])
     merged_down = merge_rows(down_weight, down_pieces, 0, arrivals, 0, 0, down_rows)

time: 488 us -> 488 us (level); the launches traced: 485 us -> 480 us
  waiting for transfers between devices: 286 us -> 269 us
  Pallas kernels: 82.5 us -> 92.4 us
    ppermute x15, waiting for transfers between devices: 172 us -> 159 us  [line_gather(): lax.ppermute(down, 'col', [(j, j - 1) for j in range(1, n_col + 1 - s)])]
    pallas_call x0 -> x1, Pallas kernels: none -> 9.61 us  [finish_rows(): pl.pallas_call(functools.partial(finish_kernel, n_row, n_col, block, tile...]
  transfers between devices with their start and end apart: 61 -> 61, of which waited for: 20 -> 21; matrix products, arithmetic and copies ran while one was open for 5% -> 5% of each run, Pallas kernels for 12% -> 14%
where the time goes in v2:
time: 488 us; the launch traced here: 480 us
  waiting for transfers between devices  269 us (55%)
  Pallas kernels  92.4 us (19%)
  starting transfers between devices  87.1 us (18%)
  local copies, waits for them, and re-layouts  23.2 us (5%)
  other arithmetic  6.19 us (1%)
    ppermute x15, waiting for transfers between devices, line_gather(): lax.ppermute(down, 'col', [(j, j - 1) for j in range(1, n_col + 1 - s)])  159 us
    pallas_call x5, Pallas kernels, merge_rows(): pl.pallas_call(functools.partial(merge_kernel, n_row, n_col, block, tile,...  82.7 us
    ppermute x14, waiting for transfers between devices, spread_rows(): piece = lax.ppermute(piece, 'row', [(k, k ^ i) for k in range(n_row)])  44.4 us
    ppermute x6, waiting for transfers between devices, gather_rows(): pieces[i] = lax.ppermute(block, 'row', [(k, k ^ i) for k in range(n_row)])  43.8 us
    ppermute x15, starting transfers between devices, line_gather(): up = lax.ppermute(up, 'col', [(j, j + 1) for j in range(s - 1, n_col - 1)])  36.4 us
    ppermute x15, waiting for transfers between devices, line_gather(): up = lax.ppermute(up, 'col', [(j, j + 1) for j in range(s - 1, n_col - 1)])  22 us
    ppermute x15, starting transfers between devices, line_gather(): lax.ppermute(down, 'col', [(j, j - 1) for j in range(1, n_col + 1 - s)])  19.4 us
    ppermute x14, starting transfers between devices, spread_rows(): piece = lax.ppermute(piece, 'row', [(k, k ^ i) for k in range(n_row)])  18 us
  transfers between devices with their start and end apart: 61, of which 21 were waited for; matrix products, arithmetic and copies ran while one was open for 5% of the time, Pallas kernels for 14%

profile of v2, /device:TPU:0, one launch (start us, length us, event | category | flops | bytes accessed | tf_op | source)
XLA Modules:
  0.0 480.0 jit_solution(10310443131639489506)
XLA Ops:
  0.7 2.4 constant_dynamic-slice_fusion.34
  4.9 5.1 %collective-permute-start.2 = (bf16[32,11264]{1,0:T(8,128)(2,1)}, bf16[32,11264]{1,0:T(8,128)(2,1)}, u32[]{:S(2)}, u32[]{:S(2)}) collective-permute-start(bf16[32,11264]{1,0:T(8,128)(2,1)} %pad_maximum_fusion.4), channel_id=1, source_target_pairs={{0,3},{1,2},{2,1},{3,0},{4,7},{5,6},{6,5},{7,4},{8,11},{9,10},{10,... | collective-permute-start | bytes 2162696 | tf_op jit(solution)/shard_map/ppermute | solution.py:52
  12.3 2.7 constant_dynamic-slice_fusion.16
  15.0 1.7 collective-permute-start.11
  16.9 2.4 constant_dynamic-slice_fusion
  24.0 1.8 collective-permute-start.13
  26.8 3.7 collective-permute-done.12
  30.4 1.7 collective-permute-start.14
  32.2 2.4 collective-permute-start.15
  34.6 7.9 %collective-permute-done.14 = bf16[32,3584]{1,0:T(8,128)(2,1)S(1)} collective-permute-done((bf16[32,3584]{1,0:T(8,128)(2,1)S(1)}, bf16[32,3584]{1,0:T(8,128)(2,1)S(1)}, u32[]{:S(2)}, u32[]{:S(2)}) %collective-permute-start.14) | collective-permute-done | bytes 229408 | tf_op jit(solution)/shard_map/ppermute | solution.py:40
  42.5 1.7 collective-permute-start.16
  44.3 6.2 %collective-permute-done.16 = bf16[32,3584]{1,0:T(8,128)(2,1)S(1)} collective-permute-done((bf16[32,3584]{1,0:T(8,128)(2,1)S(1)}, bf16[32,3584]{1,0:T(8,128)(2,1)S(1)}, u32[]{:S(2)}, u32[]{:S(2)}) %collective-permute-start.16) | collective-permute-done | bytes 229408 | tf_op jit(solution)/shard_map/ppermute | solution.py:40
  52.7 7.7 %collective-permute-done.30 = bf16[32,4608]{1,0:T(8,128)(2,1)S(1)} collective-permute-done((bf16[32,4608]{1,0:T(8,128)(2,1)S(1)}, bf16[32,4608]{1,0:T(8,128)(2,1)S(1)}, u32[]{:S(2)}, u32[]{:S(2)}) %collective-permute-start.30) | collective-permute-done | bytes 294944 | tf_op jit(solution)/shard_map/ppermute | solution.py:40
  61.9 4.0 collective-permute-done.31
  66.0 1.7 collective-permute-start.33
  70.3 10.5 %collective-permute-done.33 = bf16[32,4608]{1,0:T(8,128)(2,1)S(1)} collective-permute-done((bf16[32,4608]{1,0:T(8,128)(2,1)S(1)}, bf16[32,4608]{1,0:T(8,128)(2,1)S(1)}, u32[]{:S(2)}, u32[]{:S(2)}) %collective-permute-start.33) | collective-permute-done | bytes 294944 | tf_op jit(solution)/shard_map/ppermute | solution.py:40
  80.8 1.7 collective-permute-start.35
  82.6 4.4 collective-permute-start.23
  87.0 3.3 collective-permute-done.35
  91.7 6.0 %collective-permute-start.36 = (bf16[256,1536]{1,0:T(8,128)(2,1)S(1)}, bf16[256,1536]{1,0:T(8,128)(2,1)}, u32[]{:S(2)}, u32[]{:S(2)}) collective-permute-start(bf16[256,1536]{1,0:T(8,128)(2,1)S(1)} %slice.49.refs_9_), channel_id=1, source_target_pairs={{0,1},{1,2},{2,3},{4,5},{5,6},{6,7},{8,9},{9,10},{10,11},{12,13},{... | collective-permute-start | bytes 2359304 | tf_op jit(solution)/shard_map/ppermute | solution.py:73
  99.2 3.8 collective-permute-start.55
  104.7 1.7 slice.50.refs_9_
  109.6 22.0 %collective-permute-done.55.refs_10_ = bf16[256,1024]{1,0:T(8,128)(2,1)} collective-permute-done((bf16[256,1024]{1,0:T(8,128)(2,1)}, bf16[256,1024]{1,0:T(8,128)(2,1)}, u32[]{:S(2)}, u32[]{:S(2)}) %collective-permute-start.55) | collective-permute-done | bytes 524320 | tf_op jit(solution)/shard_map/ppermute | solution.py:73
  131.6 4.4 collective-permute-start.17
  138.7 5.2 %collective-permute-start.40 = (bf16[256,2048]{1,0:T(8,128)(2,1)S(1)}, bf16[256,2048]{1,0:T(8,128)(2,1)S(1)}, u32[]{:S(2)}, u32[]{:S(2)}) collective-permute-start(bf16[256,2048]{1,0:T(8,128)(2,1)S(1)} %slice.50.refs_9_), channel_id=1, source_target_pairs={{0,1},{1,2},{2,3},{4,5},{5,6},{6,7},{8,9},{9,10},{10,11},{12,13},{... | collective-permute-start | bytes 3145736 | tf_op jit(solution)/shard_map/ppermute | solution.py:73
  145.6 35.3 %collective-permute-done.38.refs_13_ = bf16[256,1536]{1,0:T(8,128)(2,1)S(1)} collective-permute-done((bf16[256,1536]{1,0:T(8,128)(2,1)S(1)}, bf16[256,1536]{1,0:T(8,128)(2,1)S(1)}, u32[]{:S(2)}, u32[]{:S(2)}) %collective-permute-start.38) | collective-permute-done | bytes 786464 | tf_op jit(solution)/shard_map/ppermute | solution.py:74
  184.5 18.8 %collective-permute-done.41.refs_15_ = bf16[256,2048]{1,0:T(8,128)(2,1)S(1)} collective-permute-done((bf16[256,2048]{1,0:T(8,128)(2,1)S(1)}, bf16[256,2048]{1,0:T(8,128)(2,1)S(1)}, u32[]{:S(2)}, u32[]{:S(2)}) %collective-permute-start.41) | collective-permute-done | bytes 1048608 | tf_op jit(solution)/shard_map/ppermute | solution.py:74
  203.5 9.4 %collective-permute-done.57.refs_13_ = bf16[256,1024]{1,0:T(8,128)(2,1)S(1)} collective-permute-done((bf16[256,1024]{1,0:T(8,128)(2,1)}, bf16[256,1024]{1,0:T(8,128)(2,1)S(1)}, u32[]{:S(2)}, u32[]{:S(2)}) %collective-permute-start.57) | collective-permute-done | bytes 524320 | tf_op jit(solution)/shard_map/ppermute | solution.py:74
  221.3 26.2 %collective-permute-done.6.refs_5_ = bf16[4,32,4096]{2,1,0:T(8,128)(2,1)S(1)} collective-permute-done((bf16[4,32,4096]{2,1,0:T(8,128)(2,1)S(1)}, bf16[4,32,4096]{2,1,0:T(8,128)(2,1)S(1)}, u32[]{:S(2)}, u32[]{:S(2)}) %collective-permute-start.6) | collective-permute-done | bytes 1048608 | tf_op jit(solution)/shard_map/ppermute | solution.py:62
  250.2 1.6 collective-permute-start.21
  255.1 14.7 %collective-permute-done.39.refs_12_ = bf16[256,1536]{1,0:T(8,128)(2,1)S(1)} collective-permute-done((bf16[256,1536]{1,0:T(8,128)(2,1)S(1)}, bf16[256,1536]{1,0:T(8,128)(2,1)S(1)}, u32[]{:S(2)}, u32[]{:S(2)}) %collective-permute-start.39) | collective-permute-done | bytes 786464 | tf_op jit(solution)/shard_map/ppermute | solution.py:74
  270.2 28.3 %collective-permute-done.58.refs_11_ = bf16[256,1024]{1,0:T(8,128)(2,1)S(1)} collective-permute-done((bf16[256,1024]{1,0:T(8,128)(2,1)S(1)}, bf16[256,1024]{1,0:T(8,128)(2,1)S(1)}, u32[]{:S(2)}, u32[]{:S(2)}) %collective-permute-start.58) | collective-permute-done | bytes 524320 | tf_op jit(solution)/shard_map/ppermute | solution.py:74
  301.2 1.7 collective-permute-start.44
  302.9 18.8 %collective-permute-done.42.refs_13_ = bf16[256,2048]{1,0:T(8,128)(2,1)} collective-permute-done((bf16[256,2048]{1,0:T(8,128)(2,1)S(1)}, bf16[256,2048]{1,0:T(8,128)(2,1)}, u32[]{:S(2)}, u32[]{:S(2)}) %collective-permute-start.42) | collective-permute-done | bytes 1048608 | tf_op jit(solution)/shard_map/ppermute | solution.py:74
  323.5 17.5 %collective-permute-done.51.refs_5_ = bf16[4,32,7168]{2,1,0:T(8,128)(2,1)S(1)} collective-permute-done((bf16[4,32,7168]{2,1,0:T(8,128)(2,1)S(1)}, bf16[4,32,7168]{2,1,0:T(8,128)(2,1)S(1)}, u32[]{:S(2)}, u32[]{:S(2)}) %collective-permute-start.51) | collective-permute-done | bytes 1835040 | tf_op jit(solution)/shard_map/ppermute | solution.py:62
  341.8 1.8 collective-permute-done.26.refs_11_
  344.9 1.6 collective-permute-start.22
  347.8 1.6 collective-permute-start.46
  350.5 1.6 collective-permute-start.45
  352.1 12.6 %shard_map.130.refs_16_ = bf16[3584,2048]{1,0:T(8,128)(2,1)} custom-call(bf16[3584,2048]{1,0:T(8,128)(2,1)} %refs_0_.6, bf16[4,32,4096]{2,1,0:T(8,128)(2,1)} %copy-done, bf16[4,32,4096]{2,1,0:T(8,128)(2,1)} %copy-done.1, bf16[4,32,4096]{2,1,0:T(8,128)(2,1)} %copy-done.2, bf16[4,32,4096]{2,1,0:T(8,128)(2,1)} %copy-done.5, bf16[4,32,4096]{2,1,0:T(8,128)(2,1)} %copy-done.3, ...), custom_call_target="tpu_custom_call" | custom-call | flops 6442450944 | bytes 19922944 | tf_op jit(solution)/shard_map/pallas_call | solution.py:296
  364.8 7.0 %collective-permute-done.20.refs_11_ = bf16[256,2048]{1,0:T(8,128)(2,1)} collective-permute-done((bf16[256,2048]{1,0:T(8,128)(2,1)}, bf16[256,2048]{1,0:T(8,128)(2,1)}, u32[]{:S(2)}, u32[]{:S(2)}) %collective-permute-start.20) | collective-permute-done | bytes 1048608 | tf_op jit(solution)/shard_map/ppermute | solution.py:74
  372.3 20.2 %collective-permute-done.43.refs_11_ = bf16[256,2048]{1,0:T(8,128)(2,1)} collective-permute-done((bf16[256,2048]{1,0:T(8,128)(2,1)}, bf16[256,2048]{1,0:T(8,128)(2,1)}, u32[]{:S(2)}, u32[]{:S(2)}) %collective-permute-start.43) | collective-permute-done | bytes 1048608 | tf_op jit(solution)/shard_map/ppermute | solution.py:74
  392.5 16.0 %shard_map.131 = bf16[3584,2048]{1,0:T(8,128)(2,1)} custom-call(bf16[3584,2048]{1,0:T(8,128)(2,1)} %refs_0_.6, bf16[4,32,4096]{2,1,0:T(8,128)(2,1)} %copy-done, bf16[4,32,4096]{2,1,0:T(8,128)(2,1)} %copy-done.1, bf16[4,32,4096]{2,1,0:T(8,128)(2,1)} %copy-done.2, bf16[4,32,4096]{2,1,0:T(8,128)(2,1)} %copy-done.5, ...), custom_call_target="tpu_custom_call", output_to_operand_aliasing={{}: (16, {})} | custom-call | flops 8589934592 | bytes 25165824 | tf_op jit(solution)/shard_map/pallas_call | solution.py:296
  410.0 16.0 %shard_map.132.refs_14_ = bf16[3584,2048]{1,0:T(8,128)(2,1)} custom-call(bf16[3584,2048]{1,0:T(8,128)(2,1)} %refs_0_.8, bf16[4,32,4096]{2,1,0:T(8,128)(2,1)} %copy-done, bf16[4,32,4096]{2,1,0:T(8,128)(2,1)} %copy-done.1, bf16[4,32,4096]{2,1,0:T(8,128)(2,1)} %copy-done.2, bf16[4,32,4096]{2,1,0:T(8,128)(2,1)} %copy-done.5, bf16[4,32,4096]{2,1,0:T(8,128)(2,1)} %copy-done.3, ...), custom_call_target="tpu_custom_call" | custom-call | flops 8589934592 | bytes 25165824 | tf_op jit(solution)/shard_map/pallas_call | solution.py:296
  426.0 4.5 collective-permute-done.47.refs_10_
  431.2 12.9 %shard_map.133.refs_0_ = bf16[3584,2048]{1,0:T(8,128)(2,1)} custom-call(bf16[3584,2048]{1,0:T(8,128)(2,1)} %refs_0_.8, bf16[4,32,4096]{2,1,0:T(8,128)(2,1)} %copy-done, bf16[4,32,4096]{2,1,0:T(8,128)(2,1)} %copy-done.1, bf16[4,32,4096]{2,1,0:T(8,128)(2,1)} %copy-done.2, bf16[4,32,4096]{2,1,0:T(8,128)(2,1)} %copy-done.5, ...), custom_call_target="tpu_custom_call", output_to_operand_aliasing={{}: (14, {})} | custom-call | flops 6442450944 | bytes 19922944 | tf_op jit(solution)/shard_map/pallas_call | solution.py:296
  444.2 9.6 %shard_map.134 = bf16[3584,2048]{1,0:T(8,128)(2,1)} custom-call(bf16[3584,2048]{1,0:T(8,128)(2,1)} %shard_map.133.refs_0_, bf16[4,32,4096]{2,1,0:T(8,128)(2,1)} %copy-done, bf16[4,32,4096]{2,1,0:T(8,128)(2,1)} %copy-done.1, bf16[4,32,4096]{2,1,0:T(8,128)(2,1)} %copy-done.2, bf16[4,32,4096]{2,1,0:T(8,128)(2,1)} %copy-done.5, ...), custom_call_target="tpu_custom_call", output_to_operand_aliasing={{}: (0, {})} | custom-call | flops 1610612736 | bytes 12582912 | tf_op jit(solution)/shard_map/pallas_call | solution.py:252
  454.6 25.3 %shard_map.135 = bf16[1024,7168]{1,0:T(8,128)(2,1)} custom-call(bf16[1024,7168]{1,0:T(8,128)(2,1)} %refs_0_.9, bf16[4,32,7168]{2,1,0:T(8,128)(2,1)} %copy-done.14, bf16[4,32,7168]{2,1,0:T(8,128)(2,1)} %collective-permute-done.48.refs_2_, bf16[4,32,7168]{2,1,0:T(8,128)(2,1)} %copy-done.36, bf16[4,32,7168]{2,1,0:T(8,128)(2,1)} %collective-permute-done.50.refs_4_, ...), custom_call_target="tpu_custom_call" | custom-call | flops 15032385536 | bytes 46137344 | tf_op jit(solution)/shard_map/pallas_call | solution.py:296
  (226 shorter events, 58.5 us)
Async XLA Ops:
  4.9 86.8 %collective-permute-start.2 = (bf16[32,11264]{1,0:T(8,128)(2,1)}, bf16[32,11264]{1,0:T(8,128)(2,1)}, u32[]{:S(2)}, u32[]{:S(2)}) collective-permute-start(bf16[32,11264]{1,0:T(8,128)(2,1)} %pad_maximum_fusion.4), channel_id=1, source_target_pairs={{0,3},{1,2},{2,1},{3,0},{4,7},{5,6},{6,5},{7,4},{8,11},{9,10},{10,... | collective-permute-start | bytes 2162696 | tf_op jit(solution)/shard_map/ppermute | solution.py:52
  10.8 88.4 %collective-permute-start.1 = (bf16[32,11264]{1,0:T(8,128)(2,1)}, bf16[32,11264]{1,0:T(8,128)(2,1)}, u32[]{:S(2)}, u32[]{:S(2)}) collective-permute-start(bf16[32,11264]{1,0:T(8,128)(2,1)} %pad_maximum_fusion.3), channel_id=1, source_target_pairs={{0,2},{1,3},{2,0},{3,1},{4,6},{5,7},{6,4},{7,5},{8,10},{9,11},{10,... | collective-permute-start | bytes 2162696 | tf_op jit(solution)/shard_map/ppermute | solution.py:52
  11.7 91.3 %collective-permute-start = (bf16[32,11264]{1,0:T(8,128)(2,1)}, bf16[32,11264]{1,0:T(8,128)(2,1)}, u32[]{:S(2)}, u32[]{:S(2)}) collective-permute-start(bf16[32,11264]{1,0:T(8,128)(2,1)} %pad_maximum_fusion.2), channel_id=1, source_target_pairs={{0,1},{1,0},{2,3},{3,2},{4,5},{5,4},{6,7},{7,6},{8,9},{9,8},{10,11... | collective-permute-start | bytes 2162696 | tf_op jit(solution)/shard_map/ppermute | solution.py:52
  51.5 14.5 %collective-permute-start.31 = (bf16[32,4608]{1,0:T(8,128)(2,1)S(1)}, bf16[32,4608]{1,0:T(8,128)(2,1)S(1)}, u32[]{:S(2)}, u32[]{:S(2)}) collective-permute-start(bf16[32,4608]{1,0:T(8,128)(2,1)S(1)} %pad_maximum_fusion.7), channel_id=1, source_target_pairs={{0,12},{4,8},{8,4},{12,0},{16,28},{20,24},{24,20},{28,16},{1,13},{... | collective-permute-start | bytes 884744 | tf_op jit(solution)/shard_map/ppermute | solution.py:40
  66.0 14.8 %collective-permute-start.33 = (bf16[32,4608]{1,0:T(8,128)(2,1)S(1)}, bf16[32,4608]{1,0:T(8,128)(2,1)S(1)}, u32[]{:S(2)}, u32[]{:S(2)}) collective-permute-start(bf16[32,4608]{1,0:T(8,128)(2,1)S(1)} %pad_maximum_fusion.9), channel_id=1, source_target_pairs={{0,20},{4,16},{8,28},{12,24},{16,4},{20,0},{24,12},{28,8},{1,21},{... | collective-permute-start | bytes 884744 | tf_op jit(solution)/shard_map/ppermute | solution.py:40
  68.8 13.8 %collective-permute-start.34 = (bf16[32,4608]{1,0:T(8,128)(2,1)S(1)}, bf16[32,4608]{1,0:T(8,128)(2,1)S(1)}, u32[]{:S(2)}, u32[]{:S(2)}) collective-permute-start(bf16[32,4608]{1,0:T(8,128)(2,1)S(1)} %pad_maximum_fusion.10), channel_id=1, source_target_pairs={{0,24},{4,28},{8,16},{12,20},{16,8},{20,12},{24,0},{28,4},{1,25},{... | collective-permute-start | bytes 884744 | tf_op jit(solution)/shard_map/ppermute | solution.py:40
  82.6 54.8 %collective-permute-start.23 = (bf16[256,1536]{1,0:T(8,128)(2,1)S(1)}, bf16[256,1536]{1,0:T(8,128)(2,1)}, u32[]{:S(2)}, u32[]{:S(2)}) collective-permute-start(bf16[256,1536]{1,0:T(8,128)(2,1)S(1)} %slice.48.refs_9_), channel_id=1, source_target_pairs={{0,1},{1,2},{2,3},{4,5},{5,6},{6,7},{8,9},{9,10},{10,11},{12,13},{... | collective-permute-start | bytes 2359304 | tf_op jit(solution)/shard_map/ppermute | solution.py:73
  90.3 48.5 %collective-permute-start.24 = (bf16[256,1536]{1,0:T(8,128)(2,1)S(1)}, bf16[256,1536]{1,0:T(8,128)(2,1)}, u32[]{:S(2)}, u32[]{:S(2)}) collective-permute-start(bf16[256,1536]{1,0:T(8,128)(2,1)S(1)} %slice.48.refs_9_), channel_id=1, source_target_pairs={{1,0},{2,1},{3,2},{5,4},{6,5},{7,6},{9,8},{10,9},{11,10},{13,12},{... | collective-permute-start | bytes 2359304 | tf_op jit(solution)/shard_map/ppermute | solution.py:74
  91.7 52.3 %collective-permute-start.36 = (bf16[256,1536]{1,0:T(8,128)(2,1)S(1)}, bf16[256,1536]{1,0:T(8,128)(2,1)}, u32[]{:S(2)}, u32[]{:S(2)}) collective-permute-start(bf16[256,1536]{1,0:T(8,128)(2,1)S(1)} %slice.49.refs_9_), channel_id=1, source_target_pairs={{0,1},{1,2},{2,3},{4,5},{5,6},{6,7},{8,9},{9,10},{10,11},{12,13},{... | collective-permute-start | bytes 2359304 | tf_op jit(solution)/shard_map/ppermute | solution.py:73
  99.2 32.4 %collective-permute-start.55 = (bf16[256,1024]{1,0:T(8,128)(2,1)}, bf16[256,1024]{1,0:T(8,128)(2,1)}, u32[]{:S(2)}, u32[]{:S(2)}) collective-permute-start(bf16[256,1024]{1,0:T(8,128)(2,1)} %slice.54.refs_9_), channel_id=1, source_target_pairs={{0,1},{1,2},{2,3},{4,5},{5,6},{6,7},{8,9},{9,10},{10,11},{12,13},{... | collective-permute-start | bytes 1572872 | tf_op jit(solution)/shard_map/ppermute | solution.py:73
  103.1 33.0 %collective-permute-start.56 = (bf16[256,1024]{1,0:T(8,128)(2,1)}, bf16[256,1024]{1,0:T(8,128)(2,1)}, u32[]{:S(2)}, u32[]{:S(2)}) collective-permute-start(bf16[256,1024]{1,0:T(8,128)(2,1)} %slice.54.refs_9_), channel_id=1, source_target_pairs={{1,0},{2,1},{3,2},{5,4},{6,5},{7,6},{9,8},{10,9},{11,10},{13,12},{... | collective-permute-start | bytes 1572872 | tf_op jit(solution)/shard_map/ppermute | solution.py:74
  131.6 49.3 %collective-permute-start.17 = (bf16[256,2048]{1,0:T(8,128)(2,1)S(1)}, bf16[256,2048]{1,0:T(8,128)(2,1)S(1)}, u32[]{:S(2)}, u32[]{:S(2)}) collective-permute-start(bf16[256,2048]{1,0:T(8,128)(2,1)S(1)} %slice.47.refs_9_), channel_id=1, source_target_pairs={{0,1},{1,2},{2,3},{4,5},{5,6},{6,7},{8,9},{9,10},{10,11},{12,13},{... | collective-permute-start | bytes 3145736 | tf_op jit(solution)/shard_map/ppermute | solution.py:73
  136.1 46.1 %collective-permute-start.18 = (bf16[256,2048]{1,0:T(8,128)(2,1)S(1)}, bf16[256,2048]{1,0:T(8,128)(2,1)S(1)}, u32[]{:S(2)}, u32[]{:S(2)}) collective-permute-start(bf16[256,2048]{1,0:T(8,128)(2,1)S(1)} %slice.47.refs_9_), channel_id=1, source_target_pairs={{1,0},{2,1},{3,2},{5,4},{6,5},{7,6},{9,8},{10,9},{11,10},{13,12},{... | collective-permute-start | bytes 3145736 | tf_op jit(solution)/shard_map/ppermute | solution.py:74
  137.4 43.5 %collective-permute-start.38 = (bf16[256,1536]{1,0:T(8,128)(2,1)S(1)}, bf16[256,1536]{1,0:T(8,128)(2,1)S(1)}, u32[]{:S(2)}, u32[]{:S(2)}) collective-permute-start(bf16[256,1536]{1,0:T(8,128)(2,1)S(1)} %slice.49.refs_9_), channel_id=1, source_target_pairs={{1,0},{2,1},{3,2},{5,4},{6,5},{7,6},{9,8},{10,9},{11,10},{13,12},{... | collective-permute-start | bytes 2359304 | tf_op jit(solution)/shard_map/ppermute | solution.py:74
  138.7 44.2 %collective-permute-start.40 = (bf16[256,2048]{1,0:T(8,128)(2,1)S(1)}, bf16[256,2048]{1,0:T(8,128)(2,1)S(1)}, u32[]{:S(2)}, u32[]{:S(2)}) collective-permute-start(bf16[256,2048]{1,0:T(8,128)(2,1)S(1)} %slice.50.refs_9_), channel_id=1, source_target_pairs={{0,1},{1,2},{2,3},{4,5},{5,6},{6,7},{8,9},{9,10},{10,11},{12,13},{... | collective-permute-start | bytes 3145736 | tf_op jit(solution)/shard_map/ppermute | solution.py:73
  144.0 59.3 %collective-permute-start.41 = (bf16[256,2048]{1,0:T(8,128)(2,1)S(1)}, bf16[256,2048]{1,0:T(8,128)(2,1)S(1)}, u32[]{:S(2)}, u32[]{:S(2)}) collective-permute-start(bf16[256,2048]{1,0:T(8,128)(2,1)S(1)} %slice.50.refs_9_), channel_id=1, source_target_pairs={{1,0},{2,1},{3,2},{5,4},{6,5},{7,6},{9,8},{10,9},{11,10},{13,12},{... | collective-permute-start | bytes 3145736 | tf_op jit(solution)/shard_map/ppermute | solution.py:74
  180.9 37.9 %collective-permute-start.3 = (bf16[4,32,4096]{2,1,0:T(8,128)(2,1)S(1)}, bf16[4,32,4096]{2,1,0:T(8,128)(2,1)S(1)}, u32[]{:S(2)}, u32[]{:S(2)}) collective-permute-start(bf16[4,32,4096]{2,1,0:T(8,128)(2,1)S(1)} %fusion.1.refs_1_), channel_id=1, source_target_pairs={{0,4},{4,0},{8,12},{12,8},{16,20},{20,16},{24,28},{28,24},{1,5},{5... | collective-permute-start | bytes 3145736 | tf_op jit(solution)/shard_map/ppermute | solution.py:64
  180.9 32.0 %collective-permute-start.57 = (bf16[256,1024]{1,0:T(8,128)(2,1)}, bf16[256,1024]{1,0:T(8,128)(2,1)S(1)}, u32[]{:S(2)}, u32[]{:S(2)}) collective-permute-start(bf16[256,1024]{1,0:T(8,128)(2,1)} %collective-permute-done.56.refs_15_), channel_id=1, source_target_pairs={{1,0},{2,1},{5,4},{6,5},{9,8},{10,9},{13,12},{14,13},{17,16},{18,1... | collective-permute-start | bytes 1572872 | tf_op jit(solution)/shard_map/ppermute | solution.py:74
  182.2 35.3 %collective-permute-start.59 = (bf16[256,1024]{1,0:T(8,128)(2,1)}, bf16[256,1024]{1,0:T(8,128)(2,1)S(1)}, u32[]{:S(2)}, u32[]{:S(2)}) collective-permute-start(bf16[256,1024]{1,0:T(8,128)(2,1)} %collective-permute-done.55.refs_10_), channel_id=1, source_target_pairs={{1,2},{2,3},{5,6},{6,7},{9,10},{10,11},{13,14},{14,15},{17,18},{18... | collective-permute-start | bytes 1572872 | tf_op jit(solution)/shard_map/ppermute | solution.py:73
  182.9 36.8 %collective-permute-start.4 = (bf16[4,32,4096]{2,1,0:T(8,128)(2,1)S(1)}, bf16[4,32,4096]{2,1,0:T(8,128)(2,1)S(1)}, u32[]{:S(2)}, u32[]{:S(2)}) collective-permute-start(bf16[4,32,4096]{2,1,0:T(8,128)(2,1)S(1)} %fusion.1.refs_1_), channel_id=1, source_target_pairs={{0,8},{4,12},{8,0},{12,4},{16,24},{20,28},{24,16},{28,20},{1,9},{5... | collective-permute-start | bytes 3145736 | tf_op jit(solution)/shard_map/ppermute | solution.py:62
  203.3 44.2 %collective-permute-start.6 = (bf16[4,32,4096]{2,1,0:T(8,128)(2,1)S(1)}, bf16[4,32,4096]{2,1,0:T(8,128)(2,1)S(1)}, u32[]{:S(2)}, u32[]{:S(2)}) collective-permute-start(bf16[4,32,4096]{2,1,0:T(8,128)(2,1)S(1)} %fusion.1.refs_1_), channel_id=1, source_target_pairs={{0,16},{4,20},{8,24},{12,28},{16,0},{20,4},{24,8},{28,12},{1,17},{... | collective-permute-start | bytes 3145736 | tf_op jit(solution)/shard_map/ppermute | solution.py:62
  212.9 36.0 %collective-permute-start.8 = (bf16[4,32,4096]{2,1,0:T(8,128)(2,1)S(1)}, bf16[4,32,4096]{2,1,0:T(8,128)(2,1)S(1)}, u32[]{:S(2)}, u32[]{:S(2)}) collective-permute-start(bf16[4,32,4096]{2,1,0:T(8,128)(2,1)S(1)} %fusion.1.refs_1_), channel_id=1, source_target_pairs={{0,24},{4,28},{8,16},{12,20},{16,8},{20,12},{24,0},{28,4},{1,25},{... | collective-permute-start | bytes 3145736 | tf_op jit(solution)/shard_map/ppermute | solution.py:62
  217.5 32.7 %collective-permute-start.25 = (bf16[256,1536]{1,0:T(8,128)(2,1)}, bf16[256,1536]{1,0:T(8,128)(2,1)S(1)}, u32[]{:S(2)}, u32[]{:S(2)}) collective-permute-start(bf16[256,1536]{1,0:T(8,128)(2,1)} %collective-permute-done.24.refs_15_), channel_id=1, source_target_pairs={{1,0},{2,1},{5,4},{6,5},{9,8},{10,9},{13,12},{14,13},{17,16},{18,1... | collective-permute-start | bytes 2359304 | tf_op jit(solution)/shard_map/ppermute | solution.py:74
  218.8 33.1 %collective-permute-start.27 = (bf16[256,1536]{1,0:T(8,128)(2,1)}, bf16[256,1536]{1,0:T(8,128)(2,1)S(1)}, u32[]{:S(2)}, u32[]{:S(2)}) collective-permute-start(bf16[256,1536]{1,0:T(8,128)(2,1)} %collective-permute-done.23.refs_10_), channel_id=1, source_target_pairs={{1,2},{2,3},{5,6},{6,7},{9,10},{10,11},{13,14},{14,15},{17,18},{18... | collective-permute-start | bytes 2359304 | tf_op jit(solution)/shard_map/ppermute | solution.py:73
  219.8 33.8 %collective-permute-start.37 = (bf16[256,1536]{1,0:T(8,128)(2,1)}, bf16[256,1536]{1,0:T(8,128)(2,1)}, u32[]{:S(2)}, u32[]{:S(2)}) collective-permute-start(bf16[256,1536]{1,0:T(8,128)(2,1)} %collective-permute-done.36.refs_10_), channel_id=1, source_target_pairs={{1,2},{2,3},{5,6},{6,7},{9,10},{10,11},{13,14},{14,15},{17,18},{18... | collective-permute-start | bytes 2359304 | tf_op jit(solution)/shard_map/ppermute | solution.py:73
  247.6 22.3 %collective-permute-start.39 = (bf16[256,1536]{1,0:T(8,128)(2,1)S(1)}, bf16[256,1536]{1,0:T(8,128)(2,1)S(1)}, u32[]{:S(2)}, u32[]{:S(2)}) collective-permute-start(bf16[256,1536]{1,0:T(8,128)(2,1)S(1)} %collective-permute-done.38.refs_13_), channel_id=1, source_target_pairs={{1,0},{2,1},{5,4},{6,5},{9,8},{10,9},{13,12},{14,13},{17,16},{18,1... | collective-permute-start | bytes 2359304 | tf_op jit(solution)/shard_map/ppermute | solution.py:74
  248.9 51.0 %collective-permute-start.19 = (bf16[256,2048]{1,0:T(8,128)(2,1)S(1)}, bf16[256,2048]{1,0:T(8,128)(2,1)}, u32[]{:S(2)}, u32[]{:S(2)}) collective-permute-start(bf16[256,2048]{1,0:T(8,128)(2,1)S(1)} %collective-permute-done.18.refs_15_), channel_id=1, source_target_pairs={{1,0},{2,1},{5,4},{6,5},{9,8},{10,9},{13,12},{14,13},{17,16},{18,1... | collective-permute-start | bytes 3145736 | tf_op jit(solution)/shard_map/ppermute | solution.py:74
  250.2 51.0 %collective-permute-start.21 = (bf16[256,2048]{1,0:T(8,128)(2,1)S(1)}, bf16[256,2048]{1,0:T(8,128)(2,1)}, u32[]{:S(2)}, u32[]{:S(2)}) collective-permute-start(bf16[256,2048]{1,0:T(8,128)(2,1)S(1)} %collective-permute-done.17.refs_10_), channel_id=1, source_target_pairs={{1,2},{2,3},{5,6},{6,7},{9,10},{10,11},{13,14},{14,15},{17,18},{18... | collective-permute-start | bytes 3145736 | tf_op jit(solution)/shard_map/ppermute | solution.py:73
  251.9 46.6 %collective-permute-start.58 = (bf16[256,1024]{1,0:T(8,128)(2,1)S(1)}, bf16[256,1024]{1,0:T(8,128)(2,1)S(1)}, u32[]{:S(2)}, u32[]{:S(2)}) collective-permute-start(bf16[256,1024]{1,0:T(8,128)(2,1)S(1)} %collective-permute-done.57.refs_13_), channel_id=1, source_target_pairs={{1,0},{5,4},{9,8},{13,12},{17,16},{21,20},{25,24},{29,28}} | collective-permute-start | bytes 1572872 | tf_op jit(solution)/shard_map/ppermute | solution.py:74
  253.6 68.6 %collective-permute-start.49 = (bf16[4,32,7168]{2,1,0:T(8,128)(2,1)S(1)}, bf16[4,32,7168]{2,1,0:T(8,128)(2,1)S(1)}, u32[]{:S(2)}, u32[]{:S(2)}) collective-permute-start(bf16[4,32,7168]{2,1,0:T(8,128)(2,1)S(1)} %fusion.refs_1_), channel_id=1, source_target_pairs={{0,8},{4,12},{8,0},{12,4},{16,24},{20,28},{24,16},{28,20},{1,9},{5... | collective-permute-start | bytes 5505032 | tf_op jit(solution)/shard_map/ppermute | solution.py:62
  269.9 71.1 %collective-permute-start.51 = (bf16[4,32,7168]{2,1,0:T(8,128)(2,1)S(1)}, bf16[4,32,7168]{2,1,0:T(8,128)(2,1)S(1)}, u32[]{:S(2)}, u32[]{:S(2)}) collective-permute-start(bf16[4,32,7168]{2,1,0:T(8,128)(2,1)S(1)} %fusion.refs_1_), channel_id=1, source_target_pairs={{0,16},{4,20},{8,24},{12,28},{16,0},{20,4},{24,8},{28,12},{1,17},{... | collective-permute-start | bytes 5505032 | tf_op jit(solution)/shard_map/ppermute | solution.py:62
  298.5 43.2 %collective-permute-start.53 = (bf16[4,32,7168]{2,1,0:T(8,128)(2,1)S(1)}, bf16[4,32,7168]{2,1,0:T(8,128)(2,1)S(1)}, u32[]{:S(2)}, u32[]{:S(2)}) collective-permute-start(bf16[4,32,7168]{2,1,0:T(8,128)(2,1)S(1)} %fusion.refs_1_), channel_id=1, source_target_pairs={{0,24},{4,28},{8,16},{12,20},{16,8},{20,12},{24,0},{28,4},{1,25},{... | collective-permute-start | bytes 5505032 | tf_op jit(solution)/shard_map/ppermute | solution.py:62
  299.9 21.8 %collective-permute-start.42 = (bf16[256,2048]{1,0:T(8,128)(2,1)S(1)}, bf16[256,2048]{1,0:T(8,128)(2,1)}, u32[]{:S(2)}, u32[]{:S(2)}) collective-permute-start(bf16[256,2048]{1,0:T(8,128)(2,1)S(1)} %collective-permute-done.41.refs_15_), channel_id=1, source_target_pairs={{1,0},{2,1},{5,4},{6,5},{9,8},{10,9},{13,12},{14,13},{17,16},{18,1... | collective-permute-start | bytes 3145736 | tf_op jit(solution)/shard_map/ppermute | solution.py:74
  301.2 20.5 %collective-permute-start.44 = (bf16[256,2048]{1,0:T(8,128)(2,1)S(1)}, bf16[256,2048]{1,0:T(8,128)(2,1)}, u32[]{:S(2)}, u32[]{:S(2)}) collective-permute-start(bf16[256,2048]{1,0:T(8,128)(2,1)S(1)} %collective-permute-done.40.refs_10_), channel_id=1, source_target_pairs={{1,2},{2,3},{5,6},{6,7},{9,10},{10,11},{13,14},{14,15},{17,18},{18... | collective-permute-start | bytes 3145736 | tf_op jit(solution)/shard_map/ppermute | solution.py:73
  321.7 24.9 %collective-permute-start.5 = (bf16[4,32,4096]{2,1,0:T(8,128)(2,1)S(1)}, bf16[4,32,4096]{2,1,0:T(8,128)(2,1)S(1)}, u32[]{:S(2)}, u32[]{:S(2)}) collective-permute-start(bf16[4,32,4096]{2,1,0:T(8,128)(2,1)S(1)} %collective-permute-done.4.refs_3_), channel_id=1, source_target_pairs={{0,4},{4,0},{8,12},{12,8},{16,20},{20,16},{24,28},{28,24},{1,5},{5... | collective-permute-start | bytes 3145736 | tf_op jit(solution)/shard_map/ppermute | solution.py:64
  321.7 26.1 %collective-permute-start.7 = (bf16[4,32,4096]{2,1,0:T(8,128)(2,1)S(1)}, bf16[4,32,4096]{2,1,0:T(8,128)(2,1)S(1)}, u32[]{:S(2)}, u32[]{:S(2)}) collective-permute-start(bf16[4,32,4096]{2,1,0:T(8,128)(2,1)S(1)} %collective-permute-done.6.refs_5_), channel_id=1, source_target_pairs={{0,4},{4,0},{8,12},{12,8},{16,20},{20,16},{24,28},{28,24},{1,5},{5... | collective-permute-start | bytes 3145736 | tf_op jit(solution)/shard_map/ppermute | solution.py:64
  322.2 21.4 %collective-permute-start.26 = (bf16[256,1536]{1,0:T(8,128)(2,1)S(1)}, bf16[256,1536]{1,0:T(8,128)(2,1)S(1)}, u32[]{:S(2)}, u32[]{:S(2)}) collective-permute-start(bf16[256,1536]{1,0:T(8,128)(2,1)S(1)} %collective-permute-done.25.refs_13_), channel_id=1, source_target_pairs={{1,0},{5,4},{9,8},{13,12},{17,16},{21,20},{25,24},{29,28}} | collective-permute-start | bytes 2359304 | tf_op jit(solution)/shard_map/ppermute | solution.py:74
  343.6 28.2 %collective-permute-start.20 = (bf16[256,2048]{1,0:T(8,128)(2,1)}, bf16[256,2048]{1,0:T(8,128)(2,1)}, u32[]{:S(2)}, u32[]{:S(2)}) collective-permute-start(bf16[256,2048]{1,0:T(8,128)(2,1)} %collective-permute-done.19.refs_13_), channel_id=1, source_target_pairs={{1,0},{5,4},{9,8},{13,12},{17,16},{21,20},{25,24},{29,28}} | collective-permute-start | bytes 3145736 | tf_op jit(solution)/shard_map/ppermute | solution.py:74
  344.9 26.9 %collective-permute-start.22 = (bf16[256,2048]{1,0:T(8,128)(2,1)}, bf16[256,2048]{1,0:T(8,128)(2,1)}, u32[]{:S(2)}, u32[]{:S(2)}) collective-permute-start(bf16[256,2048]{1,0:T(8,128)(2,1)} %collective-permute-done.21.refs_12_), channel_id=1, source_target_pairs={{2,3},{6,7},{10,11},{14,15},{18,19},{22,23},{26,27},{30,31}} | collective-permute-start | bytes 3145736 | tf_op jit(solution)/shard_map/ppermute | solution.py:73
  346.5 46.0 %collective-permute-start.43 = (bf16[256,2048]{1,0:T(8,128)(2,1)}, bf16[256,2048]{1,0:T(8,128)(2,1)}, u32[]{:S(2)}, u32[]{:S(2)}) collective-permute-start(bf16[256,2048]{1,0:T(8,128)(2,1)} %collective-permute-done.42.refs_13_), channel_id=1, source_target_pairs={{1,0},{5,4},{9,8},{13,12},{17,16},{21,20},{25,24},{29,28}} | collective-permute-start | bytes 3145736 | tf_op jit(solution)/shard_map/ppermute | solution.py:74
  347.8 16.9 %collective-permute-start.46 = (bf16[256,1536]{1,0:T(8,128)(2,1)}, bf16[256,1536]{1,0:T(8,128)(2,1)}, u32[]{:S(2)}, u32[]{:S(2)}) collective-permute-start(bf16[256,1536]{1,0:T(8,128)(2,1)} %collective-permute-done.37.refs_11_), channel_id=1, source_target_pairs={{2,3},{6,7},{10,11},{14,15},{18,19},{22,23},{26,27},{30,31}} | collective-permute-start | bytes 2359304 | tf_op jit(solution)/shard_map/ppermute | solution.py:73
  350.5 58.1 %collective-permute-start.45 = (bf16[256,2048]{1,0:T(8,128)(2,1)}, bf16[256,2048]{1,0:T(8,128)(2,1)}, u32[]{:S(2)}, u32[]{:S(2)}) collective-permute-start(bf16[256,2048]{1,0:T(8,128)(2,1)} %collective-permute-done.44.refs_12_), channel_id=1, source_target_pairs={{2,3},{6,7},{10,11},{14,15},{18,19},{22,23},{26,27},{30,31}} | collective-permute-start | bytes 3145736 | tf_op jit(solution)/shard_map/ppermute | solution.py:73
  364.7 89.1 %collective-permute-start.48 = (bf16[4,32,7168]{2,1,0:T(8,128)(2,1)S(1)}, bf16[4,32,7168]{2,1,0:T(8,128)(2,1)}, u32[]{:S(2)}, u32[]{:S(2)}) collective-permute-start(bf16[4,32,7168]{2,1,0:T(8,128)(2,1)S(1)} %fusion.refs_1_), channel_id=1, source_target_pairs={{0,4},{4,0},{8,12},{12,8},{16,20},{20,16},{24,28},{28,24},{1,5},{5... | collective-permute-start | bytes 5505032 | tf_op jit(solution)/shard_map/ppermute | solution.py:64
  371.8 82.0 %collective-permute-start.50 = (bf16[4,32,7168]{2,1,0:T(8,128)(2,1)}, bf16[4,32,7168]{2,1,0:T(8,128)(2,1)}, u32[]{:S(2)}, u32[]{:S(2)}) collective-permute-start(bf16[4,32,7168]{2,1,0:T(8,128)(2,1)} %copy-done.36), channel_id=1, source_target_pairs={{0,4},{4,0},{8,12},{12,8},{16,20},{20,16},{24,28},{28,24},{1,5},{5... | collective-permute-start | bytes 5505032 | tf_op jit(solution)/shard_map/ppermute | solution.py:64
  371.8 82.0 %collective-permute-start.52 = (bf16[4,32,7168]{2,1,0:T(8,128)(2,1)}, bf16[4,32,7168]{2,1,0:T(8,128)(2,1)}, u32[]{:S(2)}, u32[]{:S(2)}) collective-permute-start(bf16[4,32,7168]{2,1,0:T(8,128)(2,1)} %copy-done.37), channel_id=1, source_target_pairs={{0,4},{4,0},{8,12},{12,8},{16,20},{20,16},{24,28},{28,24},{1,5},{5... | collective-permute-start | bytes 5505032 | tf_op jit(solution)/shard_map/ppermute | solution.py:64
  392.5 61.3 %collective-permute-start.54 = (bf16[4,32,7168]{2,1,0:T(8,128)(2,1)}, bf16[4,32,7168]{2,1,0:T(8,128)(2,1)}, u32[]{:S(2)}, u32[]{:S(2)}) collective-permute-start(bf16[4,32,7168]{2,1,0:T(8,128)(2,1)} %copy-done.38), channel_id=1, source_target_pairs={{0,4},{4,0},{8,12},{12,8},{16,20},{20,16},{24,28},{28,24},{1,5},{5... | collective-permute-start | bytes 5505032 | tf_op jit(solution)/shard_map/ppermute | solution.py:64
  408.6 22.0 %collective-permute-start.47 = (bf16[256,1536]{1,0:T(8,128)(2,1)S(1)}, bf16[256,1536]{1,0:T(8,128)(2,1)S(1)}, u32[]{:S(2)}, u32[]{:S(2)}) collective-permute-start(bf16[256,1536]{1,0:T(8,128)(2,1)S(1)} %copy-done.21), channel_id=1, source_target_pairs={{1,0},{5,4},{9,8},{13,12},{17,16},{21,20},{25,24},{29,28}} | collective-permute-start | bytes 2359304 | tf_op jit(solution)/shard_map/ppermute | solution.py:74
  430.5 23.2 %collective-permute-start.60 = (bf16[256,1024]{1,0:T(8,128)(2,1)S(1)}, bf16[256,1024]{1,0:T(8,128)(2,1)S(1)}, u32[]{:S(2)}, u32[]{:S(2)}) collective-permute-start(bf16[256,1024]{1,0:T(8,128)(2,1)S(1)} %copy-done.41), channel_id=1, source_target_pairs={{2,3},{6,7},{10,11},{14,15},{18,19},{22,23},{26,27},{30,31}} | collective-permute-start | bytes 1572872 | tf_op jit(solution)/shard_map/ppermute | solution.py:73
  (59 other events, 2029.9 us)

commit v3 on v2

--- a/solution.py
+++ b/solution.py
@@ -244,8 +244,8 @@
     n_col = lax.axis_size("col")
     depth = a_pieces[0].shape[1]
     width = done.shape[1]
-    block = next(b for b in range(896, 0, -128) if rows % b == 0 and first % b == 0)
-    tile = next(size for size in (1024, 512, 256, 128) if width % size == 0)
+    block = next(b for b in (256, 128) if rows % b == 0 and first % b == 0)
+    tile = next(size for size in (2048, 1024, 512, 256, 128) if width % size == 0)
     skip = first // block
     anywhere = pl.BlockSpec(memory_space=pl.ANY)
     spec = pl.BlockSpec((block, tile), lambda t, g: (g + skip, t))
@@ -388,7 +388,7 @@
         return done
 
     merged_gate = merged(gate_weight, mlp_pieces, 0, gate_mine, 0, (1, 1))
-    merged_up = merged(up_weight, mlp_pieces, gate_cols, rest_mine, down_rows, (4, 3), True)
+    merged_up = merged(up_weight, mlp_pieces, gate_cols, rest_mine, down_rows, (3, 4), True)
 
     arrivals = line_gather(rest_mine[:, :down_rows])
     merged_down = merge_rows(down_weight, down_pieces, 0, arrivals, 0, 0, down_rows)

time: 488 us -> 524 us (1.074)
  the two profiles are of different devices: /device:TPU:0 before, /device:TPU:17 now
where the time goes in v3:
time: 524 us; the launch traced here: 521 us
  waiting for transfers between devices  278 us (53%)
  starting transfers between devices  116 us (22%)
  Pallas kernels  94.9 us (18%)
  local copies, waits for them, and re-layouts  24 us (5%)
  other arithmetic  6.27 us (1%)
    ppermute x15, waiting for transfers between devices, line_gather(): up = lax.ppermute(up, 'col', [(j, j + 1) for j in range(s - 1, n_col - 1)])  107 us
    pallas_call x5, Pallas kernels, merge_rows(): pl.pallas_call(functools.partial(merge_kernel, n_row, n_col, block, tile,...  82.5 us
    ppermute x15, waiting for transfers between devices, line_gather(): lax.ppermute(down, 'col', [(j, j - 1) for j in range(1, n_col + 1 - s)])  68.4 us
    ppermute x6, waiting for transfers between devices, gather_rows(): pieces[i] = lax.ppermute(block, 'row', [(k, k ^ i) for k in range(n_row)])  52.2 us
    ppermute x14, waiting for transfers between devices, spread_rows(): piece = lax.ppermute(piece, 'row', [(k, k ^ i) for k in range(n_row)])  50.6 us
    ppermute x15, starting transfers between devices, line_gather(): up = lax.ppermute(up, 'col', [(j, j + 1) for j in range(s - 1, n_col - 1)])  39.2 us
    ppermute x15, starting transfers between devices, line_gather(): lax.ppermute(down, 'col', [(j, j - 1) for j in range(1, n_col + 1 - s)])  37.7 us
    ppermute x8, starting transfers between devices, gather_rows(): lax.ppermute(pieces[i], 'row', [(k, k ^ 1) for k in range(n_row)])  17.7 us
  transfers between devices with their start and end apart: 61, of which 20 were waited for; matrix products, arithmetic and copies ran while one was open for 4% of the time, Pallas kernels for 13%

profile of v3, /device:TPU:17, one launch (start us, length us, event | category | flops | bytes accessed | tf_op | source)
XLA Modules:
  0.0 521.3 jit_solution(15915011242019014021)
XLA Ops:
  0.7 2.5 constant_dynamic-slice_fusion.34
  6.0 3.2 collective-permute-start.1
  10.1 2.7 constant_dynamic-slice_fusion.16
  15.4 2.4 constant_dynamic-slice_fusion
  25.1 4.2 collective-permute-done.12
  32.2 9.6 %collective-permute-done.14 = bf16[32,3584]{1,0:T(8,128)(2,1)S(1)} collective-permute-done((bf16[32,3584]{1,0:T(8,128)(2,1)S(1)}, bf16[32,3584]{1,0:T(8,128)(2,1)S(1)}, u32[]{:S(2)}, u32[]{:S(2)}) %collective-permute-start.14) | collective-permute-done | bytes 229408 | tf_op jit(solution)/shard_map/ppermute | solution.py:40
  43.5 5.9 %collective-permute-done.16 = bf16[32,3584]{1,0:T(8,128)(2,1)S(1)} collective-permute-done((bf16[32,3584]{1,0:T(8,128)(2,1)S(1)}, bf16[32,3584]{1,0:T(8,128)(2,1)S(1)}, u32[]{:S(2)}, u32[]{:S(2)}) %collective-permute-start.16) | collective-permute-done | bytes 229408 | tf_op jit(solution)/shard_map/ppermute | solution.py:40
  50.8 7.6 %collective-permute-done.30 = bf16[32,4608]{1,0:T(8,128)(2,1)S(1)} collective-permute-done((bf16[32,4608]{1,0:T(8,128)(2,1)S(1)}, bf16[32,4608]{1,0:T(8,128)(2,1)S(1)}, u32[]{:S(2)}, u32[]{:S(2)}) %collective-permute-start.30) | collective-permute-done | bytes 294944 | tf_op jit(solution)/shard_map/ppermute | solution.py:40
  59.7 5.1 collective-permute-done.31
  67.9 12.3 %collective-permute-done.33 = bf16[32,4608]{1,0:T(8,128)(2,1)S(1)} collective-permute-done((bf16[32,4608]{1,0:T(8,128)(2,1)S(1)}, bf16[32,4608]{1,0:T(8,128)(2,1)S(1)}, u32[]{:S(2)}, u32[]{:S(2)}) %collective-permute-start.33) | collective-permute-done | bytes 294944 | tf_op jit(solution)/shard_map/ppermute | solution.py:40
  81.7 2.8 collective-permute-start.23
  84.5 5.6 %collective-permute-done.35 = bf16[32,4608]{1,0:T(8,128)(2,1)S(1)} collective-permute-done((bf16[32,4608]{1,0:T(8,128)(2,1)S(1)}, bf16[32,4608]{1,0:T(8,128)(2,1)S(1)}, u32[]{:S(2)}, u32[]{:S(2)}) %collective-permute-start.35) | collective-permute-done | bytes 294944 | tf_op jit(solution)/shard_map/ppermute | solution.py:40
  92.4 4.0 collective-permute-start.40
  99.8 3.4 collective-permute-start.56
  108.4 22.3 %collective-permute-done.55.refs_10_ = bf16[256,1024]{1,0:T(8,128)(2,1)} collective-permute-done((bf16[256,1024]{1,0:T(8,128)(2,1)}, bf16[256,1024]{1,0:T(8,128)(2,1)}, u32[]{:S(2)}, u32[]{:S(2)}) %collective-permute-start.55) | collective-permute-done | bytes 524320 | tf_op jit(solution)/shard_map/ppermute | solution.py:73
  130.7 2.3 collective-permute-start.17
  133.0 3.0 collective-permute-start.18
  136.1 2.3 collective-permute-start.36
  138.4 2.9 collective-permute-start.38
  141.4 2.3 collective-permute-start.41
  144.0 53.2 %collective-permute-done.41.refs_15_ = bf16[256,1536]{1,0:T(8,128)(2,1)S(1)} collective-permute-done((bf16[256,1536]{1,0:T(8,128)(2,1)S(1)}, bf16[256,1536]{1,0:T(8,128)(2,1)S(1)}, u32[]{:S(2)}, u32[]{:S(2)}) %collective-permute-start.41) | collective-permute-done | bytes 786464 | tf_op jit(solution)/shard_map/ppermute | solution.py:74
  197.2 2.6 collective-permute-start.3
  199.8 3.0 collective-permute-start.57
  206.3 8.0 %collective-permute-done.57.refs_13_ = bf16[256,1024]{1,0:T(8,128)(2,1)S(1)} collective-permute-done((bf16[256,1024]{1,0:T(8,128)(2,1)}, bf16[256,1024]{1,0:T(8,128)(2,1)S(1)}, u32[]{:S(2)}, u32[]{:S(2)}) %collective-permute-start.57) | collective-permute-done | bytes 524320 | tf_op jit(solution)/shard_map/ppermute | solution.py:74
  218.7 4.0 collective-permute-start.25
  224.9 4.4 collective-permute-done.4.refs_3_
  229.3 4.0 collective-permute-start.42
  233.3 19.4 %collective-permute-done.6.refs_5_ = bf16[4,32,4096]{2,1,0:T(8,128)(2,1)S(1)} collective-permute-done((bf16[4,32,4096]{2,1,0:T(8,128)(2,1)S(1)}, bf16[4,32,4096]{2,1,0:T(8,128)(2,1)S(1)}, u32[]{:S(2)}, u32[]{:S(2)}) %collective-permute-start.6) | collective-permute-done | bytes 1048608 | tf_op jit(solution)/shard_map/ppermute | solution.py:62
  254.7 5.2 collective-permute-start.19
  263.8 8.8 %collective-permute-done.44.refs_12_ = bf16[256,1536]{1,0:T(8,128)(2,1)} collective-permute-done((bf16[256,1536]{1,0:T(8,128)(2,1)}, bf16[256,1536]{1,0:T(8,128)(2,1)}, u32[]{:S(2)}, u32[]{:S(2)}) %collective-permute-start.44) | collective-permute-done | bytes 786464 | tf_op jit(solution)/shard_map/ppermute | solution.py:73
  272.6 7.1 %collective-permute-done.19.refs_13_ = bf16[256,2048]{1,0:T(8,128)(2,1)} collective-permute-done((bf16[256,2048]{1,0:T(8,128)(2,1)S(1)}, bf16[256,2048]{1,0:T(8,128)(2,1)}, u32[]{:S(2)}, u32[]{:S(2)}) %collective-permute-start.19) | collective-permute-done | bytes 1048608 | tf_op jit(solution)/shard_map/ppermute | solution.py:74
  281.6 13.5 %collective-permute-done.21.refs_12_ = bf16[256,2048]{1,0:T(8,128)(2,1)} collective-permute-done((bf16[256,2048]{1,0:T(8,128)(2,1)S(1)}, bf16[256,2048]{1,0:T(8,128)(2,1)}, u32[]{:S(2)}, u32[]{:S(2)}) %collective-permute-start.21) | collective-permute-done | bytes 1048608 | tf_op jit(solution)/shard_map/ppermute | solution.py:73
  296.4 21.1 %collective-permute-done.37.refs_11_ = bf16[256,2048]{1,0:T(8,128)(2,1)} collective-permute-done((bf16[256,2048]{1,0:T(8,128)(2,1)S(1)}, bf16[256,2048]{1,0:T(8,128)(2,1)}, u32[]{:S(2)}, u32[]{:S(2)}) %collective-permute-start.37) | collective-permute-done | bytes 1048608 | tf_op jit(solution)/shard_map/ppermute | solution.py:73
  317.5 2.3 collective-permute-start.5
  320.9 28.4 %collective-permute-done.51.refs_5_ = bf16[4,32,7168]{2,1,0:T(8,128)(2,1)S(1)} collective-permute-done((bf16[4,32,7168]{2,1,0:T(8,128)(2,1)S(1)}, bf16[4,32,7168]{2,1,0:T(8,128)(2,1)S(1)}, u32[]{:S(2)}, u32[]{:S(2)}) %collective-permute-start.51) | collective-permute-done | bytes 1835040 | tf_op jit(solution)/shard_map/ppermute | solution.py:62
  350.0 2.8 collective-permute-start.28
  354.5 10.6 %collective-permute-done.28.refs_14_ = bf16[256,1536]{1,0:T(8,128)(2,1)S(1)} collective-permute-done((bf16[256,1536]{1,0:T(8,128)(2,1)S(1)}, bf16[256,1536]{1,0:T(8,128)(2,1)S(1)}, u32[]{:S(2)}, u32[]{:S(2)}) %collective-permute-start.28) | collective-permute-done | bytes 786464 | tf_op jit(solution)/shard_map/ppermute | solution.py:73
  365.2 5.1 collective-permute-start.22
  377.3 12.6 %shard_map.130.refs_16_ = bf16[3584,2048]{1,0:T(8,128)(2,1)} custom-call(bf16[3584,2048]{1,0:T(8,128)(2,1)} %refs_0_.6, bf16[4,32,4096]{2,1,0:T(8,128)(2,1)} %copy-done, bf16[4,32,4096]{2,1,0:T(8,128)(2,1)} %copy-done.1, bf16[4,32,4096]{2,1,0:T(8,128)(2,1)} %copy-done.2, bf16[4,32,4096]{2,1,0:T(8,128)(2,1)} %copy-done.5, bf16[4,32,4096]{2,1,0:T(8,128)(2,1)} %copy-done.3, ...), custom_call_target="tpu_custom_call" | custom-call | flops 6442450944 | bytes 19922944 | tf_op jit(solution)/shard_map/pallas_call | solution.py:296
  389.9 5.8 %collective-permute-start.48 = (bf16[4,32,7168]{2,1,0:T(8,128)(2,1)S(1)}, bf16[4,32,7168]{2,1,0:T(8,128)(2,1)}, u32[]{:S(2)}, u32[]{:S(2)}) collective-permute-start(bf16[4,32,7168]{2,1,0:T(8,128)(2,1)S(1)} %fusion.refs_1_), channel_id=1, source_target_pairs={{0,4},{4,0},{8,12},{12,8},{16,20},{20,16},{24,28},{28,24},{1,5},{5... | collective-permute-start | bytes 5505032 | tf_op jit(solution)/shard_map/ppermute | solution.py:64
  395.8 30.4 %collective-permute-done.45.refs_14_ = bf16[256,1536]{1,0:T(8,128)(2,1)} collective-permute-done((bf16[256,1536]{1,0:T(8,128)(2,1)}, bf16[256,1536]{1,0:T(8,128)(2,1)}, u32[]{:S(2)}, u32[]{:S(2)}) %collective-permute-start.45) | collective-permute-done | bytes 786464 | tf_op jit(solution)/shard_map/ppermute | solution.py:73
  427.1 6.3 %collective-permute-start.50 = (bf16[4,32,7168]{2,1,0:T(8,128)(2,1)}, bf16[4,32,7168]{2,1,0:T(8,128)(2,1)}, u32[]{:S(2)}, u32[]{:S(2)}) collective-permute-start(bf16[4,32,7168]{2,1,0:T(8,128)(2,1)} %copy-done.35), channel_id=1, source_target_pairs={{0,4},{4,0},{8,12},{12,8},{16,20},{20,16},{24,28},{28,24},{1,5},{5... | collective-permute-start | bytes 5505032 | tf_op jit(solution)/shard_map/ppermute | solution.py:64
  433.9 12.6 %shard_map.132.refs_14_ = bf16[3584,2048]{1,0:T(8,128)(2,1)} custom-call(bf16[3584,2048]{1,0:T(8,128)(2,1)} %refs_0_.8, bf16[4,32,4096]{2,1,0:T(8,128)(2,1)} %copy-done, bf16[4,32,4096]{2,1,0:T(8,128)(2,1)} %copy-done.1, bf16[4,32,4096]{2,1,0:T(8,128)(2,1)} %copy-done.2, bf16[4,32,4096]{2,1,0:T(8,128)(2,1)} %copy-done.5, bf16[4,32,4096]{2,1,0:T(8,128)(2,1)} %copy-done.3, ...), custom_call_target="tpu_custom_call" | custom-call | flops 6442450944 | bytes 19922944 | tf_op jit(solution)/shard_map/pallas_call | solution.py:296
  446.5 16.0 %shard_map.133.refs_0_ = bf16[3584,2048]{1,0:T(8,128)(2,1)} custom-call(bf16[3584,2048]{1,0:T(8,128)(2,1)} %refs_0_.8, bf16[4,32,4096]{2,1,0:T(8,128)(2,1)} %copy-done, bf16[4,32,4096]{2,1,0:T(8,128)(2,1)} %copy-done.1, bf16[4,32,4096]{2,1,0:T(8,128)(2,1)} %copy-done.2, bf16[4,32,4096]{2,1,0:T(8,128)(2,1)} %copy-done.5, ...), custom_call_target="tpu_custom_call", output_to_operand_aliasing={{}: (14, {})} | custom-call | flops 8589934592 | bytes 25165824 | tf_op jit(solution)/shard_map/pallas_call | solution.py:296
  462.6 4.0 collective-permute-start.60
  466.6 16.0 %shard_map.131 = bf16[3584,2048]{1,0:T(8,128)(2,1)} custom-call(bf16[3584,2048]{1,0:T(8,128)(2,1)} %refs_0_.6, bf16[4,32,4096]{2,1,0:T(8,128)(2,1)} %copy-done, bf16[4,32,4096]{2,1,0:T(8,128)(2,1)} %copy-done.1, bf16[4,32,4096]{2,1,0:T(8,128)(2,1)} %copy-done.2, bf16[4,32,4096]{2,1,0:T(8,128)(2,1)} %copy-done.5, ...), custom_call_target="tpu_custom_call", output_to_operand_aliasing={{}: (16, {})} | custom-call | flops 8589934592 | bytes 25165824 | tf_op jit(solution)/shard_map/pallas_call | solution.py:296
  482.7 12.4 %shard_map.134 = bf16[3584,2048]{1,0:T(8,128)(2,1)} custom-call(bf16[3584,2048]{1,0:T(8,128)(2,1)} %shard_map.133.refs_0_, bf16[4,32,4096]{2,1,0:T(8,128)(2,1)} %copy-done, bf16[4,32,4096]{2,1,0:T(8,128)(2,1)} %copy-done.1, bf16[4,32,4096]{2,1,0:T(8,128)(2,1)} %copy-done.2, bf16[4,32,4096]{2,1,0:T(8,128)(2,1)} %copy-done.5, ...), custom_call_target="tpu_custom_call", output_to_operand_aliasing={{}: (0, {})} | custom-call | flops 2147483648 | bytes 16777216 | tf_op jit(solution)/shard_map/pallas_call | solution.py:252
  495.9 25.3 %shard_map.135 = bf16[1024,7168]{1,0:T(8,128)(2,1)} custom-call(bf16[1024,7168]{1,0:T(8,128)(2,1)} %refs_0_.9, bf16[4,32,7168]{2,1,0:T(8,128)(2,1)} %copy-done.14, bf16[4,32,7168]{2,1,0:T(8,128)(2,1)} %collective-permute-done.48.refs_2_, bf16[4,32,7168]{2,1,0:T(8,128)(2,1)} %copy-done.35, bf16[4,32,7168]{2,1,0:T(8,128)(2,1)} %collective-permute-done.50.refs_4_, ...), custom_call_target="tpu_custom_call" | custom-call | flops 15032385536 | bytes 46137344 | tf_op jit(solution)/shard_map/pallas_call | solution.py:296
  (222 shorter events, 67.9 us)
Async XLA Ops:
  4.9 87.5 %collective-permute-start.2 = (bf16[32,11264]{1,0:T(8,128)(2,1)}, bf16[32,11264]{1,0:T(8,128)(2,1)}, u32[]{:S(2)}, u32[]{:S(2)}) collective-permute-start(bf16[32,11264]{1,0:T(8,128)(2,1)} %pad_maximum_fusion.4), channel_id=1, source_target_pairs={{0,3},{1,2},{2,1},{3,0},{4,7},{5,6},{6,5},{7,4},{8,11},{9,10},{10,... | collective-permute-start | bytes 2162696 | tf_op jit(solution)/shard_map/ppermute | solution.py:52
  6.0 91.9 %collective-permute-start.1 = (bf16[32,11264]{1,0:T(8,128)(2,1)}, bf16[32,11264]{1,0:T(8,128)(2,1)}, u32[]{:S(2)}, u32[]{:S(2)}) collective-permute-start(bf16[32,11264]{1,0:T(8,128)(2,1)} %pad_maximum_fusion.3), channel_id=1, source_target_pairs={{0,2},{1,3},{2,0},{3,1},{4,6},{5,7},{6,4},{7,5},{8,10},{9,11},{10,... | collective-permute-start | bytes 2162696 | tf_op jit(solution)/shard_map/ppermute | solution.py:52
  10.1 89.7 %collective-permute-start = (bf16[32,11264]{1,0:T(8,128)(2,1)}, bf16[32,11264]{1,0:T(8,128)(2,1)}, u32[]{:S(2)}, u32[]{:S(2)}) collective-permute-start(bf16[32,11264]{1,0:T(8,128)(2,1)} %pad_maximum_fusion.2), channel_id=1, source_target_pairs={{0,1},{1,0},{2,3},{3,2},{4,5},{5,4},{6,7},{7,6},{8,9},{9,8},{10,11... | collective-permute-start | bytes 2162696 | tf_op jit(solution)/shard_map/ppermute | solution.py:52
  50.2 14.6 %collective-permute-start.31 = (bf16[32,4608]{1,0:T(8,128)(2,1)S(1)}, bf16[32,4608]{1,0:T(8,128)(2,1)S(1)}, u32[]{:S(2)}, u32[]{:S(2)}) collective-permute-start(bf16[32,4608]{1,0:T(8,128)(2,1)S(1)} %pad_maximum_fusion.7), channel_id=1, source_target_pairs={{0,12},{4,8},{8,4},{12,0},{16,28},{20,24},{24,20},{28,16},{1,13},{... | collective-permute-start | bytes 884744 | tf_op jit(solution)/shard_map/ppermute | solution.py:40
  64.8 15.4 %collective-permute-start.33 = (bf16[32,4608]{1,0:T(8,128)(2,1)S(1)}, bf16[32,4608]{1,0:T(8,128)(2,1)S(1)}, u32[]{:S(2)}, u32[]{:S(2)}) collective-permute-start(bf16[32,4608]{1,0:T(8,128)(2,1)S(1)} %pad_maximum_fusion.9), channel_id=1, source_target_pairs={{0,20},{4,16},{8,28},{12,24},{16,4},{20,0},{24,12},{28,8},{1,21},{... | collective-permute-start | bytes 884744 | tf_op jit(solution)/shard_map/ppermute | solution.py:40
  66.6 15.0 %collective-permute-start.34 = (bf16[32,4608]{1,0:T(8,128)(2,1)S(1)}, bf16[32,4608]{1,0:T(8,128)(2,1)S(1)}, u32[]{:S(2)}, u32[]{:S(2)}) collective-permute-start(bf16[32,4608]{1,0:T(8,128)(2,1)S(1)} %pad_maximum_fusion.10), channel_id=1, source_target_pairs={{0,24},{4,28},{8,16},{12,20},{16,8},{20,12},{24,0},{28,4},{1,25},{... | collective-permute-start | bytes 884744 | tf_op jit(solution)/shard_map/ppermute | solution.py:40
  81.7 54.4 %collective-permute-start.23 = (bf16[256,1536]{1,0:T(8,128)(2,1)S(1)}, bf16[256,1536]{1,0:T(8,128)(2,1)}, u32[]{:S(2)}, u32[]{:S(2)}) collective-permute-start(bf16[256,1536]{1,0:T(8,128)(2,1)S(1)} %slice.48.refs_9_), channel_id=1, source_target_pairs={{0,1},{1,2},{2,3},{4,5},{5,6},{6,7},{8,9},{9,10},{10,11},{12,13},{... | collective-permute-start | bytes 2359304 | tf_op jit(solution)/shard_map/ppermute | solution.py:73
  90.1 48.4 %collective-permute-start.24 = (bf16[256,1536]{1,0:T(8,128)(2,1)S(1)}, bf16[256,1536]{1,0:T(8,128)(2,1)}, u32[]{:S(2)}, u32[]{:S(2)}) collective-permute-start(bf16[256,1536]{1,0:T(8,128)(2,1)S(1)} %slice.48.refs_9_), channel_id=1, source_target_pairs={{1,0},{2,1},{3,2},{5,4},{6,5},{7,6},{9,8},{10,9},{11,10},{13,12},{... | collective-permute-start | bytes 2359304 | tf_op jit(solution)/shard_map/ppermute | solution.py:74
  92.4 49.0 %collective-permute-start.40 = (bf16[256,1536]{1,0:T(8,128)(2,1)S(1)}, bf16[256,1536]{1,0:T(8,128)(2,1)}, u32[]{:S(2)}, u32[]{:S(2)}) collective-permute-start(bf16[256,1536]{1,0:T(8,128)(2,1)S(1)} %slice.50.refs_9_), channel_id=1, source_target_pairs={{0,1},{1,2},{2,3},{4,5},{5,6},{6,7},{8,9},{9,10},{10,11},{12,13},{... | collective-permute-start | bytes 2359304 | tf_op jit(solution)/shard_map/ppermute | solution.py:73
  97.9 32.9 %collective-permute-start.55 = (bf16[256,1024]{1,0:T(8,128)(2,1)}, bf16[256,1024]{1,0:T(8,128)(2,1)}, u32[]{:S(2)}, u32[]{:S(2)}) collective-permute-start(bf16[256,1024]{1,0:T(8,128)(2,1)} %slice.54.refs_9_), channel_id=1, source_target_pairs={{0,1},{1,2},{2,3},{4,5},{5,6},{6,7},{8,9},{9,10},{10,11},{12,13},{... | collective-permute-start | bytes 1572872 | tf_op jit(solution)/shard_map/ppermute | solution.py:73
  99.8 33.2 %collective-permute-start.56 = (bf16[256,1024]{1,0:T(8,128)(2,1)}, bf16[256,1024]{1,0:T(8,128)(2,1)}, u32[]{:S(2)}, u32[]{:S(2)}) collective-permute-start(bf16[256,1024]{1,0:T(8,128)(2,1)} %slice.54.refs_9_), channel_id=1, source_target_pairs={{1,0},{2,1},{3,2},{5,4},{6,5},{7,6},{9,8},{10,9},{11,10},{13,12},{... | collective-permute-start | bytes 1572872 | tf_op jit(solution)/shard_map/ppermute | solution.py:74
  130.7 69.1 %collective-permute-start.17 = (bf16[256,2048]{1,0:T(8,128)(2,1)S(1)}, bf16[256,2048]{1,0:T(8,128)(2,1)S(1)}, u32[]{:S(2)}, u32[]{:S(2)}) collective-permute-start(bf16[256,2048]{1,0:T(8,128)(2,1)S(1)} %slice.47.refs_9_), channel_id=1, source_target_pairs={{0,1},{1,2},{2,3},{4,5},{5,6},{6,7},{8,9},{9,10},{10,11},{12,13},{... | collective-permute-start | bytes 3145736 | tf_op jit(solution)/shard_map/ppermute | solution.py:73
  133.0 69.8 %collective-permute-start.18 = (bf16[256,2048]{1,0:T(8,128)(2,1)S(1)}, bf16[256,2048]{1,0:T(8,128)(2,1)S(1)}, u32[]{:S(2)}, u32[]{:S(2)}) collective-permute-start(bf16[256,2048]{1,0:T(8,128)(2,1)S(1)} %slice.47.refs_9_), channel_id=1, source_target_pairs={{1,0},{2,1},{3,2},{5,4},{6,5},{7,6},{9,8},{10,9},{11,10},{13,12},{... | collective-permute-start | bytes 3145736 | tf_op jit(solution)/shard_map/ppermute | solution.py:74
  136.1 68.8 %collective-permute-start.36 = (bf16[256,2048]{1,0:T(8,128)(2,1)S(1)}, bf16[256,2048]{1,0:T(8,128)(2,1)S(1)}, u32[]{:S(2)}, u32[]{:S(2)}) collective-permute-start(bf16[256,2048]{1,0:T(8,128)(2,1)S(1)} %slice.49.refs_9_), channel_id=1, source_target_pairs={{0,1},{1,2},{2,3},{4,5},{5,6},{6,7},{8,9},{9,10},{10,11},{12,13},{... | collective-permute-start | bytes 3145736 | tf_op jit(solution)/shard_map/ppermute | solution.py:73
  138.4 67.7 %collective-permute-start.38 = (bf16[256,2048]{1,0:T(8,128)(2,1)S(1)}, bf16[256,2048]{1,0:T(8,128)(2,1)S(1)}, u32[]{:S(2)}, u32[]{:S(2)}) collective-permute-start(bf16[256,2048]{1,0:T(8,128)(2,1)S(1)} %slice.49.refs_9_), channel_id=1, source_target_pairs={{1,0},{2,1},{3,2},{5,4},{6,5},{7,6},{9,8},{10,9},{11,10},{13,12},{... | collective-permute-start | bytes 3145736 | tf_op jit(solution)/shard_map/ppermute | solution.py:74
  141.4 55.8 %collective-permute-start.41 = (bf16[256,1536]{1,0:T(8,128)(2,1)S(1)}, bf16[256,1536]{1,0:T(8,128)(2,1)S(1)}, u32[]{:S(2)}, u32[]{:S(2)}) collective-permute-start(bf16[256,1536]{1,0:T(8,128)(2,1)S(1)} %slice.50.refs_9_), channel_id=1, source_target_pairs={{1,0},{2,1},{3,2},{5,4},{6,5},{7,6},{9,8},{10,9},{11,10},{13,12},{... | collective-permute-start | bytes 2359304 | tf_op jit(solution)/shard_map/ppermute | solution.py:74
  197.2 25.5 %collective-permute-start.3 = (bf16[4,32,4096]{2,1,0:T(8,128)(2,1)S(1)}, bf16[4,32,4096]{2,1,0:T(8,128)(2,1)S(1)}, u32[]{:S(2)}, u32[]{:S(2)}) collective-permute-start(bf16[4,32,4096]{2,1,0:T(8,128)(2,1)S(1)} %fusion.1.refs_1_), channel_id=1, source_target_pairs={{0,4},{4,0},{8,12},{12,8},{16,20},{20,16},{24,28},{28,24},{1,5},{5... | collective-permute-start | bytes 3145736 | tf_op jit(solution)/shard_map/ppermute | solution.py:64
  199.8 14.5 %collective-permute-start.57 = (bf16[256,1024]{1,0:T(8,128)(2,1)}, bf16[256,1024]{1,0:T(8,128)(2,1)S(1)}, u32[]{:S(2)}, u32[]{:S(2)}) collective-permute-start(bf16[256,1024]{1,0:T(8,128)(2,1)} %collective-permute-done.56.refs_15_), channel_id=1, source_target_pairs={{1,0},{2,1},{5,4},{6,5},{9,8},{10,9},{13,12},{14,13},{17,16},{18,1... | collective-permute-start | bytes 1572872 | tf_op jit(solution)/shard_map/ppermute | solution.py:74
  202.9 15.8 %collective-permute-start.59 = (bf16[256,1024]{1,0:T(8,128)(2,1)}, bf16[256,1024]{1,0:T(8,128)(2,1)S(1)}, u32[]{:S(2)}, u32[]{:S(2)}) collective-permute-start(bf16[256,1024]{1,0:T(8,128)(2,1)} %collective-permute-done.55.refs_10_), channel_id=1, source_target_pairs={{1,2},{2,3},{5,6},{6,7},{9,10},{10,11},{13,14},{14,15},{17,18},{18... | collective-permute-start | bytes 1572872 | tf_op jit(solution)/shard_map/ppermute | solution.py:73
  204.8 24.5 %collective-permute-start.4 = (bf16[4,32,4096]{2,1,0:T(8,128)(2,1)S(1)}, bf16[4,32,4096]{2,1,0:T(8,128)(2,1)S(1)}, u32[]{:S(2)}, u32[]{:S(2)}) collective-permute-start(bf16[4,32,4096]{2,1,0:T(8,128)(2,1)S(1)} %fusion.1.refs_1_), channel_id=1, source_target_pairs={{0,8},{4,12},{8,0},{12,4},{16,24},{20,28},{24,16},{28,20},{1,9},{5... | collective-permute-start | bytes 3145736 | tf_op jit(solution)/shard_map/ppermute | solution.py:62
  206.1 46.6 %collective-permute-start.6 = (bf16[4,32,4096]{2,1,0:T(8,128)(2,1)S(1)}, bf16[4,32,4096]{2,1,0:T(8,128)(2,1)S(1)}, u32[]{:S(2)}, u32[]{:S(2)}) collective-permute-start(bf16[4,32,4096]{2,1,0:T(8,128)(2,1)S(1)} %fusion.1.refs_1_), channel_id=1, source_target_pairs={{0,16},{4,20},{8,24},{12,28},{16,0},{20,4},{24,8},{28,12},{1,17},{... | collective-permute-start | bytes 3145736 | tf_op jit(solution)/shard_map/ppermute | solution.py:62
  214.4 40.3 %collective-permute-start.8 = (bf16[4,32,4096]{2,1,0:T(8,128)(2,1)S(1)}, bf16[4,32,4096]{2,1,0:T(8,128)(2,1)S(1)}, u32[]{:S(2)}, u32[]{:S(2)}) collective-permute-start(bf16[4,32,4096]{2,1,0:T(8,128)(2,1)S(1)} %fusion.1.refs_1_), channel_id=1, source_target_pairs={{0,24},{4,28},{8,16},{12,20},{16,8},{20,12},{24,0},{28,4},{1,25},{... | collective-permute-start | bytes 3145736 | tf_op jit(solution)/shard_map/ppermute | solution.py:62
  218.7 41.1 %collective-permute-start.25 = (bf16[256,1536]{1,0:T(8,128)(2,1)}, bf16[256,1536]{1,0:T(8,128)(2,1)S(1)}, u32[]{:S(2)}, u32[]{:S(2)}) collective-permute-start(bf16[256,1536]{1,0:T(8,128)(2,1)} %collective-permute-done.24.refs_15_), channel_id=1, source_target_pairs={{1,0},{2,1},{5,4},{6,5},{9,8},{10,9},{13,12},{14,13},{17,16},{18,1... | collective-permute-start | bytes 2359304 | tf_op jit(solution)/shard_map/ppermute | solution.py:74
  222.8 39.0 %collective-permute-start.27 = (bf16[256,1536]{1,0:T(8,128)(2,1)}, bf16[256,1536]{1,0:T(8,128)(2,1)S(1)}, u32[]{:S(2)}, u32[]{:S(2)}) collective-permute-start(bf16[256,1536]{1,0:T(8,128)(2,1)} %collective-permute-done.23.refs_10_), channel_id=1, source_target_pairs={{1,2},{2,3},{5,6},{6,7},{9,10},{10,11},{13,14},{14,15},{17,18},{18... | collective-permute-start | bytes 2359304 | tf_op jit(solution)/shard_map/ppermute | solution.py:73
  229.3 34.4 %collective-permute-start.42 = (bf16[256,1536]{1,0:T(8,128)(2,1)S(1)}, bf16[256,1536]{1,0:T(8,128)(2,1)}, u32[]{:S(2)}, u32[]{:S(2)}) collective-permute-start(bf16[256,1536]{1,0:T(8,128)(2,1)S(1)} %collective-permute-done.41.refs_15_), channel_id=1, source_target_pairs={{1,0},{2,1},{5,4},{6,5},{9,8},{10,9},{13,12},{14,13},{17,16},{18,1... | collective-permute-start | bytes 2359304 | tf_op jit(solution)/shard_map/ppermute | solution.py:74
  252.7 19.9 %collective-permute-start.44 = (bf16[256,1536]{1,0:T(8,128)(2,1)}, bf16[256,1536]{1,0:T(8,128)(2,1)}, u32[]{:S(2)}, u32[]{:S(2)}) collective-permute-start(bf16[256,1536]{1,0:T(8,128)(2,1)} %collective-permute-done.40.refs_10_), channel_id=1, source_target_pairs={{1,2},{2,3},{5,6},{6,7},{9,10},{10,11},{13,14},{14,15},{17,18},{18... | collective-permute-start | bytes 2359304 | tf_op jit(solution)/shard_map/ppermute | solution.py:73
  254.7 25.0 %collective-permute-start.19 = (bf16[256,2048]{1,0:T(8,128)(2,1)S(1)}, bf16[256,2048]{1,0:T(8,128)(2,1)}, u32[]{:S(2)}, u32[]{:S(2)}) collective-permute-start(bf16[256,2048]{1,0:T(8,128)(2,1)S(1)} %collective-permute-done.18.refs_15_), channel_id=1, source_target_pairs={{1,0},{2,1},{5,4},{6,5},{9,8},{10,9},{13,12},{14,13},{17,16},{18,1... | collective-permute-start | bytes 3145736 | tf_op jit(solution)/shard_map/ppermute | solution.py:74
  259.9 35.2 %collective-permute-start.21 = (bf16[256,2048]{1,0:T(8,128)(2,1)S(1)}, bf16[256,2048]{1,0:T(8,128)(2,1)}, u32[]{:S(2)}, u32[]{:S(2)}) collective-permute-start(bf16[256,2048]{1,0:T(8,128)(2,1)S(1)} %collective-permute-done.17.refs_10_), channel_id=1, source_target_pairs={{1,2},{2,3},{5,6},{6,7},{9,10},{10,11},{13,14},{14,15},{17,18},{18... | collective-permute-start | bytes 3145736 | tf_op jit(solution)/shard_map/ppermute | solution.py:73
  263.7 57.1 %collective-permute-start.49 = (bf16[4,32,7168]{2,1,0:T(8,128)(2,1)S(1)}, bf16[4,32,7168]{2,1,0:T(8,128)(2,1)S(1)}, u32[]{:S(2)}, u32[]{:S(2)}) collective-permute-start(bf16[4,32,7168]{2,1,0:T(8,128)(2,1)S(1)} %fusion.refs_1_), channel_id=1, source_target_pairs={{0,8},{4,12},{8,0},{12,4},{16,24},{20,28},{24,16},{28,20},{1,9},{5... | collective-permute-start | bytes 5505032 | tf_op jit(solution)/shard_map/ppermute | solution.py:62
  272.6 76.7 %collective-permute-start.51 = (bf16[4,32,7168]{2,1,0:T(8,128)(2,1)S(1)}, bf16[4,32,7168]{2,1,0:T(8,128)(2,1)S(1)}, u32[]{:S(2)}, u32[]{:S(2)}) collective-permute-start(bf16[4,32,7168]{2,1,0:T(8,128)(2,1)S(1)} %fusion.refs_1_), channel_id=1, source_target_pairs={{0,16},{4,20},{8,24},{12,28},{16,0},{20,4},{24,8},{28,12},{1,17},{... | collective-permute-start | bytes 5505032 | tf_op jit(solution)/shard_map/ppermute | solution.py:62
  272.6 77.4 %collective-permute-start.53 = (bf16[4,32,7168]{2,1,0:T(8,128)(2,1)S(1)}, bf16[4,32,7168]{2,1,0:T(8,128)(2,1)S(1)}, u32[]{:S(2)}, u32[]{:S(2)}) collective-permute-start(bf16[4,32,7168]{2,1,0:T(8,128)(2,1)S(1)} %fusion.refs_1_), channel_id=1, source_target_pairs={{0,24},{4,28},{8,16},{12,20},{16,8},{20,12},{24,0},{28,4},{1,25},{... | collective-permute-start | bytes 5505032 | tf_op jit(solution)/shard_map/ppermute | solution.py:62
  279.7 37.9 %collective-permute-start.37 = (bf16[256,2048]{1,0:T(8,128)(2,1)S(1)}, bf16[256,2048]{1,0:T(8,128)(2,1)}, u32[]{:S(2)}, u32[]{:S(2)}) collective-permute-start(bf16[256,2048]{1,0:T(8,128)(2,1)S(1)} %collective-permute-done.36.refs_10_), channel_id=1, source_target_pairs={{1,2},{2,3},{5,6},{6,7},{9,10},{10,11},{13,14},{14,15},{17,18},{18... | collective-permute-start | bytes 3145736 | tf_op jit(solution)/shard_map/ppermute | solution.py:73
  295.1 24.8 %collective-permute-start.39 = (bf16[256,2048]{1,0:T(8,128)(2,1)S(1)}, bf16[256,2048]{1,0:T(8,128)(2,1)S(1)}, u32[]{:S(2)}, u32[]{:S(2)}) collective-permute-start(bf16[256,2048]{1,0:T(8,128)(2,1)S(1)} %collective-permute-done.38.refs_13_), channel_id=1, source_target_pairs={{1,0},{2,1},{5,4},{6,5},{9,8},{10,9},{13,12},{14,13},{17,16},{18,1... | collective-permute-start | bytes 3145736 | tf_op jit(solution)/shard_map/ppermute | solution.py:74
  317.5 52.7 %collective-permute-start.5 = (bf16[4,32,4096]{2,1,0:T(8,128)(2,1)S(1)}, bf16[4,32,4096]{2,1,0:T(8,128)(2,1)S(1)}, u32[]{:S(2)}, u32[]{:S(2)}) collective-permute-start(bf16[4,32,4096]{2,1,0:T(8,128)(2,1)S(1)} %collective-permute-done.4.refs_3_), channel_id=1, source_target_pairs={{0,4},{4,0},{8,12},{12,8},{16,20},{20,16},{24,28},{28,24},{1,5},{5... | collective-permute-start | bytes 3145736 | tf_op jit(solution)/shard_map/ppermute | solution.py:64
  319.8 52.7 %collective-permute-start.7 = (bf16[4,32,4096]{2,1,0:T(8,128)(2,1)S(1)}, bf16[4,32,4096]{2,1,0:T(8,128)(2,1)S(1)}, u32[]{:S(2)}, u32[]{:S(2)}) collective-permute-start(bf16[4,32,4096]{2,1,0:T(8,128)(2,1)S(1)} %collective-permute-done.6.refs_5_), channel_id=1, source_target_pairs={{0,4},{4,0},{8,12},{12,8},{16,20},{20,16},{24,28},{28,24},{1,5},{5... | collective-permute-start | bytes 3145736 | tf_op jit(solution)/shard_map/ppermute | solution.py:64
  320.8 53.3 %collective-permute-start.9 = (bf16[4,32,4096]{2,1,0:T(8,128)(2,1)S(1)}, bf16[4,32,4096]{2,1,0:T(8,128)(2,1)S(1)}, u32[]{:S(2)}, u32[]{:S(2)}) collective-permute-start(bf16[4,32,4096]{2,1,0:T(8,128)(2,1)S(1)} %collective-permute-done.8.refs_7_), channel_id=1, source_target_pairs={{0,4},{4,0},{8,12},{12,8},{16,20},{20,16},{24,28},{28,24},{1,5},{5... | collective-permute-start | bytes 3145736 | tf_op jit(solution)/shard_map/ppermute | solution.py:64
  350.0 15.2 %collective-permute-start.28 = (bf16[256,1536]{1,0:T(8,128)(2,1)S(1)}, bf16[256,1536]{1,0:T(8,128)(2,1)S(1)}, u32[]{:S(2)}, u32[]{:S(2)}) collective-permute-start(bf16[256,1536]{1,0:T(8,128)(2,1)S(1)} %collective-permute-done.27.refs_12_), channel_id=1, source_target_pairs={{2,3},{6,7},{10,11},{14,15},{18,19},{22,23},{26,27},{30,31}} | collective-permute-start | bytes 2359304 | tf_op jit(solution)/shard_map/ppermute | solution.py:73
  352.8 74.3 %collective-permute-start.20 = (bf16[256,2048]{1,0:T(8,128)(2,1)}, bf16[256,2048]{1,0:T(8,128)(2,1)}, u32[]{:S(2)}, u32[]{:S(2)}) collective-permute-start(bf16[256,2048]{1,0:T(8,128)(2,1)} %collective-permute-done.19.refs_13_), channel_id=1, source_target_pairs={{1,0},{5,4},{9,8},{13,12},{17,16},{21,20},{25,24},{29,28}} | collective-permute-start | bytes 3145736 | tf_op jit(solution)/shard_map/ppermute | solution.py:74
  365.2 68.2 %collective-permute-start.22 = (bf16[256,2048]{1,0:T(8,128)(2,1)}, bf16[256,2048]{1,0:T(8,128)(2,1)}, u32[]{:S(2)}, u32[]{:S(2)}) collective-permute-start(bf16[256,2048]{1,0:T(8,128)(2,1)} %collective-permute-done.21.refs_12_), channel_id=1, source_target_pairs={{2,3},{6,7},{10,11},{14,15},{18,19},{22,23},{26,27},{30,31}} | collective-permute-start | bytes 3145736 | tf_op jit(solution)/shard_map/ppermute | solution.py:73
  370.3 63.2 %collective-permute-start.46 = (bf16[256,2048]{1,0:T(8,128)(2,1)}, bf16[256,2048]{1,0:T(8,128)(2,1)}, u32[]{:S(2)}, u32[]{:S(2)}) collective-permute-start(bf16[256,2048]{1,0:T(8,128)(2,1)} %collective-permute-done.37.refs_11_), channel_id=1, source_target_pairs={{2,3},{6,7},{10,11},{14,15},{18,19},{22,23},{26,27},{30,31}} | collective-permute-start | bytes 3145736 | tf_op jit(solution)/shard_map/ppermute | solution.py:73
  372.5 17.4 %collective-permute-start.43 = (bf16[256,1536]{1,0:T(8,128)(2,1)}, bf16[256,1536]{1,0:T(8,128)(2,1)}, u32[]{:S(2)}, u32[]{:S(2)}) collective-permute-start(bf16[256,1536]{1,0:T(8,128)(2,1)} %collective-permute-done.42.refs_13_), channel_id=1, source_target_pairs={{1,0},{5,4},{9,8},{13,12},{17,16},{21,20},{25,24},{29,28}} | collective-permute-start | bytes 2359304 | tf_op jit(solution)/shard_map/ppermute | solution.py:74
  375.1 51.1 %collective-permute-start.45 = (bf16[256,1536]{1,0:T(8,128)(2,1)}, bf16[256,1536]{1,0:T(8,128)(2,1)}, u32[]{:S(2)}, u32[]{:S(2)}) collective-permute-start(bf16[256,1536]{1,0:T(8,128)(2,1)} %collective-permute-done.44.refs_12_), channel_id=1, source_target_pairs={{2,3},{6,7},{10,11},{14,15},{18,19},{22,23},{26,27},{30,31}} | collective-permute-start | bytes 2359304 | tf_op jit(solution)/shard_map/ppermute | solution.py:73
  389.9 105.2 %collective-permute-start.48 = (bf16[4,32,7168]{2,1,0:T(8,128)(2,1)S(1)}, bf16[4,32,7168]{2,1,0:T(8,128)(2,1)}, u32[]{:S(2)}, u32[]{:S(2)}) collective-permute-start(bf16[4,32,7168]{2,1,0:T(8,128)(2,1)S(1)} %fusion.refs_1_), channel_id=1, source_target_pairs={{0,4},{4,0},{8,12},{12,8},{16,20},{20,16},{24,28},{28,24},{1,5},{5... | collective-permute-start | bytes 5505032 | tf_op jit(solution)/shard_map/ppermute | solution.py:64
  426.2 36.4 %collective-permute-start.47 = (bf16[256,2048]{1,0:T(8,128)(2,1)}, bf16[256,2048]{1,0:T(8,128)(2,1)S(1)}, u32[]{:S(2)}, u32[]{:S(2)}) collective-permute-start(bf16[256,2048]{1,0:T(8,128)(2,1)} %copy-done.19), channel_id=1, source_target_pairs={{1,0},{5,4},{9,8},{13,12},{17,16},{21,20},{25,24},{29,28}} | collective-permute-start | bytes 3145736 | tf_op jit(solution)/shard_map/ppermute | solution.py:74
  427.1 68.0 %collective-permute-start.50 = (bf16[4,32,7168]{2,1,0:T(8,128)(2,1)}, bf16[4,32,7168]{2,1,0:T(8,128)(2,1)}, u32[]{:S(2)}, u32[]{:S(2)}) collective-permute-start(bf16[4,32,7168]{2,1,0:T(8,128)(2,1)} %copy-done.35), channel_id=1, source_target_pairs={{0,4},{4,0},{8,12},{12,8},{16,20},{20,16},{24,28},{28,24},{1,5},{5... | collective-permute-start | bytes 5505032 | tf_op jit(solution)/shard_map/ppermute | solution.py:64
  433.4 61.7 %collective-permute-start.52 = (bf16[4,32,7168]{2,1,0:T(8,128)(2,1)}, bf16[4,32,7168]{2,1,0:T(8,128)(2,1)}, u32[]{:S(2)}, u32[]{:S(2)}) collective-permute-start(bf16[4,32,7168]{2,1,0:T(8,128)(2,1)} %copy-done.36), channel_id=1, source_target_pairs={{0,4},{4,0},{8,12},{12,8},{16,20},{20,16},{24,28},{28,24},{1,5},{5... | collective-permute-start | bytes 5505032 | tf_op jit(solution)/shard_map/ppermute | solution.py:64
  433.5 61.6 %collective-permute-start.54 = (bf16[4,32,7168]{2,1,0:T(8,128)(2,1)}, bf16[4,32,7168]{2,1,0:T(8,128)(2,1)}, u32[]{:S(2)}, u32[]{:S(2)}) collective-permute-start(bf16[4,32,7168]{2,1,0:T(8,128)(2,1)} %copy-done.37), channel_id=1, source_target_pairs={{0,4},{4,0},{8,12},{12,8},{16,20},{20,16},{24,28},{28,24},{1,5},{5... | collective-permute-start | bytes 5505032 | tf_op jit(solution)/shard_map/ppermute | solution.py:64
  462.6 32.5 %collective-permute-start.60 = (bf16[256,1024]{1,0:T(8,128)(2,1)S(1)}, bf16[256,1024]{1,0:T(8,128)(2,1)S(1)}, u32[]{:S(2)}, u32[]{:S(2)}) collective-permute-start(bf16[256,1024]{1,0:T(8,128)(2,1)S(1)} %copy-done.40), channel_id=1, source_target_pairs={{2,3},{6,7},{10,11},{14,15},{18,19},{22,23},{26,27},{30,31}} | collective-permute-start | bytes 1572872 | tf_op jit(solution)/shard_map/ppermute | solution.py:73
  (57 other events, 1814.1 us)
